TPU v7x, 32 devices: a whole 2x2x4 slice. The times are simulated.
32 devices in a mesh: cols: 4 (over y, x), rows: 8 (over z, core).
Axes of the slice: x: 2, y: 2, z: 4, core: 2. Of those that a mesh axis runs over, the one named last changes fastest.
Arguments:
- gradient: float32 [128, 8192], P('cols', 'rows'), may hold values from -100 to 100
- width_factor: float32 [128, 128], P(None, 'cols'), may hold values from -3 to 4, as said below
- diag_blocks: float32 [64, 128, 128], P('rows'), may hold values from -2 to 24, as said below
- jacobi_inverse: float32 [64, 128, 128], P('rows'), may hold values from -2 to 2, as said below
- coupling_tiles: bfloat16 [32, 128, 128], P('rows'), may hold values from -4 to 4, as said below
- tile_local: int32 [32], P('rows'), may hold values from 0 to 7
- tile_remote: int32 [32], P('rows'), may hold values from 0 to 63, as said below
- tile_count: int32 [8], P('rows'), may hold values from 0 to 3, as said below
Outputs:
- solution: float32 [128, 8192], P('cols', 'rows')
- residual: float32 [128, 8192], P('cols', 'rows')
Inputs may be any that keep to these rules, and one draw needn't show every extreme that they name: `tile_remote`: the live entries are the first tile_count entries of each device's list; they name distinct devices other than the owner, each at most once. For a live entry of device d naming block J of device e, device e has a live entry naming d's block with its tile the transpose. Pad entries hold valid indices. `tile_count`: at most 3 on one device, reached on some device. `coupling_tiles`: with diag_blocks and the live entries, M is symmetric positive definite. `diag_blocks`: symmetric positive definite tiles. `jacobi_inverse`: the inverses of diag_blocks, symmetric. `width_factor`: symmetric positive definite.
All inputs are finite; a program needn't handle non-finite values.
Results may differ from a plain program's by a relative error of at most 0.0085.
Values may be sent and summed in bfloat16 or wider, within the bound.
No kernel may reach another device: no remote copies, remote signals or barrier semaphores. Data moves between devices by JAX's collectives and lax.ppermute only.
A program may use at most 64 MiB of HBM per device.

v0:
```python
import jax
import jax.numpy as jnp
from jax import lax
from jax.experimental import pallas as pl
from jax.experimental.pallas import tpu as pltpu
from jax.sharding import PartitionSpec as P


BLOCK = 128
ITERS = 6
STRETCH = 1.1
GATHER_BYTES = 8 * 2**20


GRANT_BYTES = 24 * 2**20
WHOLE_BYTES = 60 * 2**20

highest = lax.Precision.HIGHEST
f32 = jnp.float32
VMEM = pl.BlockSpec(memory_space=pltpu.VMEM)
SMEM = pl.BlockSpec(memory_space=pltpu.SMEM)


def dot(a, b):
    return jnp.dot(a, b, precision=highest, preferred_element_type=f32)


def call(kernel, outs, *args, scalars=0, scratch=(), place=VMEM, grant=GRANT_BYTES):
    specs = [SMEM] * scalars + [place] * (len(args) - scalars)
    many = isinstance(outs, tuple)
    return pl.pallas_call(
        kernel,
        out_shape=outs,
        in_specs=specs,
        out_specs=tuple([VMEM] * len(outs)) if many else VMEM,
        scratch_shapes=list(scratch),
        compiler_params=pltpu.CompilerParams(vmem_limit_bytes=grant),
    )(*args)


def split(x):
    high = x.astype(jnp.bfloat16)
    return high, (x - high.astype(f32)).astype(jnp.bfloat16)


def plain_dot(a, b):
    return jnp.dot(a, b, preferred_element_type=f32)


def dot3(a, b):
    tall = a.shape[0]
    high, low = split(a)
    right, rest = split(b)
    both = plain_dot(jnp.concatenate([high, low], 0), right)
    return both[:tall] + (both[tall:] + plain_dot(high, rest))


def pack_kernel(local, gradient, jacobi, tiles, packed, inverse, coupling, part, done):
    slots = packed.shape[0]
    contract = (((1,), (1,)), ((), ()))
    copies = []
    for slot in range(slots):
        block = local[slot]
        columns = pl.ds(pl.multiple_of(block * BLOCK, BLOCK), BLOCK)
        moves = [
            (jacobi.at[block], inverse.at[slot]),
            (tiles.at[slot], coupling.at[slot]),
            (gradient.at[:, columns], part.at[slot]),
        ]
        for i, (source, target) in enumerate(moves):
            copy = pltpu.make_async_copy(source, target, done.at[slot, i])
            copy.start()
            copies.append(copy)
    for slot in range(slots):
        for copy in copies[3 * slot : 3 * slot + 3]:
            copy.wait()
        halves = jnp.concatenate(split(inverse[slot]), 0)
        both = lax.dot_general(halves, coupling[slot], contract, preferred_element_type=f32)
        packed[slot, :BLOCK, :] = both[:BLOCK] + both[BLOCK:]
        packed[slot, BLOCK:, :] = part[slot]


def chain_kernel(sources, near, far, chain, high, low, held, out):
    groups, slots = near.shape[:2]
    half = groups * slots
    total = 2 * half
    width = near.shape[2] - BLOCK
    for q in range(total):
        ref = near if q < half else far
        group, slot = divmod(q % half, slots)
        high[q], low[q] = split(ref[group, slot, :BLOCK, :])
        held[q] = ref[group, slot, BLOCK:, :]
    out[total] = jnp.zeros((width, BLOCK), f32)

    def step(j, carry):
        for q in range(total):
            first, second = split(held[q])
            both = jnp.dot(
                jnp.concatenate([first, second], 0), high[q], preferred_element_type=f32
            )
            rest = jnp.dot(first, low[q], preferred_element_type=f32)
            out[q] = both[:width] + both[width:] + rest
        for q in range(total):
            value = out[sources[q * slots]]
            for i in range(1, slots):
                value += out[sources[q * slots + i]]
            held[q] = value
        for slot in range(slots):
            chain[j, slot] = held[slot]
        return carry

    lax.fori_loop(0, ITERS, step, 0)


def shift(x, axis, by):
    size = lax.axis_size(axis)
    return lax.ppermute(x, axis, [(i, (i - by) % size) for i in range(size)])


def whole_pieces(gradient, factor):
    piece = jnp.concatenate([gradient, factor.T], axis=1)
    others = range(1, lax.axis_size("cols"))
    return [piece] + [shift(piece, "cols", o) for o in others]


def chain_gathered(gradient, factor, jacobi, tiles, whole_local, local, remote, live):
    width = gradient.shape[0]
    blocks, slots = jacobi.shape[0], local.shape[0]
    devices = lax.axis_size("rows")
    groups = devices // 2
    packed = call(
        pack_kernel,
        jax.ShapeDtypeStruct((slots, BLOCK + width, BLOCK), f32),
        whole_local,
        gradient,
        jacobi,
        tiles,
        scalars=1,
        scratch=[
            pltpu.VMEM((slots, BLOCK, BLOCK), f32),
            pltpu.VMEM((slots, BLOCK, BLOCK), tiles.dtype),
            pltpu.VMEM((slots, width, BLOCK), f32),
            pltpu.SemaphoreType.DMA((slots, 3)),
        ],
        place=pl.BlockSpec(memory_space=pl.ANY),
        grant=WHOLE_BYTES,
    )
    near = [packed] + [shift(packed, "rows", 2 * o) for o in range(1, groups)]
    gradient, factor, _ = lax.optimization_barrier((gradient, factor, packed))
    pieces = whole_pieces(gradient, factor)
    own = jnp.concatenate([local, remote, live.astype(jnp.int32)])
    own = jnp.pad(own, (0, BLOCK - own.shape[0]))
    told = jnp.broadcast_to(own[None, None, :], (devices, 1, BLOCK))
    told = lax.all_to_all(told, "rows", 0, 0, tiled=True)[:, 0]
    near, pieces, told = lax.optimization_barrier((near, pieces, told))
    near = jnp.stack(near)
    far = lax.ppermute(near, "rows", [(i, i ^ 1) for i in range(devices)])

    me = lax.axis_index("rows")
    position = jnp.arange(devices, dtype=jnp.int32)
    base = me ^ (position // groups)
    device = (base + 2 * (position % groups)) % devices
    pick = (device[:, None] == jnp.arange(devices, dtype=jnp.int32)[None, :]).astype(jnp.int32)
    told = jnp.sum(pick[:, :, None] * told[None, :, :], axis=1)
    locals_, remotes, lives = (
        told[:, i * slots : (i + 1) * slots] for i in range(3)
    )
    owner = (remotes // blocks).reshape(-1)
    holder = jnp.broadcast_to(device[:, None], locals_.shape).reshape(-1)
    alive = lives.reshape(-1) > 0
    meets = (
        (owner[:, None] == holder[None, :])
        & (owner[None, :] == holder[:, None])
        & alive[None, :]
    )
    total = devices * slots
    numbers = jnp.arange(total, dtype=jnp.int32)
    partner = jnp.sum(jnp.where(meets, numbers[None, :], 0), axis=1).reshape(devices, slots)
    same = (
        (locals_[:, :, None] == locals_[:, None, :])
        & (lives[:, None, :] > 0)
        & (lives[:, :, None] > 0)
    )
    sources = jnp.where(same, partner[:, None, :], total).reshape(-1)
    chain = call(
        chain_kernel,
        jax.ShapeDtypeStruct((ITERS, slots, width, BLOCK), f32),
        sources,
        near,
        far,
        scalars=1,
        scratch=[
            pltpu.VMEM((total, BLOCK, BLOCK), jnp.bfloat16),
            pltpu.VMEM((total, BLOCK, BLOCK), jnp.bfloat16),
            pltpu.VMEM((total, width, BLOCK), f32),
            pltpu.VMEM((total + 1, width, BLOCK), f32),
        ],
    )
    return chain, pieces


def chain_exchanged(gradient, jacobi, tiles, local, remote, live):
    width = gradient.shape[0]
    blocks = jacobi.shape[0]
    devices = lax.axis_size("rows")
    owner = remote // blocks
    placing = (
        (local[:, None] == jnp.arange(blocks, dtype=jnp.int32)[None, :]) & live[:, None]
    ).astype(f32)
    meets = live[:, None] & (owner[:, None] == jnp.arange(devices, dtype=jnp.int32)[None, :])
    granted = jnp.sum(jnp.where(meets, local[:, None], 0), axis=0)
    vector = jnp.transpose(gradient.reshape(width, blocks, BLOCK), (1, 0, 2))
    steps = []
    for _ in range(ITERS):
        sent = jnp.einsum("nej,nji->nei", vector, jacobi, precision=highest)[granted]
        incoming = lax.all_to_all(sent, "rows", 0, 0, tiled=True)
        products = jnp.einsum(
            "kej,kji->kei", incoming[owner], tiles.astype(f32), precision=highest
        )
        vector = jnp.einsum("kei,kn->nei", products, placing, precision=highest)
        steps.append(vector)
    return jnp.stack(steps)


def basis_kernel(turn, *refs):
    devices = len(refs) - 5
    pieces, jacobi = refs[:devices], refs[devices]
    mixes, plain, smooth, scale = refs[devices + 1 :]
    width = pieces[0].shape[0]
    blocks = jacobi.shape[0]
    rows = blocks * BLOCK
    factor = jnp.concatenate([piece[:, rows:] for piece in pieces], 0)
    factor = pltpu.roll(factor, turn[0], 1)
    norm = jnp.max(jnp.sum(jnp.abs(factor), axis=1, keepdims=True), axis=0, keepdims=True)
    power = factor / norm
    for _ in range(3):
        power = dot(power, power)
    bound = jnp.sum(jnp.sum(power * power, axis=1, keepdims=True), axis=0, keepdims=True)
    for _ in range(4):
        bound = jnp.sqrt(bound)
    ratio = 2.0 / (STRETCH * bound * norm)
    scale[...] = jnp.broadcast_to(ratio, scale.shape)
    factor = factor * ratio

    row = lax.broadcasted_iota(jnp.int32, (width, BLOCK), 0)
    lane = lax.broadcasted_iota(jnp.int32, (width, BLOCK), 1)
    kept = [[(row == lane).astype(f32)]]
    for k in range(ITERS):
        last = kept[k]
        terms = [last[0]] + [last[j] + last[j - 1] for j in range(1, k + 1)] + [last[k]]
        image = dot(jnp.concatenate(terms, 0), factor)
        fresh = []
        for j in range(k + 2):
            value = image[j * width : (j + 1) * width]
            if j <= k:
                value = value - last[j]
            if k:
                value = 2.0 * value
                if j <= k - 1:
                    value = value - kept[k - 1][j]
            fresh.append(value)
        kept.append(fresh)
    at = 0
    for j in range(1, ITERS + 1):
        for k in range(j, ITERS + 1):
            mixes[at : at + width, :] = kept[k][j]
            at += width
    first = jnp.concatenate([kept[k][0] for k in range(ITERS + 1)], 0)
    for b in range(blocks):
        columns = slice(b * BLOCK, (b + 1) * BLOCK)
        whole = jnp.concatenate([piece[:, columns] for piece in pieces], 0)
        value = dot(first, whole)
        plain[b] = value
        smooth[b] = dot(value[: ITERS * width], jacobi[b])


def mix_kernel(local, index, *refs):
    devices = len(refs) - 8
    chains = refs[:devices]
    gradient, mixes, plain, smooth, jacobi = refs[devices : devices + 5]
    added, smoothed, gram = refs[devices + 5 :]
    slots, width = chains[0].shape[1:3]
    blocks = jacobi.shape[0]
    short = (ITERS - 1) * width
    totals = [0.0] * ITERS
    at = 0
    for j in range(1, ITERS + 1):
        count = (ITERS + 1 - j) * width
        whole = jnp.concatenate(
            [
                jnp.concatenate([chain[j - 1, slot] for chain in chains], 0)
                for slot in range(slots)
            ],
            1,
        )
        part = dot3(mixes[at : at + count, :], whole)
        at += count
        for k in range(j, ITERS + 1):
            totals[k - 1] += part[(k - j) * width : (k - j + 1) * width]
    for slot in range(slots):
        columns = slice(slot * BLOCK, (slot + 1) * BLOCK)
        value = jnp.concatenate([total[:, columns] for total in totals], 0)
        added[slot] = value
        smoothed[slot] = dot3(value[:short], jacobi[local[slot]])
    added[slots] = jnp.zeros(added.shape[1:], f32)
    smoothed[slots] = jnp.zeros(smoothed.shape[1:], f32)

    sums = {}
    for b in range(blocks):
        slot = index[b]
        for r in range(0, width, 8):
            s = [plain[b, k * width + r : k * width + r + 8, :] for k in range(ITERS + 1)]
            y = [smooth[b, k * width + r : k * width + r + 8, :] for k in range(ITERS)]
            for k in range(1, ITERS + 1):
                rows = slice((k - 1) * width + r, (k - 1) * width + r + 8)
                s[k] = s[k] + added[slot, rows, :]
                if k < ITERS:
                    y[k] = y[k] + smoothed[slot, rows, :]
            g = gradient[r : r + 8, b * BLOCK : (b + 1) * BLOCK]
            f = [s[0] + s[1]]
            for j in range(1, ITERS):
                f.append(0.5 * (s[j - 1] + s[j + 1]) + s[j])
            for i in range(ITERS):
                for j in range(i + 1):
                    sums[i, j] = sums.get((i, j), 0.0) + y[i] * f[j]
                sums[i, ITERS] = sums.get((i, ITERS), 0.0) + y[i] * g
    lane = lax.broadcasted_iota(jnp.int32, (1, BLOCK), 1)
    result = jnp.zeros((1, BLOCK), f32)
    for (i, j), value in sums.items():
        value = jnp.sum(jnp.sum(value, axis=0, keepdims=True), axis=1, keepdims=True)
        here = lane == 16 * i + j
        if j < ITERS:
            here = here | (lane == 16 * j + i)
        result = jnp.where(here, value, result)
    gram[...] = result


def finish_kernel(
    index, grams, scale, gradient, plain, smooth, added, smoothed, solution, residual, extra, less
):
    width = gradient.shape[0]
    blocks = plain.shape[0]
    slots = added.shape[0] - 1
    flat = jnp.sum(grams[:, 0, :], axis=0, keepdims=True)
    row = lax.broadcasted_iota(jnp.int32, (8, BLOCK), 0)
    lane = lax.broadcasted_iota(jnp.int32, (8, BLOCK), 1)
    table = jnp.zeros((8, BLOCK), f32)
    for i in range(ITERS):
        moved = flat if i == 0 else pltpu.roll(flat, BLOCK - 16 * i, 1)
        table = jnp.where((row == i) & (lane <= ITERS), moved, table)
    for p in range(ITERS):
        pivot = table[p : p + 1, :] / table[p : p + 1, p : p + 1]
        table = jnp.where(row == p, pivot, table - table[:, p : p + 1] * pivot)
    steps = [table[j : j + 1, ITERS : ITERS + 1] for j in range(ITERS)]
    takes = []
    for k in range(ITERS + 1):
        value = 0.0
        if k > 0:
            value += steps[k - 1] * (1.0 if k == 1 else 0.5)
        if k < ITERS:
            value += steps[k]
        if k + 1 < ITERS:
            value += 0.5 * steps[k + 1]
        takes.append(jnp.broadcast_to(value, (width, BLOCK)))
    longer = scale[0:1, 0:1]
    gives = [jnp.broadcast_to(longer * step, (width, BLOCK)) for step in steps]

    def combine(weights, ref, b, start):
        total = None
        for j, weight in enumerate(weights):
            term = weight * ref[b, (start + j) * width : (start + j + 1) * width, :]
            total = term if total is None else total + term
        return total

    for slot in range(slots):
        extra[slot] = combine(gives[1:], smoothed, slot, 0)
        less[slot] = combine(takes[1:], added, slot, 0)
    extra[slots] = jnp.zeros((width, BLOCK), f32)
    less[slots] = jnp.zeros((width, BLOCK), f32)
    for b in range(blocks):
        columns = slice(b * BLOCK, (b + 1) * BLOCK)
        slot = index[b]
        solution[:, columns] = combine(gives, smooth, b, 0) + extra[slot]
        residual[:, columns] = gradient[:, columns] - combine(takes, plain, b, 0) - less[slot]


def on_device(
    gradient,
    width_factor,
    diag_blocks,
    jacobi_inverse,
    coupling_tiles,
    tile_local,
    tile_remote,
    tile_count,
    exchange=False,
):
    width, rows = gradient.shape
    blocks = diag_blocks.shape[0]
    columns = lax.axis_size("cols")
    devices = lax.axis_size("rows")
    slots = tile_local.shape[0] - 1
    live = jnp.arange(slots, dtype=jnp.int32) < tile_count[0]
    lists = (tile_local[:slots], tile_remote[:slots], live)

    numbers = jnp.arange(blocks, dtype=jnp.int32)
    gathered = devices * slots * BLOCK * (BLOCK + width) * 4
    if gathered <= GATHER_BYTES and devices % 2 == 0 and not exchange:
        chain, pieces = chain_gathered(
            gradient, width_factor, jacobi_inverse, coupling_tiles, tile_local, *lists
        )
        at = tile_local
        here = (lists[0][None, :] == numbers[:, None]) & live[None, :]
        order = jnp.arange(slots, dtype=jnp.int32)[None, :]
        index = jnp.min(jnp.where(here, order, slots), axis=1)
    else:
        chain = chain_exchanged(gradient, jacobi_inverse, coupling_tiles[:slots], *lists)
        pieces = whole_pieces(gradient, width_factor)
        at, index = numbers, numbers
    units = chain.shape[1]
    chains = [chain] + [shift(chain, "cols", o) for o in range(1, columns)]

    turn = (BLOCK - width * lax.axis_index("cols")) % BLOCK
    shape = jax.ShapeDtypeStruct
    count = ITERS * (ITERS + 1) // 2
    mixes, plain, smooth, scale = call(
        basis_kernel,
        (
            shape((count * width, BLOCK), f32),
            shape((blocks, (ITERS + 1) * width, BLOCK), f32),
            shape((blocks, ITERS * width, BLOCK), f32),
            shape((8, BLOCK), f32),
        ),
        turn.astype(jnp.int32).reshape(1),
        *pieces,
        jacobi_inverse,
        scalars=1,
    )
    added, smoothed, gram = call(
        mix_kernel,
        (
            shape((units + 1, ITERS * width, BLOCK), f32),
            shape((units + 1, (ITERS - 1) * width, BLOCK), f32),
            shape((1, BLOCK), f32),
        ),
        at,
        index,
        *chains,
        gradient,
        mixes,
        plain,
        smooth,
        jacobi_inverse,
        scalars=2,
    )
    everyone = columns * devices
    grams = lax.all_to_all(
        jnp.broadcast_to(gram[None], (everyone, 1, BLOCK)),
        ("cols", "rows"),
        0,
        0,
        tiled=True,
    )
    return call(
        finish_kernel,
        (shape((width, rows), f32), shape((width, rows), f32)),
        index,
        grams,
        scale,
        gradient,
        plain,
        smooth,
        added,
        smoothed,
        scalars=1,
        scratch=[pltpu.VMEM((units + 1, width, BLOCK), f32)] * 2,
    )


def solution(mesh):
    placed = (
        P("cols", "rows"),
        P(None, "cols"),
        P("rows", None, None),
        P("rows", None, None),
        P("rows", None, None),
        P("rows"),
        P("rows"),
        P("rows"),
    )

    return jax.shard_map(
        on_device,
        mesh=mesh,
        in_specs=placed,
        out_specs=(P("cols", "rows"), P("cols", "rows")),
        check_vma=False,
    )
```

profile of v0, /device:TPU:0, one launch (start us, length us, event | category | flops | bytes accessed | tf_op | source)
XLA Modules:
  0.0 70.7 jit_solution(9587349964435127508)
XLA Ops:
  0.7 3.0 %shard_map.86 = f32[3,160,128]{2,1,0:T(8,128)} custom-call(s32[4]{0:T(128)} %local.3, f32[32,1024]{1,0:T(8,128)} %gradient.3, f32[8,128,128]{2,1,0:T(8,128)} %refs_8_.1, bf16[4,128,128]{2,1,0:T(8,128)(2,1)} %tiles.1), custom_call_target="tpu_custom_call" | custom-call | tf_op jit(solution)/shard_map/pallas_call | solution.py:31
  3.7 3.0 %collective-permute-start.5 = (f32[32,1152]{1,0:T(8,128)S(1)}, f32[32,1152]{1,0:T(8,128)S(1)}, u32[]{:S(2)}, u32[]{:S(2)}) collective-permute-start(f32[32,1152]{1,0:T(8,128)S(1)} %pad_maximum_fusion.1.refs_0_), channel_id=1, source_target_pairs={{0,8},{8,16},{16,24},{24,0},{1,9},{9,17},{17,25},{25,1},{2,10},{10... | collective-permute-start | bytes 442376 | tf_op jit(solution)/shard_map/ppermute | solution.py:117
  6.7 1.5 %collective-permute-start.4 = (f32[32,1152]{1,0:T(8,128)S(1)}, f32[32,1152]{1,0:T(8,128)S(1)}, u32[]{:S(2)}, u32[]{:S(2)}) collective-permute-start(f32[32,1152]{1,0:T(8,128)S(1)} %pad_maximum_fusion.1.refs_0_), channel_id=1, source_target_pairs={{0,16},{8,24},{16,0},{24,8},{1,17},{9,25},{17,1},{25,9},{2,18},{10... | collective-permute-start | bytes 442376 | tf_op jit(solution)/shard_map/ppermute | solution.py:117
  8.2 1.6 %collective-permute-start.2 = (f32[3,160,128]{2,1,0:T(8,128)S(1)}, f32[3,160,128]{2,1,0:T(8,128)S(1)}, u32[]{:S(2)}, u32[]{:S(2)}) collective-permute-start(f32[3,160,128]{2,1,0:T(8,128)S(1)} %copy-done.3), channel_id=1, source_target_pairs={{0,2},{1,3},{2,4},{3,5},{4,6},{5,7},{6,0},{7,1},{8,10},{9,11},{10,... | collective-permute-start | bytes 737288 | tf_op jit(solution)/shard_map/ppermute | solution.py:117
  9.8 2.6 %collective-permute-start.1 = (f32[3,160,128]{2,1,0:T(8,128)S(1)}, f32[3,160,128]{2,1,0:T(8,128)S(1)}, u32[]{:S(2)}, u32[]{:S(2)}) collective-permute-start(f32[3,160,128]{2,1,0:T(8,128)S(1)} %copy-done.3), channel_id=1, source_target_pairs={{0,4},{1,5},{2,6},{3,7},{4,0},{5,1},{6,2},{7,3},{8,12},{9,13},{10,... | collective-permute-start | bytes 737288 | tf_op jit(solution)/shard_map/ppermute | solution.py:117
  12.4 1.3 %collective-permute-start = (f32[3,160,128]{2,1,0:T(8,128)S(1)}, f32[3,160,128]{2,1,0:T(8,128)S(1)}, u32[]{:S(2)}, u32[]{:S(2)}) collective-permute-start(f32[3,160,128]{2,1,0:T(8,128)S(1)} %copy-done.3), channel_id=1, source_target_pairs={{0,6},{1,7},{2,0},{3,1},{4,2},{5,3},{6,4},{7,5},{8,14},{9,15},{10,... | collective-permute-start | bytes 737288 | tf_op jit(solution)/shard_map/ppermute | solution.py:117
  14.4 1.5 %collective-permute-start.3 = (f32[32,1152]{1,0:T(8,128)S(1)}, f32[32,1152]{1,0:T(8,128)S(1)}, u32[]{:S(2)}, u32[]{:S(2)}) collective-permute-start(f32[32,1152]{1,0:T(8,128)S(1)} %pad_maximum_fusion.1.refs_0_), channel_id=1, source_target_pairs={{0,24},{8,0},{16,8},{24,16},{1,25},{9,1},{17,9},{25,17},{2,26},{10... | collective-permute-start | bytes 442376 | tf_op jit(solution)/shard_map/ppermute | solution.py:117
  15.9 0.7 copy-done.2
  16.6 0.6 broadcast_in_dim.48
  17.2 3.3 %all-to-all-start = ((s32[8,1,128]{2,1,0:T(1,128)}), s32[8,1,128]{2,1,0:T(1,128)S(1)}, u32[]{:S(2)}, u32[]{:S(2)}) async-start(s32[8,1,128]{2,1,0:T(1,128)} %broadcast_in_dim.48), calls=%async_computation | async-start | bytes 8192 | tf_op jit(solution)/shard_map/all_to_all | solution.py:154
  20.6 12.6 %all-to-all-done = s32[8,1,128]{2,1,0:T(1,128)S(1)} async-done(((s32[8,1,128]{2,1,0:T(1,128)}), s32[8,1,128]{2,1,0:T(1,128)S(1)}, u32[]{:S(2)}, u32[]{:S(2)}) %all-to-all-start) | async-done | bytes 4128 | tf_op jit(solution)/shard_map/all_to_all | solution.py:154
  33.5 0.1 eq.91
  33.5 0.1 multiply_reduce_fusion
  33.7 0.1 gt.15
  33.8 0.1 fusion.9
  33.9 0.1 eq.89
  34.0 0.2 select_reduce_fusion
  34.2 0.1 broadcast_in_dim.78
  34.2 0.1 and_select_fusion
  34.3 0.1 select_n.62.sources
  34.5 1.4 %collective-permute-done.6.far = f32[4,3,160,128]{3,2,1,0:T(8,128)S(1)} collective-permute-done((f32[4,3,160,128]{3,2,1,0:T(8,128)S(1)}, f32[4,3,160,128]{3,2,1,0:T(8,128)S(1)}, u32[]{:S(2)}, u32[]{:S(2)}) %collective-permute-start.6) | collective-permute-done | bytes 983072 | tf_op jit(solution)/shard_map/ppermute | solution.py:157
  35.9 4.3 %shard_map.87.refs_0_ = f32[6,3,32,128]{3,2,1,0:T(8,128)S(1)} custom-call(s32[72]{0:T(128)S(1)} %select_n.62.sources, f32[4,3,160,128]{3,2,1,0:T(8,128)S(1)} %pad_maximum_fusion.near, f32[4,3,160,128]{3,2,1,0:T(8,128)S(1)} %collective-permute-done.6.far), custom_call_target="tpu_custom_call" | custom-call | tf_op jit(solution)/shard_map/pallas_call | solution.py:31
  40.1 0.5 collective-permute-start.9
  40.7 1.5 %collective-permute-start.8 = (f32[6,3,32,128]{3,2,1,0:T(8,128)S(1)}, f32[6,3,32,128]{3,2,1,0:T(8,128)S(1)}, u32[]{:S(2)}, u32[]{:S(2)}) collective-permute-start(f32[6,3,32,128]{3,2,1,0:T(8,128)S(1)} %shard_map.87.refs_0_), channel_id=1, source_target_pairs={{0,16},{8,24},{16,0},{24,8},{1,17},{9,25},{17,1},{25,9},{2,18},{10... | collective-permute-start | bytes 884744 | tf_op jit(solution)/shard_map/ppermute | solution.py:117
  42.2 1.4 %collective-permute-start.7 = (f32[6,3,32,128]{3,2,1,0:T(8,128)S(1)}, f32[6,3,32,128]{3,2,1,0:T(8,128)S(1)}, u32[]{:S(2)}, u32[]{:S(2)}) collective-permute-start(f32[6,3,32,128]{3,2,1,0:T(8,128)S(1)} %shard_map.87.refs_0_), channel_id=1, source_target_pairs={{0,24},{8,0},{16,8},{24,16},{1,25},{9,1},{17,9},{25,17},{2,26},{10... | collective-permute-start | bytes 884744 | tf_op jit(solution)/shard_map/ppermute | solution.py:117
  43.6 0.1 select_reduce_fusion.1.index
  43.8 4.6 %shard_map.88 = (f32[672,128]{1,0:T(8,128)S(1)}, f32[8,224,128]{2,1,0:T(8,128)S(1)}, f32[8,192,128]{2,1,0:T(8,128)S(1)}, f32[8,128]{1,0:T(8,128)S(1)}) custom-call(s32[1]{0:T(128)} %bitcast.7.turn, f32[32,1152]{1,0:T(8,128)S(1)} %pad_maximum_fusion.1.refs_0_, f32[32,1152]{1,0:T(8,128)S(1)} %collective-permute-done.3.refs_1_, ...), custom_call_target="tpu_custom_call" | custom-call | tf_op jit(solution)/shard_map/pallas_call | solution.py:31
  48.4 2.6 %collective-permute-done.9.refs_3_ = f32[6,3,32,128]{3,2,1,0:T(8,128)S(1)} collective-permute-done((f32[6,3,32,128]{3,2,1,0:T(8,128)S(1)}, f32[6,3,32,128]{3,2,1,0:T(8,128)S(1)}, u32[]{:S(2)}, u32[]{:S(2)}) %collective-permute-start.9) | collective-permute-done | bytes 294944 | tf_op jit(solution)/shard_map/ppermute | solution.py:117
  51.0 4.7 %collective-permute-done.8.refs_2_ = f32[6,3,32,128]{3,2,1,0:T(8,128)S(1)} collective-permute-done((f32[6,3,32,128]{3,2,1,0:T(8,128)S(1)}, f32[6,3,32,128]{3,2,1,0:T(8,128)S(1)}, u32[]{:S(2)}, u32[]{:S(2)}) %collective-permute-start.8) | collective-permute-done | bytes 294944 | tf_op jit(solution)/shard_map/ppermute | solution.py:117
  55.8 1.9 %shard_map.89 = (f32[4,192,128]{2,1,0:T(8,128)S(1)}, f32[4,160,128]{2,1,0:T(8,128)S(1)}, f32[1,128]{1,0:T(1,128)S(1)}) custom-call(s32[4]{0:T(128)S(1)} %copy-done.2, s32[8]{0:T(128)S(1)} %select_reduce_fusion.1.index, f32[6,3,32,128]{3,2,1,0:T(8,128)S(1)} %shard_map.87.refs_0_, f32[6,3,32,128]{3,2,1,0:T(8,128)S(1)} %collective-permute-done.7.refs_1_, ...), custom_call_target="tpu_custom_call" | custom-call | tf_op jit(solution)/shard_map/pallas_call | solution.py:31
  57.7 10.9 %all_to_all.10.grams = f32[32,1,128]{2,1,0:T(1,128)S(1)} all-to-all(f32[32,1,128]{2,1,0:T(1,128)S(1)} %broadcast_in_dim.82), channel_id=1, replica_groups=mesh['cols'=4,'rows'=8] {'cols','rows'}, dimensions={0} | all-to-all | bytes 32768 | tf_op jit(solution)/shard_map/all_to_all | solution.py:457
  68.6 2.0 %shard_map.90 = (f32[32,1024]{1,0:T(8,128)}, f32[32,1024]{1,0:T(8,128)}) custom-call(s32[8]{0:T(128)S(1)} %select_reduce_fusion.1.index, f32[32,1,128]{2,1,0:T(1,128)S(1)} %all_to_all.10.grams, f32[8,128]{1,0:T(8,128)S(1)} %get-tuple-element.35.scale, f32[32,1024]{1,0:T(8,128)S(1)} %copy-done.1, f32[8,224,128]{2,1,0:T(8,128)S(1)} %get-tuple-element.32.refs_6_.plain, ...), custom_call_target="tpu_custom_call" | custom-call | tf_op jit(solution)/shard_map/pallas_call | solution.py:31
  (30 shorter events, 0.6 us)
Async XLA Ops:
  0.6 3.0 %copy-start.1 = (f32[32,1024]{1,0:T(8,128)S(1)}, f32[32,1024]{1,0:T(8,128)}, u32[]{:S(2)}) copy-start(f32[32,1024]{1,0:T(8,128)} %gradient.3) | copy-start | bytes 393220
  0.6 3.0 %copy-start.4 = (f32[128,32]{0,1:T(8,128)S(1)}, f32[128,32]{0,1:T(8,128)}, u32[]{:S(2)}) copy-start(f32[128,32]{0,1:T(8,128)} %param.9) | copy-start | bytes 49156
  3.6 4.6 %copy-start.3 = (f32[3,160,128]{2,1,0:T(8,128)S(1)}, f32[3,160,128]{2,1,0:T(8,128)}, u32[]{:S(2)}) copy-start(f32[3,160,128]{2,1,0:T(8,128)} %shard_map.86) | copy-start | bytes 737284
  3.7 10.7 %collective-permute-start.5 = (f32[32,1152]{1,0:T(8,128)S(1)}, f32[32,1152]{1,0:T(8,128)S(1)}, u32[]{:S(2)}, u32[]{:S(2)}) collective-permute-start(f32[32,1152]{1,0:T(8,128)S(1)} %pad_maximum_fusion.1.refs_0_), channel_id=1, source_target_pairs={{0,8},{8,16},{16,24},{24,0},{1,9},{9,17},{17,25},{25,1},{2,10},{10... | collective-permute-start | bytes 442376 | tf_op jit(solution)/shard_map/ppermute | solution.py:117
  6.7 26.4 %collective-permute-start.4 = (f32[32,1152]{1,0:T(8,128)S(1)}, f32[32,1152]{1,0:T(8,128)S(1)}, u32[]{:S(2)}, u32[]{:S(2)}) collective-permute-start(f32[32,1152]{1,0:T(8,128)S(1)} %pad_maximum_fusion.1.refs_0_), channel_id=1, source_target_pairs={{0,16},{8,24},{16,0},{24,8},{1,17},{9,25},{17,1},{25,9},{2,18},{10... | collective-permute-start | bytes 442376 | tf_op jit(solution)/shard_map/ppermute | solution.py:117
  8.2 24.9 %collective-permute-start.2 = (f32[3,160,128]{2,1,0:T(8,128)S(1)}, f32[3,160,128]{2,1,0:T(8,128)S(1)}, u32[]{:S(2)}, u32[]{:S(2)}) collective-permute-start(f32[3,160,128]{2,1,0:T(8,128)S(1)} %copy-done.3), channel_id=1, source_target_pairs={{0,2},{1,3},{2,4},{3,5},{4,6},{5,7},{6,0},{7,1},{8,10},{9,11},{10,... | collective-permute-start | bytes 737288 | tf_op jit(solution)/shard_map/ppermute | solution.py:117
  9.8 23.4 %collective-permute-start.1 = (f32[3,160,128]{2,1,0:T(8,128)S(1)}, f32[3,160,128]{2,1,0:T(8,128)S(1)}, u32[]{:S(2)}, u32[]{:S(2)}) collective-permute-start(f32[3,160,128]{2,1,0:T(8,128)S(1)} %copy-done.3), channel_id=1, source_target_pairs={{0,4},{1,5},{2,6},{3,7},{4,0},{5,1},{6,2},{7,3},{8,12},{9,13},{10,... | collective-permute-start | bytes 737288 | tf_op jit(solution)/shard_map/ppermute | solution.py:117
  12.4 20.8 %collective-permute-start = (f32[3,160,128]{2,1,0:T(8,128)S(1)}, f32[3,160,128]{2,1,0:T(8,128)S(1)}, u32[]{:S(2)}, u32[]{:S(2)}) collective-permute-start(f32[3,160,128]{2,1,0:T(8,128)S(1)} %copy-done.3), channel_id=1, source_target_pairs={{0,6},{1,7},{2,0},{3,1},{4,2},{5,3},{6,4},{7,5},{8,14},{9,15},{10,... | collective-permute-start | bytes 737288 | tf_op jit(solution)/shard_map/ppermute | solution.py:117
  14.4 18.7 %collective-permute-start.3 = (f32[32,1152]{1,0:T(8,128)S(1)}, f32[32,1152]{1,0:T(8,128)S(1)}, u32[]{:S(2)}, u32[]{:S(2)}) collective-permute-start(f32[32,1152]{1,0:T(8,128)S(1)} %pad_maximum_fusion.1.refs_0_), channel_id=1, source_target_pairs={{0,24},{8,0},{16,8},{24,16},{1,25},{9,1},{17,9},{25,17},{2,26},{10... | collective-permute-start | bytes 442376 | tf_op jit(solution)/shard_map/ppermute | solution.py:117
  15.9 0.7 copy-start.2
  15.9 0.7 copy-start.5
  17.2 15.9 %all-to-all-start = ((s32[8,1,128]{2,1,0:T(1,128)}), s32[8,1,128]{2,1,0:T(1,128)S(1)}, u32[]{:S(2)}, u32[]{:S(2)}) async-start(s32[8,1,128]{2,1,0:T(1,128)} %broadcast_in_dim.48), calls=%async_computation | async-start | bytes 8192 | tf_op jit(solution)/shard_map/all_to_all | solution.py:154
  33.2 2.6 %collective-permute-start.6 = (f32[4,3,160,128]{3,2,1,0:T(8,128)S(1)}, f32[4,3,160,128]{3,2,1,0:T(8,128)S(1)}, u32[]{:S(2)}, u32[]{:S(2)}) collective-permute-start(f32[4,3,160,128]{3,2,1,0:T(8,128)S(1)} %pad_maximum_fusion.near), channel_id=1, source_target_pairs={{0,1},{1,0},{2,3},{3,2},{4,5},{5,4},{6,7},{7,6},{8,9},{9,8},{10,11... | collective-permute-start | bytes 2949128 | tf_op jit(solution)/shard_map/ppermute | solution.py:157
  34.4 9.3 %copy-start = (f32[8,128,128]{2,1,0:T(8,128)S(1)}, f32[8,128,128]{2,1,0:T(8,128)}, u32[]{:S(2)}) copy-start(f32[8,128,128]{2,1,0:T(8,128)} %refs_8_.1) | copy-start | bytes 1572868
  40.1 10.9 %collective-permute-start.9 = (f32[6,3,32,128]{3,2,1,0:T(8,128)S(1)}, f32[6,3,32,128]{3,2,1,0:T(8,128)S(1)}, u32[]{:S(2)}, u32[]{:S(2)}) collective-permute-start(f32[6,3,32,128]{3,2,1,0:T(8,128)S(1)} %shard_map.87.refs_0_), channel_id=1, source_target_pairs={{0,8},{8,16},{16,24},{24,0},{1,9},{9,17},{17,25},{25,1},{2,10},{10... | collective-permute-start | bytes 884744 | tf_op jit(solution)/shard_map/ppermute | solution.py:117
  40.7 15.1 %collective-permute-start.8 = (f32[6,3,32,128]{3,2,1,0:T(8,128)S(1)}, f32[6,3,32,128]{3,2,1,0:T(8,128)S(1)}, u32[]{:S(2)}, u32[]{:S(2)}) collective-permute-start(f32[6,3,32,128]{3,2,1,0:T(8,128)S(1)} %shard_map.87.refs_0_), channel_id=1, source_target_pairs={{0,16},{8,24},{16,0},{24,8},{1,17},{9,25},{17,1},{25,9},{2,18},{10... | collective-permute-start | bytes 884744 | tf_op jit(solution)/shard_map/ppermute | solution.py:117
  42.2 13.6 %collective-permute-start.7 = (f32[6,3,32,128]{3,2,1,0:T(8,128)S(1)}, f32[6,3,32,128]{3,2,1,0:T(8,128)S(1)}, u32[]{:S(2)}, u32[]{:S(2)}) collective-permute-start(f32[6,3,32,128]{3,2,1,0:T(8,128)S(1)} %shard_map.87.refs_0_), channel_id=1, source_target_pairs={{0,24},{8,0},{16,8},{24,16},{1,25},{9,1},{17,9},{25,17},{2,26},{10... | collective-permute-start | bytes 884744 | tf_op jit(solution)/shard_map/ppermute | solution.py:117
where the time goes:
time: 70.9 us; the launch traced here: 70.7 us
  waiting for transfers between devices  21.4 us (30%)
  starting transfers between devices  18.4 us (26%)
  Pallas kernels  15.8 us (22%)
  blocking collectives  10.9 us (15%)
  local copies, waits for them, and re-layouts  1.83 us (3%)
  between operations  1.48 us (2%)
  other arithmetic  0.89 us (1%)
    pallas_call x5, Pallas kernels, call(): pl.pallas_call(kernel, out_shape=outs, in_specs=specs, out_specs=tuple([V...  15.8 us
    ppermute x9, starting transfers between devices, shift(): return lax.ppermute(x, axis, [(i, (i - by) % size) for i in range(size)])  15 us
    all_to_all x1, waiting for transfers between devices, chain_gathered(): told = lax.all_to_all(told, 'rows', 0, 0, tiled=True)[:, 0]  12.6 us
    all_to_all x1, blocking collectives, on_device(): lax.all_to_all(jnp.broadcast_to(gram[None], (everyone, 1, BLOCK)), ('cols...  10.9 us
    ppermute x9, waiting for transfers between devices, shift(): return lax.ppermute(x, axis, [(i, (i - by) % size) for i in range(size)])  7.4 us
    all_to_all x1, starting transfers between devices, chain_gathered(): told = lax.all_to_all(told, 'rows', 0, 0, tiled=True)[:, 0]  3.31 us
    ppermute x1, waiting for transfers between devices, chain_gathered(): far = lax.ppermute(near, 'rows', [(i, i ^ 1) for i in range(devices)])  1.42 us
  transfers between devices with their start and end apart: 11, of which 4 were waited for; matrix products, arithmetic and copies ran while one was open for 3% of the time, Pallas kernels for 7%

commit v1 on v0

--- a/solution.py
+++ b/solution.py
@@ -80,33 +80,34 @@
         packed[slot, BLOCK:, :] = part[slot]
 
 
-def chain_kernel(sources, near, far, chain, high, low, held, out):
+def chain_kernel(sources, give, near, far, *refs):
+    sends, (high, low, held, out) = refs[:-4], refs[-4:]
     groups, slots = near.shape[:2]
     half = groups * slots
     total = 2 * half
-    width = near.shape[2] - BLOCK
+    width = held.shape[1]
+    share = sends[0].shape[1]
     for q in range(total):
         ref = near if q < half else far
         group, slot = divmod(q % half, slots)
         high[q], low[q] = split(ref[group, slot, :BLOCK, :])
         held[q] = ref[group, slot, BLOCK:, :]
+    held[total] = jnp.zeros((width, BLOCK), f32)
     out[total] = jnp.zeros((width, BLOCK), f32)
 
     def step(j, carry):
         for q in range(total):
             first, second = split(held[q])
-            both = jnp.dot(
-                jnp.concatenate([first, second], 0), high[q], preferred_element_type=f32
-            )
-            rest = jnp.dot(first, low[q], preferred_element_type=f32)
-            out[q] = both[:width] + both[width:] + rest
+            both = plain_dot(jnp.concatenate([first, second], 0), high[q])
+            out[q] = both[:width] + both[width:] + plain_dot(first, low[q])
         for q in range(total):
             value = out[sources[q * slots]]
             for i in range(1, slots):
                 value += out[sources[q * slots + i]]
             held[q] = value
-        for slot in range(slots):
-            chain[j, slot] = held[slot]
+        for o, send in enumerate(sends):
+            for p in range(share):
+                send[j, p] = held[give[o * share + p]]
         return carry
 
     lax.fori_loop(0, ITERS, step, 0)
@@ -123,10 +124,11 @@
     return [piece] + [shift(piece, "cols", o) for o in others]
 
 
-def chain_gathered(gradient, factor, jacobi, tiles, whole_local, local, remote, live):
+def chain_gathered(gradient, factor, jacobi, tiles, whole_local, order, local, remote, live):
     width = gradient.shape[0]
     blocks, slots = jacobi.shape[0], local.shape[0]
     devices = lax.axis_size("rows")
+    columns = lax.axis_size("cols")
     groups = devices // 2
     packed = call(
         pack_kernel,
@@ -182,24 +184,27 @@
         & (lives[:, :, None] > 0)
     )
     sources = jnp.where(same, partner[:, None, :], total).reshape(-1)
-    chain = call(
+    share = order.shape[0] // columns
+    shape = jax.ShapeDtypeStruct
+    sends = call(
         chain_kernel,
-        jax.ShapeDtypeStruct((ITERS, slots, width, BLOCK), f32),
+        tuple([shape((ITERS, share, width, BLOCK), f32)] * columns),
         sources,
+        jnp.where(order < slots, order, total),
         near,
         far,
-        scalars=1,
+        scalars=2,
         scratch=[
             pltpu.VMEM((total, BLOCK, BLOCK), jnp.bfloat16),
             pltpu.VMEM((total, BLOCK, BLOCK), jnp.bfloat16),
-            pltpu.VMEM((total, width, BLOCK), f32),
+            pltpu.VMEM((total + 1, width, BLOCK), f32),
             pltpu.VMEM((total + 1, width, BLOCK), f32),
         ],
     )
-    return chain, pieces
-
-
-def chain_exchanged(gradient, jacobi, tiles, local, remote, live):
+    return list(sends), pieces
+
+
+def chain_exchanged(gradient, jacobi, tiles, order, local, remote, live):
     width = gradient.shape[0]
     blocks = jacobi.shape[0]
     devices = lax.axis_size("rows")
@@ -219,13 +224,18 @@
         )
         vector = jnp.einsum("kei,kn->nei", products, placing, precision=highest)
         steps.append(vector)
-    return jnp.stack(steps)
+    columns = lax.axis_size("cols")
+    share = order.shape[0] // columns
+    chain = jnp.pad(jnp.stack(steps), ((0, 0), (0, share * columns - blocks), (0, 0), (0, 0)))
+    return [
+        lax.dynamic_slice_in_dim(chain, order[o * share], share, 1) for o in range(columns)
+    ]
 
 
 def basis_kernel(turn, *refs):
     devices = len(refs) - 5
     pieces, jacobi = refs[:devices], refs[devices]
-    mixes, plain, smooth, scale = refs[devices + 1 :]
+    scaled, plain, smooth, scale = refs[devices + 1 :]
     width = pieces[0].shape[0]
     blocks = jacobi.shape[0]
     rows = blocks * BLOCK
@@ -241,31 +251,15 @@
     ratio = 2.0 / (STRETCH * bound * norm)
     scale[...] = jnp.broadcast_to(ratio, scale.shape)
     factor = factor * ratio
+    scaled[...] = factor
 
     row = lax.broadcasted_iota(jnp.int32, (width, BLOCK), 0)
     lane = lax.broadcasted_iota(jnp.int32, (width, BLOCK), 1)
-    kept = [[(row == lane).astype(f32)]]
+    kept = [(row == lane).astype(f32)]
     for k in range(ITERS):
-        last = kept[k]
-        terms = [last[0]] + [last[j] + last[j - 1] for j in range(1, k + 1)] + [last[k]]
-        image = dot(jnp.concatenate(terms, 0), factor)
-        fresh = []
-        for j in range(k + 2):
-            value = image[j * width : (j + 1) * width]
-            if j <= k:
-                value = value - last[j]
-            if k:
-                value = 2.0 * value
-                if j <= k - 1:
-                    value = value - kept[k - 1][j]
-            fresh.append(value)
-        kept.append(fresh)
-    at = 0
-    for j in range(1, ITERS + 1):
-        for k in range(j, ITERS + 1):
-            mixes[at : at + width, :] = kept[k][j]
-            at += width
-    first = jnp.concatenate([kept[k][0] for k in range(ITERS + 1)], 0)
+        value = dot(kept[k], factor) - kept[k]
+        kept.append(2.0 * value - kept[k - 1] if k else value)
+    first = jnp.concatenate(kept, 0)
     for b in range(blocks):
         columns = slice(b * BLOCK, (b + 1) * BLOCK)
         whole = jnp.concatenate([piece[:, columns] for piece in pieces], 0)
@@ -274,56 +268,84 @@
         smooth[b] = dot(value[: ITERS * width], jacobi[b])
 
 
-def mix_kernel(local, index, *refs):
-    devices = len(refs) - 8
-    chains = refs[:devices]
-    gradient, mixes, plain, smooth, jacobi = refs[devices : devices + 5]
-    added, smoothed, gram = refs[devices + 5 :]
-    slots, width = chains[0].shape[1:3]
+def make_basis(pieces, jacobi):
+    width = pieces[0].shape[0]
     blocks = jacobi.shape[0]
-    short = (ITERS - 1) * width
-    totals = [0.0] * ITERS
-    at = 0
-    for j in range(1, ITERS + 1):
-        count = (ITERS + 1 - j) * width
-        whole = jnp.concatenate(
-            [
-                jnp.concatenate([chain[j - 1, slot] for chain in chains], 0)
-                for slot in range(slots)
-            ],
-            1,
-        )
-        part = dot3(mixes[at : at + count, :], whole)
-        at += count
-        for k in range(j, ITERS + 1):
-            totals[k - 1] += part[(k - j) * width : (k - j + 1) * width]
-    for slot in range(slots):
-        columns = slice(slot * BLOCK, (slot + 1) * BLOCK)
-        value = jnp.concatenate([total[:, columns] for total in totals], 0)
-        added[slot] = value
-        smoothed[slot] = dot3(value[:short], jacobi[local[slot]])
-    added[slots] = jnp.zeros(added.shape[1:], f32)
-    smoothed[slots] = jnp.zeros(smoothed.shape[1:], f32)
-
+    shape = jax.ShapeDtypeStruct
+    turn = (BLOCK - width * lax.axis_index("cols")) % BLOCK
+    return call(
+        basis_kernel,
+        (
+            shape((BLOCK, BLOCK), f32),
+            shape((blocks, (ITERS + 1) * width, BLOCK), f32),
+            shape((blocks, ITERS * width, BLOCK), f32),
+            shape((8, BLOCK), f32),
+        ),
+        turn.astype(jnp.int32).reshape(1),
+        *pieces,
+        jacobi,
+        scalars=1,
+    )
+
+
+def mix_kernel(held, used, where, *refs):
+    devices = (len(refs) - 5) // 3
+    parts, pieces = refs[:devices], refs[devices : 2 * devices]
+    scaled, jacobi, plain, smooth = refs[2 * devices : 2 * devices + 4]
+    gram, backs = refs[2 * devices + 4], refs[2 * devices + 5 :]
+    share, width = parts[0].shape[1:3]
+    blocks = jacobi.shape[0]
+    none = devices * share
     sums = {}
+
+    def gather(s, y, weight):
+        y = [weight * value for value in y]
+        f = [s[0] + s[1]]
+        for j in range(1, ITERS):
+            f.append(0.5 * (s[j - 1] + s[j + 1]) + s[j])
+        for i in range(ITERS):
+            for j in range(i + 1):
+                sums[i, j] = sums.get((i, j), 0.0) + y[i] * f[j]
+            sums[i, ITERS] = sums.get((i, ITERS), 0.0) + y[i] * s[0]
+
+    for p in range(share):
+        block = held[p]
+        columns = pl.ds(pl.multiple_of(block * BLOCK, BLOCK), BLOCK)
+        now = [jnp.concatenate([piece[:, columns] for piece in pieces], 0)]
+        for j in range(ITERS):
+            now.append(jnp.concatenate([part[j, p] for part in parts], 0))
+        past = None
+        chosen = [now[0]]
+        for k in range(ITERS):
+            left = ITERS - k
+            image = dot3(
+                scaled[...], jnp.concatenate([now[i] + now[i + 1] for i in range(left)], 1)
+            )
+            fresh = []
+            for i in range(left):
+                value = image[:, i * BLOCK : (i + 1) * BLOCK] - now[i]
+                fresh.append(2.0 * value - past[i] if k else value)
+            past, now = now, fresh
+            chosen.append(now[0])
+        for o, back in enumerate(backs):
+            for k in range(ITERS):
+                back[k, p] = chosen[k + 1][o * width : (o + 1) * width]
+        soft = dot3(jnp.concatenate(chosen[:ITERS], 0), jacobi[block])
+        weight = jnp.where(used[p] > 0, 1.0, 0.0)
+        for r in range(0, BLOCK, 8):
+            gather(
+                [value[r : r + 8] for value in chosen],
+                [soft[k * BLOCK + r : k * BLOCK + r + 8] for k in range(ITERS)],
+                weight,
+            )
     for b in range(blocks):
-        slot = index[b]
+        weight = jnp.where(where[b] < none, 0.0, 1.0)
         for r in range(0, width, 8):
-            s = [plain[b, k * width + r : k * width + r + 8, :] for k in range(ITERS + 1)]
-            y = [smooth[b, k * width + r : k * width + r + 8, :] for k in range(ITERS)]
-            for k in range(1, ITERS + 1):
-                rows = slice((k - 1) * width + r, (k - 1) * width + r + 8)
-                s[k] = s[k] + added[slot, rows, :]
-                if k < ITERS:
-                    y[k] = y[k] + smoothed[slot, rows, :]
-            g = gradient[r : r + 8, b * BLOCK : (b + 1) * BLOCK]
-            f = [s[0] + s[1]]
-            for j in range(1, ITERS):
-                f.append(0.5 * (s[j - 1] + s[j + 1]) + s[j])
-            for i in range(ITERS):
-                for j in range(i + 1):
-                    sums[i, j] = sums.get((i, j), 0.0) + y[i] * f[j]
-                sums[i, ITERS] = sums.get((i, ITERS), 0.0) + y[i] * g
+            gather(
+                [plain[b, k * width + r : k * width + r + 8, :] for k in range(ITERS + 1)],
+                [smooth[b, k * width + r : k * width + r + 8, :] for k in range(ITERS)],
+                weight,
+            )
     lane = lax.broadcasted_iota(jnp.int32, (1, BLOCK), 1)
     result = jnp.zeros((1, BLOCK), f32)
     for (i, j), value in sums.items():
@@ -335,12 +357,12 @@
     gram[...] = result
 
 
-def finish_kernel(
-    index, grams, scale, gradient, plain, smooth, added, smoothed, solution, residual, extra, less
-):
+def finish_kernel(held, where, grams, scale, gradient, plain, smooth, jacobi, *refs):
+    backs, (solution, residual, extra, less) = refs[:-4], refs[-4:]
     width = gradient.shape[0]
     blocks = plain.shape[0]
-    slots = added.shape[0] - 1
+    share = backs[0].shape[1]
+    none = len(backs) * share
     flat = jnp.sum(grams[:, 0, :], axis=0, keepdims=True)
     row = lax.broadcasted_iota(jnp.int32, (8, BLOCK), 0)
     lane = lax.broadcasted_iota(jnp.int32, (8, BLOCK), 1)
@@ -372,16 +394,27 @@
             total = term if total is None else total + term
         return total
 
-    for slot in range(slots):
-        extra[slot] = combine(gives[1:], smoothed, slot, 0)
-        less[slot] = combine(takes[1:], added, slot, 0)
-    extra[slots] = jnp.zeros((width, BLOCK), f32)
-    less[slots] = jnp.zeros((width, BLOCK), f32)
+    for n in range(none):
+        back = backs[n // share]
+        total, left = 0.0, 0.0
+        for k in range(ITERS):
+            value = back[k, n % share]
+            left = left + takes[k + 1] * value
+            if k + 1 < ITERS:
+                total = total + gives[k + 1] * value
+        less[n] = left
+        extra[n] = dot3(total, jacobi[held[n]])
+    extra[none] = jnp.zeros((width, BLOCK), f32)
+    less[none] = jnp.zeros((width, BLOCK), f32)
     for b in range(blocks):
         columns = slice(b * BLOCK, (b + 1) * BLOCK)
-        slot = index[b]
-        solution[:, columns] = combine(gives, smooth, b, 0) + extra[slot]
-        residual[:, columns] = gradient[:, columns] - combine(takes, plain, b, 0) - less[slot]
+        n = where[b]
+        own = n >= none
+        rest = jnp.where(own, combine(gives[1:], smooth, b, 1), extra[n])
+        solution[:, columns] = gives[0] * smooth[b, :width, :] + rest
+        rest = jnp.where(own, combine(takes[1:], plain, b, 1), less[n])
+        start = gradient[:, columns]
+        residual[:, columns] = start - takes[0] * start - rest
 
 
 def on_device(
@@ -403,55 +436,54 @@
     live = jnp.arange(slots, dtype=jnp.int32) < tile_count[0]
     lists = (tile_local[:slots], tile_remote[:slots], live)
 
-    numbers = jnp.arange(blocks, dtype=jnp.int32)
     gathered = devices * slots * BLOCK * (BLOCK + width) * 4
-    if gathered <= GATHER_BYTES and devices % 2 == 0 and not exchange:
-        chain, pieces = chain_gathered(
-            gradient, width_factor, jacobi_inverse, coupling_tiles, tile_local, *lists
+    whole = gathered <= GATHER_BYTES and devices % 2 == 0 and not exchange
+    units = slots if whole else blocks
+    share = -(-units // columns)
+    numbers = jnp.arange(columns * share, dtype=jnp.int32)
+    dealer = (lax.axis_index("cols") + columns - numbers // share) % columns
+    order = dealer * share + numbers % share
+    if whole:
+        sends, pieces = chain_gathered(
+            gradient, width_factor, jacobi_inverse, coupling_tiles, tile_local, order, *lists
         )
-        at = tile_local
-        here = (lists[0][None, :] == numbers[:, None]) & live[None, :]
-        order = jnp.arange(slots, dtype=jnp.int32)[None, :]
-        index = jnp.min(jnp.where(here, order, slots), axis=1)
+        local = lists[0]
+        earlier = jnp.arange(slots)[:, None] > jnp.arange(slots)[None, :]
+        repeat = jnp.any(earlier & (local[:, None] == local[None, :]), axis=1)
+        fit = order[:, None] == jnp.arange(slots, dtype=jnp.int32)[None, :]
+        held = jnp.sum(jnp.where(fit, local[None, :], 0), axis=1)
+        used = jnp.sum(jnp.where(fit & (live & ~repeat)[None, :], 1, 0), axis=1)
     else:
-        chain = chain_exchanged(gradient, jacobi_inverse, coupling_tiles[:slots], *lists)
+        sends = chain_exchanged(
+            gradient, jacobi_inverse, coupling_tiles[:slots], order, *lists
+        )
         pieces = whole_pieces(gradient, width_factor)
-        at, index = numbers, numbers
-    units = chain.shape[1]
-    chains = [chain] + [shift(chain, "cols", o) for o in range(1, columns)]
-
-    turn = (BLOCK - width * lax.axis_index("cols")) % BLOCK
+        held = jnp.minimum(order, blocks - 1)
+        used = (order < blocks).astype(jnp.int32)
+    mine = (held[None, :] == jnp.arange(blocks, dtype=jnp.int32)[:, None]) & (used > 0)[None, :]
+    where = jnp.min(jnp.where(mine, numbers[None, :], columns * share), axis=1)
+    parts = [sends[0]]
+    for o in range(1, columns):
+        parts.append(shift(sends[o], "cols", o))
+
     shape = jax.ShapeDtypeStruct
-    count = ITERS * (ITERS + 1) // 2
-    mixes, plain, smooth, scale = call(
-        basis_kernel,
-        (
-            shape((count * width, BLOCK), f32),
-            shape((blocks, (ITERS + 1) * width, BLOCK), f32),
-            shape((blocks, ITERS * width, BLOCK), f32),
-            shape((8, BLOCK), f32),
+    scaled, plain, smooth, scale = make_basis(pieces, jacobi_inverse)
+    gram, *backs = call(
+        mix_kernel,
+        tuple(
+            [shape((1, BLOCK), f32)]
+            + [shape((ITERS, share, width, BLOCK), f32)] * columns
         ),
-        turn.astype(jnp.int32).reshape(1),
+        held,
+        used,
+        where,
+        *parts,
         *pieces,
+        scaled,
         jacobi_inverse,
-        scalars=1,
-    )
-    added, smoothed, gram = call(
-        mix_kernel,
-        (
-            shape((units + 1, ITERS * width, BLOCK), f32),
-            shape((units + 1, (ITERS - 1) * width, BLOCK), f32),
-            shape((1, BLOCK), f32),
-        ),
-        at,
-        index,
-        *chains,
-        gradient,
-        mixes,
         plain,
         smooth,
-        jacobi_inverse,
-        scalars=2,
+        scalars=3,
     )
     everyone = columns * devices
     grams = lax.all_to_all(
@@ -461,19 +493,22 @@
         0,
         tiled=True,
     )
+    for o in range(1, columns):
+        backs[o] = shift(backs[o], "cols", -o)
     return call(
         finish_kernel,
         (shape((width, rows), f32), shape((width, rows), f32)),
-        index,
+        held,
+        where,
         grams,
         scale,
         gradient,
         plain,
         smooth,
-        added,
-        smoothed,
-        scalars=1,
-        scratch=[pltpu.VMEM((units + 1, width, BLOCK), f32)] * 2,
+        jacobi_inverse,
+        *backs,
+        scalars=2,
+        scratch=[pltpu.VMEM((columns * share + 1, width, BLOCK), f32)] * 2,
     )
 
 

time: 70.9 us -> 67.3 us (0.949)
  waiting for transfers between devices: 21.4 us -> 14.2 us
  starting transfers between devices: 18.4 us -> 21.4 us
  Pallas kernels: 15.8 us -> 17 us
  blocking collectives: 10.9 us -> 9.86 us
    ppermute x9 -> x12, waiting for transfers between devices: 7.4 us -> 0.6 us  [shift(): return lax.ppermute(x, axis, [(i, (i - by) % size) for i in range(size)])]
    ppermute x9 -> x12, starting transfers between devices: 15 us -> 18.1 us  [shift(): return lax.ppermute(x, axis, [(i, (i - by) % size) for i in range(size)])]
    pallas_call x5, Pallas kernels: 15.8 us -> 17 us  [call(): pl.pallas_call(kernel, out_shape=outs, in_specs=specs, out_specs=tuple([V...]
    all_to_all x1, blocking collectives: 10.9 us -> 9.86 us  [on_device(): lax.all_to_all(jnp.broadcast_to(gram[None], (everyone, 1, BLOCK)), ('cols...]
  transfers between devices with their start and end apart: 11 -> 14, of which waited for: 4 -> 3; matrix products, arithmetic and copies ran while one was open for 3% -> 3% of each run, Pallas kernels for 7% -> 7%
where the time goes in v1:
time: 67.3 us; the launch traced here: 67 us
  starting transfers between devices  21.4 us (32%)
  Pallas kernels  17 us (25%)
  waiting for transfers between devices  14.2 us (21%)
  blocking collectives  9.86 us (15%)
  local copies, waits for them, and re-layouts  1.79 us (3%)
  between operations  1.5 us (2%)
  other arithmetic  1.26 us (2%)
    ppermute x12, starting transfers between devices, shift(): return lax.ppermute(x, axis, [(i, (i - by) % size) for i in range(size)])  18.1 us
    pallas_call x5, Pallas kernels, call(): pl.pallas_call(kernel, out_shape=outs, in_specs=specs, out_specs=tuple([V...  17 us
    all_to_all x1, waiting for transfers between devices, chain_gathered(): told = lax.all_to_all(told, 'rows', 0, 0, tiled=True)[:, 0]  11.9 us
    all_to_all x1, blocking collectives, on_device(): lax.all_to_all(jnp.broadcast_to(gram[None], (everyone, 1, BLOCK)), ('cols...  9.86 us
    all_to_all x1, starting transfers between devices, chain_gathered(): told = lax.all_to_all(told, 'rows', 0, 0, tiled=True)[:, 0]  3.31 us
    ppermute x1, waiting for transfers between devices, chain_gathered(): far = lax.ppermute(near, 'rows', [(i, i ^ 1) for i in range(devices)])  1.63 us
  transfers between devices with their start and end apart: 14, of which 3 were waited for; matrix products, arithmetic and copies ran while one was open for 3% of the time, Pallas kernels for 7%

profile of v1, /device:TPU:0, one launch (start us, length us, event | category | flops | bytes accessed | tf_op | source)
XLA Modules:
  0.0 67.0 jit_solution(17659816850704120594)
XLA Ops:
  0.7 3.0 %shard_map.86 = f32[3,160,128]{2,1,0:T(8,128)} custom-call(s32[4]{0:T(128)} %local.1, f32[32,1024]{1,0:T(8,128)} %gradient.3, f32[8,128,128]{2,1,0:T(8,128)} %jacobi.3, bf16[4,128,128]{2,1,0:T(8,128)(2,1)} %tiles.1), custom_call_target="tpu_custom_call" | custom-call | tf_op jit(solution)/shard_map/pallas_call | solution.py:31
  3.7 3.0 %collective-permute-start.5 = (f32[32,1152]{1,0:T(8,128)S(1)}, f32[32,1152]{1,0:T(8,128)S(1)}, u32[]{:S(2)}, u32[]{:S(2)}) collective-permute-start(f32[32,1152]{1,0:T(8,128)S(1)} %pad_maximum_fusion.1.refs_0_.refs_4_), channel_id=1, source_target_pairs={{0,8},{8,16},{16,24},{24,0},{1,9},{9,17},{17,25},{25,1},{2,10},{10... | collective-permute-start | bytes 442376 | tf_op jit(solution)/shard_map/ppermute | solution.py:118
  6.7 1.5 %collective-permute-start.4 = (f32[32,1152]{1,0:T(8,128)S(1)}, f32[32,1152]{1,0:T(8,128)S(1)}, u32[]{:S(2)}, u32[]{:S(2)}) collective-permute-start(f32[32,1152]{1,0:T(8,128)S(1)} %pad_maximum_fusion.1.refs_0_.refs_4_), channel_id=1, source_target_pairs={{0,16},{8,24},{16,0},{24,8},{1,17},{9,25},{17,1},{25,9},{2,18},{10... | collective-permute-start | bytes 442376 | tf_op jit(solution)/shard_map/ppermute | solution.py:118
  8.2 1.6 %collective-permute-start.2 = (f32[3,160,128]{2,1,0:T(8,128)S(1)}, f32[3,160,128]{2,1,0:T(8,128)S(1)}, u32[]{:S(2)}, u32[]{:S(2)}) collective-permute-start(f32[3,160,128]{2,1,0:T(8,128)S(1)} %copy-done.2), channel_id=1, source_target_pairs={{0,2},{1,3},{2,4},{3,5},{4,6},{5,7},{6,0},{7,1},{8,10},{9,11},{10,... | collective-permute-start | bytes 737288 | tf_op jit(solution)/shard_map/ppermute | solution.py:118
  9.8 2.6 %collective-permute-start.1 = (f32[3,160,128]{2,1,0:T(8,128)S(1)}, f32[3,160,128]{2,1,0:T(8,128)S(1)}, u32[]{:S(2)}, u32[]{:S(2)}) collective-permute-start(f32[3,160,128]{2,1,0:T(8,128)S(1)} %copy-done.2), channel_id=1, source_target_pairs={{0,4},{1,5},{2,6},{3,7},{4,0},{5,1},{6,2},{7,3},{8,12},{9,13},{10,... | collective-permute-start | bytes 737288 | tf_op jit(solution)/shard_map/ppermute | solution.py:118
  12.4 1.3 %collective-permute-start = (f32[3,160,128]{2,1,0:T(8,128)S(1)}, f32[3,160,128]{2,1,0:T(8,128)S(1)}, u32[]{:S(2)}, u32[]{:S(2)}) collective-permute-start(f32[3,160,128]{2,1,0:T(8,128)S(1)} %copy-done.2), channel_id=1, source_target_pairs={{0,6},{1,7},{2,0},{3,1},{4,2},{5,3},{6,4},{7,5},{8,14},{9,15},{10,... | collective-permute-start | bytes 737288 | tf_op jit(solution)/shard_map/ppermute | solution.py:118
  14.4 0.6 copy-done.4
  15.1 0.6 broadcast_in_dim.107
  15.7 3.3 %all-to-all-start = ((s32[8,1,128]{2,1,0:T(1,128)}), s32[8,1,128]{2,1,0:T(1,128)S(1)}, u32[]{:S(2)}, u32[]{:S(2)}) async-start(s32[8,1,128]{2,1,0:T(1,128)} %broadcast_in_dim.107), calls=%async_computation | async-start | bytes 8192 | tf_op jit(solution)/shard_map/all_to_all | solution.py:156
  19.1 0.2 fusion.6
  19.4 0.2 select_reduce_fusion.2
  19.5 1.5 %collective-permute-start.3 = (f32[32,1152]{1,0:T(8,128)S(1)}, f32[32,1152]{1,0:T(8,128)S(1)}, u32[]{:S(2)}, u32[]{:S(2)}) collective-permute-start(f32[32,1152]{1,0:T(8,128)S(1)} %pad_maximum_fusion.1.refs_0_.refs_4_), channel_id=1, source_target_pairs={{0,24},{8,0},{16,8},{24,16},{1,25},{9,1},{17,9},{25,17},{2,26},{10... | collective-permute-start | bytes 442376 | tf_op jit(solution)/shard_map/ppermute | solution.py:118
  21.2 11.9 %all-to-all-done = s32[8,1,128]{2,1,0:T(1,128)S(1)} async-done(((s32[8,1,128]{2,1,0:T(1,128)}), s32[8,1,128]{2,1,0:T(1,128)S(1)}, u32[]{:S(2)}, u32[]{:S(2)}) %all-to-all-start) | async-done | bytes 4128 | tf_op jit(solution)/shard_map/all_to_all | solution.py:156
  33.3 0.1 multiply_reduce_fusion
  33.5 0.1 gt.39
  33.7 0.2 select_reduce_fusion
  34.0 0.1 and_select_fusion
  34.1 0.1 select_n.102.sources
  34.2 1.6 %collective-permute-done.6.far = f32[4,3,160,128]{3,2,1,0:T(8,128)S(1)} collective-permute-done((f32[4,3,160,128]{3,2,1,0:T(8,128)S(1)}, f32[4,3,160,128]{3,2,1,0:T(8,128)S(1)}, u32[]{:S(2)}, u32[]{:S(2)}) %collective-permute-start.6) | collective-permute-done | bytes 983072 | tf_op jit(solution)/shard_map/ppermute | solution.py:159
  35.9 4.3 %shard_map.87 = (f32[6,1,32,128]{3,2,1,0:T(8,128)S(1)}, f32[6,1,32,128]{3,2,1,0:T(8,128)S(1)}, f32[6,1,32,128]{3,2,1,0:T(8,128)S(1)}, f32[6,1,32,128]{3,2,1,0:T(8,128)S(1)}) custom-call(s32[72]{0:T(128)S(1)} %select_n.102.sources, s32[4]{0:T(128)S(1)} %compare_select_fusion.give, f32[4,3,160,128]{3,2,1,0:T(8,128)S(1)} %pad_maximum_fusion.near, ...), custom_call_target="tpu_custom_call" | custom-call | tf_op jit(solution)/shard_map/pallas_call | solution.py:31
  40.1 1.5 %collective-permute-start.7 = (f32[6,1,32,128]{3,2,1,0:T(8,128)S(1)}, f32[6,1,32,128]{3,2,1,0:T(8,128)S(1)}, u32[]{:S(2)}, u32[]{:S(2)}) collective-permute-start(f32[6,1,32,128]{3,2,1,0:T(8,128)S(1)} %get-tuple-element.34), channel_id=1, source_target_pairs={{0,24},{8,0},{16,8},{24,16},{1,25},{9,1},{17,9},{25,17},{2,26},{10... | collective-permute-start | bytes 294920 | tf_op jit(solution)/shard_map/ppermute | solution.py:118
  41.6 0.5 collective-permute-start.8
  42.1 0.6 collective-permute-start.9
  42.7 0.1 select_reduce_fusion.1.where
  42.8 4.9 %shard_map.88 = (f32[128,128]{1,0:T(8,128)S(1)}, f32[8,224,128]{2,1,0:T(8,128)S(1)}, f32[8,192,128]{2,1,0:T(8,128)S(1)}, f32[8,128]{1,0:T(8,128)S(1)}) custom-call(s32[1]{0:T(128)} %bitcast.7.turn, f32[32,1152]{1,0:T(8,128)S(1)} %pad_maximum_fusion.1.refs_0_.refs_4_, f32[32,1152]{1,0:T(8,128)S(1)} %collective-permute-done.3.refs_1_.refs_5_, ...), custom_call_target="tpu_custom_call" | custom-call | tf_op jit(solution)/shard_map/pallas_call | solution.py:31
  47.8 0.6 collective-permute-done.8.refs_2_
  48.4 2.8 %shard_map.89 = (f32[1,128]{1,0:T(1,128)S(1)}, f32[6,1,32,128]{3,2,1,0:T(8,128)S(1)}, f32[6,1,32,128]{3,2,1,0:T(8,128)S(1)}, f32[6,1,32,128]{3,2,1,0:T(8,128)S(1)}, f32[6,1,32,128]{3,2,1,0:T(8,128)S(1)}) custom-call(s32[4]{0:T(128)S(1)} %get-tuple-element.51.held, s32[4]{0:T(128)S(1)} %get-tuple-element.50.used, s32[8]{0:T(128)S(1)} %select_reduce_fusion.1.where, ...), custom_call_target="tpu_custom_call" | custom-call | tf_op jit(solution)/shard_map/pallas_call | solution.py:31
  51.1 1.9 %collective-permute-start.10 = (f32[6,1,32,128]{3,2,1,0:T(8,128)S(1)}, f32[6,1,32,128]{3,2,1,0:T(8,128)S(1)}, u32[]{:S(2)}, u32[]{:S(2)}) collective-permute-start(f32[6,1,32,128]{3,2,1,0:T(8,128)S(1)} %get-tuple-element.47), channel_id=1, source_target_pairs={{0,8},{8,16},{16,24},{24,0},{1,9},{9,17},{17,25},{25,1},{2,10},{10... | collective-permute-start | bytes 294920 | tf_op jit(solution)/shard_map/ppermute | solution.py:118
  53.0 0.5 collective-permute-start.11
  53.5 1.6 %collective-permute-start.12 = (f32[6,1,32,128]{3,2,1,0:T(8,128)S(1)}, f32[6,1,32,128]{3,2,1,0:T(8,128)S(1)}, u32[]{:S(2)}, u32[]{:S(2)}) collective-permute-start(f32[6,1,32,128]{3,2,1,0:T(8,128)S(1)} %get-tuple-element.49), channel_id=1, source_target_pairs={{0,24},{8,0},{16,8},{24,16},{1,25},{9,1},{17,9},{25,17},{2,26},{10... | collective-permute-start | bytes 294920 | tf_op jit(solution)/shard_map/ppermute | solution.py:118
  55.1 9.9 %all_to_all.10.grams = f32[32,1,128]{2,1,0:T(1,128)S(1)} all-to-all(f32[32,1,128]{2,1,0:T(1,128)S(1)} %broadcast_in_dim.116), channel_id=1, replica_groups=mesh['cols'=4,'rows'=8] {'cols','rows'}, dimensions={0} | all-to-all | bytes 32768 | tf_op jit(solution)/shard_map/all_to_all | solution.py:489
  64.9 2.1 %shard_map.90 = (f32[32,1024]{1,0:T(8,128)}, f32[32,1024]{1,0:T(8,128)}) custom-call(s32[4]{0:T(128)S(1)} %get-tuple-element.51.held, s32[8]{0:T(128)S(1)} %select_reduce_fusion.1.where, f32[32,1,128]{2,1,0:T(1,128)S(1)} %all_to_all.10.grams, f32[8,128]{1,0:T(8,128)S(1)} %get-tuple-element.45.scale, f32[32,1024]{1,0:T(8,128)S(1)} %copy-done.1, ...), custom_call_target="tpu_custom_call" | custom-call | tf_op jit(solution)/shard_map/pallas_call | solution.py:31
  (41 shorter events, 0.9 us)
Async XLA Ops:
  0.6 3.0 %copy-start.1 = (f32[32,1024]{1,0:T(8,128)S(1)}, f32[32,1024]{1,0:T(8,128)}, u32[]{:S(2)}) copy-start(f32[32,1024]{1,0:T(8,128)} %gradient.3) | copy-start | bytes 393220
  0.6 3.0 %copy-start.3 = (f32[128,32]{0,1:T(8,128)S(1)}, f32[128,32]{0,1:T(8,128)}, u32[]{:S(2)}) copy-start(f32[128,32]{0,1:T(8,128)} %param.9) | copy-start | bytes 49156
  3.6 4.6 %copy-start.2 = (f32[3,160,128]{2,1,0:T(8,128)S(1)}, f32[3,160,128]{2,1,0:T(8,128)}, u32[]{:S(2)}) copy-start(f32[3,160,128]{2,1,0:T(8,128)} %shard_map.86) | copy-start | bytes 737284
  3.7 15.9 %collective-permute-start.5 = (f32[32,1152]{1,0:T(8,128)S(1)}, f32[32,1152]{1,0:T(8,128)S(1)}, u32[]{:S(2)}, u32[]{:S(2)}) collective-permute-start(f32[32,1152]{1,0:T(8,128)S(1)} %pad_maximum_fusion.1.refs_0_.refs_4_), channel_id=1, source_target_pairs={{0,8},{8,16},{16,24},{24,0},{1,9},{9,17},{17,25},{25,1},{2,10},{10... | collective-permute-start | bytes 442376 | tf_op jit(solution)/shard_map/ppermute | solution.py:118
  6.7 26.4 %collective-permute-start.4 = (f32[32,1152]{1,0:T(8,128)S(1)}, f32[32,1152]{1,0:T(8,128)S(1)}, u32[]{:S(2)}, u32[]{:S(2)}) collective-permute-start(f32[32,1152]{1,0:T(8,128)S(1)} %pad_maximum_fusion.1.refs_0_.refs_4_), channel_id=1, source_target_pairs={{0,16},{8,24},{16,0},{24,8},{1,17},{9,25},{17,1},{25,9},{2,18},{10... | collective-permute-start | bytes 442376 | tf_op jit(solution)/shard_map/ppermute | solution.py:118
  8.2 24.9 %collective-permute-start.2 = (f32[3,160,128]{2,1,0:T(8,128)S(1)}, f32[3,160,128]{2,1,0:T(8,128)S(1)}, u32[]{:S(2)}, u32[]{:S(2)}) collective-permute-start(f32[3,160,128]{2,1,0:T(8,128)S(1)} %copy-done.2), channel_id=1, source_target_pairs={{0,2},{1,3},{2,4},{3,5},{4,6},{5,7},{6,0},{7,1},{8,10},{9,11},{10,... | collective-permute-start | bytes 737288 | tf_op jit(solution)/shard_map/ppermute | solution.py:118
  9.8 23.4 %collective-permute-start.1 = (f32[3,160,128]{2,1,0:T(8,128)S(1)}, f32[3,160,128]{2,1,0:T(8,128)S(1)}, u32[]{:S(2)}, u32[]{:S(2)}) collective-permute-start(f32[3,160,128]{2,1,0:T(8,128)S(1)} %copy-done.2), channel_id=1, source_target_pairs={{0,4},{1,5},{2,6},{3,7},{4,0},{5,1},{6,2},{7,3},{8,12},{9,13},{10,... | collective-permute-start | bytes 737288 | tf_op jit(solution)/shard_map/ppermute | solution.py:118
  12.4 20.8 %collective-permute-start = (f32[3,160,128]{2,1,0:T(8,128)S(1)}, f32[3,160,128]{2,1,0:T(8,128)S(1)}, u32[]{:S(2)}, u32[]{:S(2)}) collective-permute-start(f32[3,160,128]{2,1,0:T(8,128)S(1)} %copy-done.2), channel_id=1, source_target_pairs={{0,6},{1,7},{2,0},{3,1},{4,2},{5,3},{6,4},{7,5},{8,14},{9,15},{10,... | collective-permute-start | bytes 737288 | tf_op jit(solution)/shard_map/ppermute | solution.py:118
  14.4 0.7 copy-start.4
  14.4 0.7 copy-start.5
  15.7 17.4 %all-to-all-start = ((s32[8,1,128]{2,1,0:T(1,128)}), s32[8,1,128]{2,1,0:T(1,128)S(1)}, u32[]{:S(2)}, u32[]{:S(2)}) async-start(s32[8,1,128]{2,1,0:T(1,128)} %broadcast_in_dim.107), calls=%async_computation | async-start | bytes 8192 | tf_op jit(solution)/shard_map/all_to_all | solution.py:156
  19.5 13.6 %collective-permute-start.3 = (f32[32,1152]{1,0:T(8,128)S(1)}, f32[32,1152]{1,0:T(8,128)S(1)}, u32[]{:S(2)}, u32[]{:S(2)}) collective-permute-start(f32[32,1152]{1,0:T(8,128)S(1)} %pad_maximum_fusion.1.refs_0_.refs_4_), channel_id=1, source_target_pairs={{0,24},{8,0},{16,8},{24,16},{1,25},{9,1},{17,9},{25,17},{2,26},{10... | collective-permute-start | bytes 442376 | tf_op jit(solution)/shard_map/ppermute | solution.py:118
  33.2 2.6 %collective-permute-start.6 = (f32[4,3,160,128]{3,2,1,0:T(8,128)S(1)}, f32[4,3,160,128]{3,2,1,0:T(8,128)S(1)}, u32[]{:S(2)}, u32[]{:S(2)}) collective-permute-start(f32[4,3,160,128]{3,2,1,0:T(8,128)S(1)} %pad_maximum_fusion.near), channel_id=1, source_target_pairs={{0,1},{1,0},{2,3},{3,2},{4,5},{5,4},{6,7},{7,6},{8,9},{9,8},{10,11... | collective-permute-start | bytes 2949128 | tf_op jit(solution)/shard_map/ppermute | solution.py:159
  34.2 8.6 %copy-start = (f32[8,128,128]{2,1,0:T(8,128)S(1)}, f32[8,128,128]{2,1,0:T(8,128)}, u32[]{:S(2)}) copy-start(f32[8,128,128]{2,1,0:T(8,128)} %jacobi.3) | copy-start | bytes 1572868
  40.1 7.6 %collective-permute-start.7 = (f32[6,1,32,128]{3,2,1,0:T(8,128)S(1)}, f32[6,1,32,128]{3,2,1,0:T(8,128)S(1)}, u32[]{:S(2)}, u32[]{:S(2)}) collective-permute-start(f32[6,1,32,128]{3,2,1,0:T(8,128)S(1)} %get-tuple-element.34), channel_id=1, source_target_pairs={{0,24},{8,0},{16,8},{24,16},{1,25},{9,1},{17,9},{25,17},{2,26},{10... | collective-permute-start | bytes 294920 | tf_op jit(solution)/shard_map/ppermute | solution.py:118
  41.6 6.7 %collective-permute-start.8 = (f32[6,1,32,128]{3,2,1,0:T(8,128)S(1)}, f32[6,1,32,128]{3,2,1,0:T(8,128)S(1)}, u32[]{:S(2)}, u32[]{:S(2)}) collective-permute-start(f32[6,1,32,128]{3,2,1,0:T(8,128)S(1)} %get-tuple-element.35), channel_id=1, source_target_pairs={{0,16},{8,24},{16,0},{24,8},{1,17},{9,25},{17,1},{25,9},{2,18},{10... | collective-permute-start | bytes 294920 | tf_op jit(solution)/shard_map/ppermute | solution.py:118
  42.1 6.2 %collective-permute-start.9 = (f32[6,1,32,128]{3,2,1,0:T(8,128)S(1)}, f32[6,1,32,128]{3,2,1,0:T(8,128)S(1)}, u32[]{:S(2)}, u32[]{:S(2)}) collective-permute-start(f32[6,1,32,128]{3,2,1,0:T(8,128)S(1)} %get-tuple-element.36), channel_id=1, source_target_pairs={{0,8},{8,16},{16,24},{24,0},{1,9},{9,17},{17,25},{25,1},{2,10},{10... | collective-permute-start | bytes 294920 | tf_op jit(solution)/shard_map/ppermute | solution.py:118
  51.1 13.8 %collective-permute-start.10 = (f32[6,1,32,128]{3,2,1,0:T(8,128)S(1)}, f32[6,1,32,128]{3,2,1,0:T(8,128)S(1)}, u32[]{:S(2)}, u32[]{:S(2)}) collective-permute-start(f32[6,1,32,128]{3,2,1,0:T(8,128)S(1)} %get-tuple-element.47), channel_id=1, source_target_pairs={{0,8},{8,16},{16,24},{24,0},{1,9},{9,17},{17,25},{25,1},{2,10},{10... | collective-permute-start | bytes 294920 | tf_op jit(solution)/shard_map/ppermute | solution.py:118
  53.0 11.9 %collective-permute-start.11 = (f32[6,1,32,128]{3,2,1,0:T(8,128)S(1)}, f32[6,1,32,128]{3,2,1,0:T(8,128)S(1)}, u32[]{:S(2)}, u32[]{:S(2)}) collective-permute-start(f32[6,1,32,128]{3,2,1,0:T(8,128)S(1)} %get-tuple-element.48), channel_id=1, source_target_pairs={{0,16},{8,24},{16,0},{24,8},{1,17},{9,25},{17,1},{25,9},{2,18},{10... | collective-permute-start | bytes 294920 | tf_op jit(solution)/shard_map/ppermute | solution.py:118
  53.5 11.4 %collective-permute-start.12 = (f32[6,1,32,128]{3,2,1,0:T(8,128)S(1)}, f32[6,1,32,128]{3,2,1,0:T(8,128)S(1)}, u32[]{:S(2)}, u32[]{:S(2)}) collective-permute-start(f32[6,1,32,128]{3,2,1,0:T(8,128)S(1)} %get-tuple-element.49), channel_id=1, source_target_pairs={{0,24},{8,0},{16,8},{24,16},{1,25},{9,1},{17,9},{25,17},{2,26},{10... | collective-permute-start | bytes 294920 | tf_op jit(solution)/shard_map/ppermute | solution.py:118

commit v2 on v1

--- a/solution.py
+++ b/solution.py
@@ -12,6 +12,7 @@
 GATHER_BYTES = 8 * 2**20
 
 
+NOWHERE = 2**20
 GRANT_BYTES = 24 * 2**20
 WHOLE_BYTES = 60 * 2**20
 
@@ -124,7 +125,7 @@
     return [piece] + [shift(piece, "cols", o) for o in others]
 
 
-def chain_gathered(gradient, factor, jacobi, tiles, whole_local, order, local, remote, live):
+def chain_gathered(gradient, factor, jacobi, tiles, whole_local, order, where, local, remote, live):
     width = gradient.shape[0]
     blocks, slots = jacobi.shape[0], local.shape[0]
     devices = lax.axis_size("rows")
@@ -153,8 +154,10 @@
     own = jnp.concatenate([local, remote, live.astype(jnp.int32)])
     own = jnp.pad(own, (0, BLOCK - own.shape[0]))
     told = jnp.broadcast_to(own[None, None, :], (devices, 1, BLOCK))
-    told = lax.all_to_all(told, "rows", 0, 0, tiled=True)[:, 0]
-    near, pieces, told = lax.optimization_barrier((near, pieces, told))
+    told = lax.all_to_all(told, "rows", 0, 0, tiled=True)
+    told = told[:, 0]
+    basis = make_basis(pieces, jacobi, where)
+    near, basis, told = lax.optimization_barrier((near, basis, told))
     near = jnp.stack(near)
     far = lax.ppermute(near, "rows", [(i, i ^ 1) for i in range(devices)])
 
@@ -201,7 +204,7 @@
             pltpu.VMEM((total + 1, width, BLOCK), f32),
         ],
     )
-    return list(sends), pieces
+    return list(sends), pieces, basis
 
 
 def chain_exchanged(gradient, jacobi, tiles, order, local, remote, live):
@@ -232,10 +235,33 @@
     ]
 
 
-def basis_kernel(turn, *refs):
+def gather_sums(sums, s, y, weight):
+    y = [weight * value for value in y]
+    f = [s[0] + s[1]]
+    for j in range(1, ITERS):
+        f.append(0.5 * (s[j - 1] + s[j + 1]) + s[j])
+    for i in range(ITERS):
+        for j in range(i + 1):
+            sums[i, j] = sums.get((i, j), 0.0) + y[i] * f[j]
+        sums[i, ITERS] = sums.get((i, ITERS), 0.0) + y[i] * s[0]
+
+
+def flat_sums(sums):
+    lane = lax.broadcasted_iota(jnp.int32, (1, BLOCK), 1)
+    result = jnp.zeros((1, BLOCK), f32)
+    for (i, j), value in sums.items():
+        value = jnp.sum(jnp.sum(value, axis=0, keepdims=True), axis=1, keepdims=True)
+        here = lane == 16 * i + j
+        if j < ITERS:
+            here = here | (lane == 16 * j + i)
+        result = jnp.where(here, value, result)
+    return result
+
+
+def basis_kernel(turn, where, *refs):
     devices = len(refs) - 5
     pieces, jacobi = refs[:devices], refs[devices]
-    scaled, plain, smooth, scale = refs[devices + 1 :]
+    scaled, powers, gram, scale = refs[devices + 1 :]
     width = pieces[0].shape[0]
     blocks = jacobi.shape[0]
     rows = blocks * BLOCK
@@ -260,54 +286,50 @@
         value = dot(kept[k], factor) - kept[k]
         kept.append(2.0 * value - kept[k - 1] if k else value)
     first = jnp.concatenate(kept, 0)
+    powers[...] = first
+    sums = {}
     for b in range(blocks):
         columns = slice(b * BLOCK, (b + 1) * BLOCK)
-        whole = jnp.concatenate([piece[:, columns] for piece in pieces], 0)
-        value = dot(first, whole)
-        plain[b] = value
-        smooth[b] = dot(value[: ITERS * width], jacobi[b])
-
-
-def make_basis(pieces, jacobi):
+        plain = dot(first, jnp.concatenate([piece[:, columns] for piece in pieces], 0))
+        smooth = dot(plain[: ITERS * width], jacobi[b])
+        weight = jnp.where(where[b] < NOWHERE, 0.0, 1.0)
+        for r in range(0, width, 8):
+            gather_sums(
+                sums,
+                [plain[k * width + r : k * width + r + 8] for k in range(ITERS + 1)],
+                [smooth[k * width + r : k * width + r + 8] for k in range(ITERS)],
+                weight,
+            )
+    gram[...] = flat_sums(sums)
+
+
+def make_basis(pieces, jacobi, where):
     width = pieces[0].shape[0]
-    blocks = jacobi.shape[0]
     shape = jax.ShapeDtypeStruct
     turn = (BLOCK - width * lax.axis_index("cols")) % BLOCK
     return call(
         basis_kernel,
         (
             shape((BLOCK, BLOCK), f32),
-            shape((blocks, (ITERS + 1) * width, BLOCK), f32),
-            shape((blocks, ITERS * width, BLOCK), f32),
+            shape(((ITERS + 1) * width, BLOCK), f32),
+            shape((1, BLOCK), f32),
             shape((8, BLOCK), f32),
         ),
         turn.astype(jnp.int32).reshape(1),
+        where,
         *pieces,
         jacobi,
-        scalars=1,
-    )
-
-
-def mix_kernel(held, used, where, *refs):
-    devices = (len(refs) - 5) // 3
+        scalars=2,
+    )
+
+
+def mix_kernel(held, used, *refs):
+    devices = (len(refs) - 4) // 3
     parts, pieces = refs[:devices], refs[devices : 2 * devices]
-    scaled, jacobi, plain, smooth = refs[2 * devices : 2 * devices + 4]
-    gram, backs = refs[2 * devices + 4], refs[2 * devices + 5 :]
+    scaled, jacobi, others = refs[2 * devices : 2 * devices + 3]
+    gram, backs = refs[2 * devices + 3], refs[2 * devices + 4 :]
     share, width = parts[0].shape[1:3]
-    blocks = jacobi.shape[0]
-    none = devices * share
     sums = {}
-
-    def gather(s, y, weight):
-        y = [weight * value for value in y]
-        f = [s[0] + s[1]]
-        for j in range(1, ITERS):
-            f.append(0.5 * (s[j - 1] + s[j + 1]) + s[j])
-        for i in range(ITERS):
-            for j in range(i + 1):
-                sums[i, j] = sums.get((i, j), 0.0) + y[i] * f[j]
-            sums[i, ITERS] = sums.get((i, ITERS), 0.0) + y[i] * s[0]
-
     for p in range(share):
         block = held[p]
         columns = pl.ds(pl.multiple_of(block * BLOCK, BLOCK), BLOCK)
@@ -333,36 +355,23 @@
         soft = dot3(jnp.concatenate(chosen[:ITERS], 0), jacobi[block])
         weight = jnp.where(used[p] > 0, 1.0, 0.0)
         for r in range(0, BLOCK, 8):
-            gather(
+            gather_sums(
+                sums,
                 [value[r : r + 8] for value in chosen],
                 [soft[k * BLOCK + r : k * BLOCK + r + 8] for k in range(ITERS)],
                 weight,
             )
-    for b in range(blocks):
-        weight = jnp.where(where[b] < none, 0.0, 1.0)
-        for r in range(0, width, 8):
-            gather(
-                [plain[b, k * width + r : k * width + r + 8, :] for k in range(ITERS + 1)],
-                [smooth[b, k * width + r : k * width + r + 8, :] for k in range(ITERS)],
-                weight,
-            )
-    lane = lax.broadcasted_iota(jnp.int32, (1, BLOCK), 1)
-    result = jnp.zeros((1, BLOCK), f32)
-    for (i, j), value in sums.items():
-        value = jnp.sum(jnp.sum(value, axis=0, keepdims=True), axis=1, keepdims=True)
-        here = lane == 16 * i + j
-        if j < ITERS:
-            here = here | (lane == 16 * j + i)
-        result = jnp.where(here, value, result)
-    gram[...] = result
-
-
-def finish_kernel(held, where, grams, scale, gradient, plain, smooth, jacobi, *refs):
-    backs, (solution, residual, extra, less) = refs[:-4], refs[-4:]
-    width = gradient.shape[0]
-    blocks = plain.shape[0]
+    gram[...] = flat_sums(sums) + others[...]
+
+
+def finish_kernel(where, grams, scale, powers, jacobi, *refs):
+    devices = (len(refs) - 4) // 2
+    pieces, backs = refs[:devices], refs[devices : 2 * devices]
+    solution, residual, extra, less = refs[2 * devices :]
+    width = pieces[0].shape[0]
+    blocks = jacobi.shape[0]
     share = backs[0].shape[1]
-    none = len(backs) * share
+    none = devices * share
     flat = jnp.sum(grams[:, 0, :], axis=0, keepdims=True)
     row = lax.broadcasted_iota(jnp.int32, (8, BLOCK), 0)
     lane = lax.broadcasted_iota(jnp.int32, (8, BLOCK), 1)
@@ -386,35 +395,30 @@
         takes.append(jnp.broadcast_to(value, (width, BLOCK)))
     longer = scale[0:1, 0:1]
     gives = [jnp.broadcast_to(longer * step, (width, BLOCK)) for step in steps]
-
-    def combine(weights, ref, b, start):
-        total = None
-        for j, weight in enumerate(weights):
-            term = weight * ref[b, (start + j) * width : (start + j + 1) * width, :]
-            total = term if total is None else total + term
-        return total
-
+    pairs = [
+        sum(
+            weight * powers[k * width : (k + 1) * width, :]
+            for k, weight in enumerate(weights)
+        )
+        for weights in (gives, takes)
+    ]
+    pairs = jnp.concatenate(pairs, 0)
     for n in range(none):
         back = backs[n // share]
-        total, left = 0.0, 0.0
-        for k in range(ITERS):
-            value = back[k, n % share]
-            left = left + takes[k + 1] * value
-            if k + 1 < ITERS:
-                total = total + gives[k + 1] * value
-        less[n] = left
-        extra[n] = dot3(total, jacobi[held[n]])
-    extra[none] = jnp.zeros((width, BLOCK), f32)
-    less[none] = jnp.zeros((width, BLOCK), f32)
+        values = [back[k, n % share] for k in range(ITERS)]
+        extra[n] = sum(weight * value for weight, value in zip(gives[1:], values))
+        less[n] = sum(weight * value for weight, value in zip(takes[1:], values))
     for b in range(blocks):
         columns = slice(b * BLOCK, (b + 1) * BLOCK)
-        n = where[b]
-        own = n >= none
-        rest = jnp.where(own, combine(gives[1:], smooth, b, 1), extra[n])
-        solution[:, columns] = gives[0] * smooth[b, :width, :] + rest
-        rest = jnp.where(own, combine(takes[1:], plain, b, 1), less[n])
-        start = gradient[:, columns]
-        residual[:, columns] = start - takes[0] * start - rest
+        whole = jnp.concatenate([piece[:, columns] for piece in pieces], 0)
+        start = whole[:width]
+        alone = dot(pairs, whole)
+        n = jnp.minimum(where[b], none - 1)
+        own = where[b] >= NOWHERE
+        total = jnp.where(own, alone[:width], gives[0] * start + extra[n])
+        solution[:, columns] = dot3(total, jacobi[b])
+        left = jnp.where(own, alone[width:], takes[0] * start + less[n])
+        residual[:, columns] = start - left
 
 
 def on_device(
@@ -444,9 +448,6 @@
     dealer = (lax.axis_index("cols") + columns - numbers // share) % columns
     order = dealer * share + numbers % share
     if whole:
-        sends, pieces = chain_gathered(
-            gradient, width_factor, jacobi_inverse, coupling_tiles, tile_local, order, *lists
-        )
         local = lists[0]
         earlier = jnp.arange(slots)[:, None] > jnp.arange(slots)[None, :]
         repeat = jnp.any(earlier & (local[:, None] == local[None, :]), axis=1)
@@ -454,20 +455,33 @@
         held = jnp.sum(jnp.where(fit, local[None, :], 0), axis=1)
         used = jnp.sum(jnp.where(fit & (live & ~repeat)[None, :], 1, 0), axis=1)
     else:
+        held = jnp.minimum(order, blocks - 1)
+        used = (order < blocks).astype(jnp.int32)
+    mine = (held[None, :] == jnp.arange(blocks, dtype=jnp.int32)[:, None]) & (used > 0)[None, :]
+    where = jnp.min(jnp.where(mine, numbers[None, :], NOWHERE), axis=1)
+    if whole:
+        sends, pieces, basis = chain_gathered(
+            gradient,
+            width_factor,
+            jacobi_inverse,
+            coupling_tiles,
+            tile_local,
+            order,
+            where,
+            *lists,
+        )
+    else:
         sends = chain_exchanged(
             gradient, jacobi_inverse, coupling_tiles[:slots], order, *lists
         )
         pieces = whole_pieces(gradient, width_factor)
-        held = jnp.minimum(order, blocks - 1)
-        used = (order < blocks).astype(jnp.int32)
-    mine = (held[None, :] == jnp.arange(blocks, dtype=jnp.int32)[:, None]) & (used > 0)[None, :]
-    where = jnp.min(jnp.where(mine, numbers[None, :], columns * share), axis=1)
+        basis = make_basis(pieces, jacobi_inverse, where)
     parts = [sends[0]]
     for o in range(1, columns):
         parts.append(shift(sends[o], "cols", o))
 
     shape = jax.ShapeDtypeStruct
-    scaled, plain, smooth, scale = make_basis(pieces, jacobi_inverse)
+    scaled, powers, others, scale = basis
     gram, *backs = call(
         mix_kernel,
         tuple(
@@ -476,39 +490,30 @@
         ),
         held,
         used,
-        where,
         *parts,
         *pieces,
         scaled,
         jacobi_inverse,
-        plain,
-        smooth,
-        scalars=3,
+        others,
+        scalars=2,
     )
     everyone = columns * devices
-    grams = lax.all_to_all(
-        jnp.broadcast_to(gram[None], (everyone, 1, BLOCK)),
-        ("cols", "rows"),
-        0,
-        0,
-        tiled=True,
-    )
+    grams = jnp.broadcast_to(gram[None], (everyone, 1, BLOCK))
+    grams = lax.all_to_all(grams, ("cols", "rows"), 0, 0, tiled=True)
     for o in range(1, columns):
         backs[o] = shift(backs[o], "cols", -o)
     return call(
         finish_kernel,
         (shape((width, rows), f32), shape((width, rows), f32)),
-        held,
         where,
         grams,
         scale,
-        gradient,
-        plain,
-        smooth,
+        powers,
         jacobi_inverse,
+        *pieces,
         *backs,
-        scalars=2,
-        scratch=[pltpu.VMEM((columns * share + 1, width, BLOCK), f32)] * 2,
+        scalars=1,
+        scratch=[pltpu.VMEM((columns * share, width, BLOCK), f32)] * 2,
     )
 
 

time: 67.3 us -> 68.9 us (1.024)
  waiting for transfers between devices: 14.2 us -> 10.5 us
  starting transfers between devices: 21.4 us -> 24.1 us
  Pallas kernels: 17 us -> 19.1 us
    all_to_all x1, waiting for transfers between devices: 11.9 us -> 0.01 us  [chain_gathered(): told = lax.all_to_all(told, 'rows', 0, 0, tiled=True)]
    ppermute x12, waiting for transfers between devices: 0.6 us -> 8.83 us  [shift(): return lax.ppermute(x, axis, [(i, (i - by) % size) for i in range(size)])]
    ppermute x12, starting transfers between devices: 18.1 us -> 20.7 us  [shift(): return lax.ppermute(x, axis, [(i, (i - by) % size) for i in range(size)])]
    pallas_call x5, Pallas kernels: 17 us -> 19.1 us  [call(): pl.pallas_call(kernel, out_shape=outs, in_specs=specs, out_specs=tuple([V...]
  transfers between devices with their start and end apart: 14 -> 14, of which waited for: 3 -> 5; matrix products, arithmetic and copies ran while one was open for 3% -> 3% of each run, Pallas kernels for 7% -> 8%
where the time goes in v2:
time: 68.9 us; the launch traced here: 68.7 us
  starting transfers between devices  24.1 us (35%)
  Pallas kernels  19.1 us (28%)
  waiting for transfers between devices  10.5 us (15%)
  blocking collectives  10.4 us (15%)
  local copies, waits for them, and re-layouts  1.79 us (3%)
  between operations  1.52 us (2%)
  other arithmetic  1.26 us (2%)
    ppermute x12, starting transfers between devices, shift(): return lax.ppermute(x, axis, [(i, (i - by) % size) for i in range(size)])  20.7 us
    pallas_call x5, Pallas kernels, call(): pl.pallas_call(kernel, out_shape=outs, in_specs=specs, out_specs=tuple([V...  19.1 us
    all_to_all x1, blocking collectives, on_device(): grams = lax.all_to_all(grams, ('cols', 'rows'), 0, 0, tiled=True)  10.4 us
    ppermute x12, waiting for transfers between devices, shift(): return lax.ppermute(x, axis, [(i, (i - by) % size) for i in range(size)])  8.83 us
    all_to_all x1, starting transfers between devices, chain_gathered(): told = lax.all_to_all(told, 'rows', 0, 0, tiled=True)  3.31 us
    ppermute x1, waiting for transfers between devices, chain_gathered(): far = lax.ppermute(near, 'rows', [(i, i ^ 1) for i in range(devices)])  1.64 us
  transfers between devices with their start and end apart: 14, of which 5 were waited for; matrix products, arithmetic and copies ran while one was open for 3% of the time, Pallas kernels for 8%

profile of v2, /device:TPU:0, one launch (start us, length us, event | category | flops | bytes accessed | tf_op | source)
XLA Modules:
  0.0 68.7 jit_solution(12345139008918088654)
XLA Ops:
  0.7 3.0 %shard_map.86 = f32[3,160,128]{2,1,0:T(8,128)} custom-call(s32[4]{0:T(128)} %local.1, f32[32,1024]{1,0:T(8,128)} %gradient.1, f32[8,128,128]{2,1,0:T(8,128)} %jacobi.3, bf16[4,128,128]{2,1,0:T(8,128)(2,1)} %tiles.1), custom_call_target="tpu_custom_call" | custom-call | tf_op jit(solution)/shard_map/pallas_call | solution.py:32
  3.7 3.0 %collective-permute-start.5 = (f32[32,1152]{1,0:T(8,128)S(1)}, f32[32,1152]{1,0:T(8,128)S(1)}, u32[]{:S(2)}, u32[]{:S(2)}) collective-permute-start(f32[32,1152]{1,0:T(8,128)S(1)} %pad_maximum_fusion.1.refs_0_.refs_4_), channel_id=1, source_target_pairs={{0,8},{8,16},{16,24},{24,0},{1,9},{9,17},{17,25},{25,1},{2,10},{10... | collective-permute-start | bytes 442376 | tf_op jit(solution)/shard_map/ppermute | solution.py:119
  6.7 1.5 %collective-permute-start.4 = (f32[32,1152]{1,0:T(8,128)S(1)}, f32[32,1152]{1,0:T(8,128)S(1)}, u32[]{:S(2)}, u32[]{:S(2)}) collective-permute-start(f32[32,1152]{1,0:T(8,128)S(1)} %pad_maximum_fusion.1.refs_0_.refs_4_), channel_id=1, source_target_pairs={{0,16},{8,24},{16,0},{24,8},{1,17},{9,25},{17,1},{25,9},{2,18},{10... | collective-permute-start | bytes 442376 | tf_op jit(solution)/shard_map/ppermute | solution.py:119
  8.2 1.4 %collective-permute-start.3 = (f32[32,1152]{1,0:T(8,128)S(1)}, f32[32,1152]{1,0:T(8,128)S(1)}, u32[]{:S(2)}, u32[]{:S(2)}) collective-permute-start(f32[32,1152]{1,0:T(8,128)S(1)} %pad_maximum_fusion.1.refs_0_.refs_4_), channel_id=1, source_target_pairs={{0,24},{8,0},{16,8},{24,16},{1,25},{9,1},{17,9},{25,17},{2,26},{10... | collective-permute-start | bytes 442376 | tf_op jit(solution)/shard_map/ppermute | solution.py:119
  9.6 1.6 %collective-permute-start.2 = (f32[3,160,128]{2,1,0:T(8,128)S(1)}, f32[3,160,128]{2,1,0:T(8,128)S(1)}, u32[]{:S(2)}, u32[]{:S(2)}) collective-permute-start(f32[3,160,128]{2,1,0:T(8,128)S(1)} %copy-done.1), channel_id=1, source_target_pairs={{0,2},{1,3},{2,4},{3,5},{4,6},{5,7},{6,0},{7,1},{8,10},{9,11},{10,... | collective-permute-start | bytes 737288 | tf_op jit(solution)/shard_map/ppermute | solution.py:119
  11.2 2.6 %collective-permute-start.1 = (f32[3,160,128]{2,1,0:T(8,128)S(1)}, f32[3,160,128]{2,1,0:T(8,128)S(1)}, u32[]{:S(2)}, u32[]{:S(2)}) collective-permute-start(f32[3,160,128]{2,1,0:T(8,128)S(1)} %copy-done.1), channel_id=1, source_target_pairs={{0,4},{1,5},{2,6},{3,7},{4,0},{5,1},{6,2},{7,3},{8,12},{9,13},{10,... | collective-permute-start | bytes 737288 | tf_op jit(solution)/shard_map/ppermute | solution.py:119
  14.5 0.6 copy-done.4
  15.2 0.6 broadcast_in_dim.107
  15.8 3.3 %all-to-all-start = ((s32[8,1,128]{2,1,0:T(1,128)}), s32[8,1,128]{2,1,0:T(1,128)S(1)}, u32[]{:S(2)}, u32[]{:S(2)}) async-start(s32[8,1,128]{2,1,0:T(1,128)} %broadcast_in_dim.107), calls=%async_computation | async-start | bytes 8192 | tf_op jit(solution)/shard_map/all_to_all | solution.py:157
  19.2 0.2 fusion.6
  19.5 0.2 select_reduce_fusion.2
  19.6 3.8 %collective-permute-start = (f32[3,160,128]{2,1,0:T(8,128)S(1)}, f32[3,160,128]{2,1,0:T(8,128)S(1)}, u32[]{:S(2)}, u32[]{:S(2)}) collective-permute-start(f32[3,160,128]{2,1,0:T(8,128)S(1)} %copy-done.1), channel_id=1, source_target_pairs={{0,6},{1,7},{2,0},{3,1},{4,2},{5,3},{6,4},{7,5},{8,14},{9,15},{10,... | collective-permute-start | bytes 737288 | tf_op jit(solution)/shard_map/ppermute | solution.py:119
  23.5 0.1 select_reduce_fusion.1.where
  23.7 5.6 %shard_map.87 = (f32[128,128]{1,0:T(8,128)S(1)}, f32[224,128]{1,0:T(8,128)S(1)}, f32[1,128]{1,0:T(1,128)S(1)}, f32[8,128]{1,0:T(8,128)S(1)}) custom-call(s32[1]{0:T(128)} %bitcast.1.turn, s32[8]{0:T(128)S(1)} %select_reduce_fusion.1.where, f32[32,1152]{1,0:T(8,128)S(1)} %pad_maximum_fusion.1.refs_0_.refs_4_, ...), custom_call_target="tpu_custom_call" | custom-call | tf_op jit(solution)/shard_map/pallas_call | solution.py:32
  29.4 3.8 %collective-permute-done = f32[3,160,128]{2,1,0:T(8,128)S(1)} collective-permute-done((f32[3,160,128]{2,1,0:T(8,128)S(1)}, f32[3,160,128]{2,1,0:T(8,128)S(1)}, u32[]{:S(2)}, u32[]{:S(2)}) %collective-permute-start) | collective-permute-done | bytes 245792 | tf_op jit(solution)/shard_map/ppermute | solution.py:119
  33.8 0.2 select_reduce_fusion
  34.0 0.1 and_select_fusion
  34.1 0.1 select_n.103.sources
  34.2 1.6 %collective-permute-done.6.far = f32[4,3,160,128]{3,2,1,0:T(8,128)S(1)} collective-permute-done((f32[4,3,160,128]{3,2,1,0:T(8,128)S(1)}, f32[4,3,160,128]{3,2,1,0:T(8,128)S(1)}, u32[]{:S(2)}, u32[]{:S(2)}) %collective-permute-start.6) | collective-permute-done | bytes 983072 | tf_op jit(solution)/shard_map/ppermute | solution.py:162
  35.9 4.3 %shard_map.88 = (f32[6,1,32,128]{3,2,1,0:T(8,128)S(1)}, f32[6,1,32,128]{3,2,1,0:T(8,128)S(1)}, f32[6,1,32,128]{3,2,1,0:T(8,128)S(1)}, f32[6,1,32,128]{3,2,1,0:T(8,128)S(1)}) custom-call(s32[72]{0:T(128)S(1)} %select_n.103.sources, s32[4]{0:T(128)S(1)} %compare_select_fusion.give, f32[4,3,160,128]{3,2,1,0:T(8,128)S(1)} %pad_maximum_fusion.near, ...), custom_call_target="tpu_custom_call" | custom-call | tf_op jit(solution)/shard_map/pallas_call | solution.py:32
  40.2 0.6 collective-permute-start.7
  40.7 1.5 %collective-permute-start.8 = (f32[6,1,32,128]{3,2,1,0:T(8,128)S(1)}, f32[6,1,32,128]{3,2,1,0:T(8,128)S(1)}, u32[]{:S(2)}, u32[]{:S(2)}) collective-permute-start(f32[6,1,32,128]{3,2,1,0:T(8,128)S(1)} %get-tuple-element.39), channel_id=1, source_target_pairs={{0,16},{8,24},{16,0},{24,8},{1,17},{9,25},{17,1},{25,9},{2,18},{10... | collective-permute-start | bytes 294920 | tf_op jit(solution)/shard_map/ppermute | solution.py:119
  42.3 0.5 collective-permute-start.9
  42.7 3.0 %collective-permute-done.7.refs_1_ = f32[6,1,32,128]{3,2,1,0:T(8,128)S(1)} collective-permute-done((f32[6,1,32,128]{3,2,1,0:T(8,128)S(1)}, f32[6,1,32,128]{3,2,1,0:T(8,128)S(1)}, u32[]{:S(2)}, u32[]{:S(2)}) %collective-permute-start.7) | collective-permute-done | bytes 98336 | tf_op jit(solution)/shard_map/ppermute | solution.py:119
  45.7 0.8 %collective-permute-done.8.refs_2_ = f32[6,1,32,128]{3,2,1,0:T(8,128)S(1)} collective-permute-done((f32[6,1,32,128]{3,2,1,0:T(8,128)S(1)}, f32[6,1,32,128]{3,2,1,0:T(8,128)S(1)}, u32[]{:S(2)}, u32[]{:S(2)}) %collective-permute-start.8) | collective-permute-done | bytes 98336 | tf_op jit(solution)/shard_map/ppermute | solution.py:119
  46.5 1.2 %collective-permute-done.9.refs_3_ = f32[6,1,32,128]{3,2,1,0:T(8,128)S(1)} collective-permute-done((f32[6,1,32,128]{3,2,1,0:T(8,128)S(1)}, f32[6,1,32,128]{3,2,1,0:T(8,128)S(1)}, u32[]{:S(2)}, u32[]{:S(2)}) %collective-permute-start.9) | collective-permute-done | bytes 98336 | tf_op jit(solution)/shard_map/ppermute | solution.py:119
  47.8 2.4 %shard_map.89 = (f32[1,128]{1,0:T(1,128)S(1)}, f32[6,1,32,128]{3,2,1,0:T(8,128)S(1)}, f32[6,1,32,128]{3,2,1,0:T(8,128)S(1)}, f32[6,1,32,128]{3,2,1,0:T(8,128)S(1)}, f32[6,1,32,128]{3,2,1,0:T(8,128)S(1)}) custom-call(s32[4]{0:T(128)S(1)} %get-tuple-element.51.held, s32[4]{0:T(128)S(1)} %get-tuple-element.50.used, ...), custom_call_target="tpu_custom_call" | custom-call | tf_op jit(solution)/shard_map/pallas_call | solution.py:32
  50.2 0.9 %collective-permute-start.10 = (f32[6,1,32,128]{3,2,1,0:T(8,128)S(1)}, f32[6,1,32,128]{3,2,1,0:T(8,128)S(1)}, u32[]{:S(2)}, u32[]{:S(2)}) collective-permute-start(f32[6,1,32,128]{3,2,1,0:T(8,128)S(1)} %get-tuple-element.47), channel_id=1, source_target_pairs={{0,8},{8,16},{16,24},{24,0},{1,9},{9,17},{17,25},{25,1},{2,10},{10... | collective-permute-start | bytes 294920 | tf_op jit(solution)/shard_map/ppermute | solution.py:119
  51.1 0.6 collective-permute-start.11
  51.7 2.7 %collective-permute-start.12 = (f32[6,1,32,128]{3,2,1,0:T(8,128)S(1)}, f32[6,1,32,128]{3,2,1,0:T(8,128)S(1)}, u32[]{:S(2)}, u32[]{:S(2)}) collective-permute-start(f32[6,1,32,128]{3,2,1,0:T(8,128)S(1)} %get-tuple-element.49), channel_id=1, source_target_pairs={{0,24},{8,0},{16,8},{24,16},{1,25},{9,1},{17,9},{25,17},{2,26},{10... | collective-permute-start | bytes 294920 | tf_op jit(solution)/shard_map/ppermute | solution.py:119
  54.4 10.4 %all_to_all.10.grams = f32[32,1,128]{2,1,0:T(1,128)S(1)} all-to-all(f32[32,1,128]{2,1,0:T(1,128)S(1)} %broadcast_in_dim.116), channel_id=1, replica_groups=mesh['cols'=4,'rows'=8] {'cols','rows'}, dimensions={0} | all-to-all | bytes 32768 | tf_op jit(solution)/shard_map/all_to_all | solution.py:502
  64.8 3.9 %shard_map.90 = (f32[32,1024]{1,0:T(8,128)}, f32[32,1024]{1,0:T(8,128)}) custom-call(s32[8]{0:T(128)S(1)} %select_reduce_fusion.1.where, f32[32,1,128]{2,1,0:T(1,128)S(1)} %all_to_all.10.grams, f32[8,128]{1,0:T(8,128)S(1)} %get-tuple-element.44.scale, f32[224,128]{1,0:T(8,128)S(1)} %get-tuple-element.45.powers, f32[8,128,128]{2,1,0:T(8,128)S(1)} %copy-done, ...), custom_call_target="tpu_custom_call" | custom-call | tf_op jit(solution)/shard_map/pallas_call | solution.py:32
  (41 shorter events, 1.1 us)
Async XLA Ops:
  0.6 23.1 %copy-start = (f32[8,128,128]{2,1,0:T(8,128)S(1)}, f32[8,128,128]{2,1,0:T(8,128)}, u32[]{:S(2)}) copy-start(f32[8,128,128]{2,1,0:T(8,128)} %jacobi.3) | copy-start | bytes 1572868
  0.6 3.0 %copy-start.2 = (f32[32,1024]{1,0:T(8,128)S(1)}, f32[32,1024]{1,0:T(8,128)}, u32[]{:S(2)}) copy-start(f32[32,1024]{1,0:T(8,128)} %gradient.1) | copy-start | bytes 393220
  0.7 3.0 %copy-start.3 = (f32[128,32]{0,1:T(8,128)S(1)}, f32[128,32]{0,1:T(8,128)}, u32[]{:S(2)}) copy-start(f32[128,32]{0,1:T(8,128)} %param.9) | copy-start | bytes 49156
  3.6 6.0 %copy-start.1 = (f32[3,160,128]{2,1,0:T(8,128)S(1)}, f32[3,160,128]{2,1,0:T(8,128)}, u32[]{:S(2)}) copy-start(f32[3,160,128]{2,1,0:T(8,128)} %shard_map.86) | copy-start | bytes 737284
  3.7 16.0 %collective-permute-start.5 = (f32[32,1152]{1,0:T(8,128)S(1)}, f32[32,1152]{1,0:T(8,128)S(1)}, u32[]{:S(2)}, u32[]{:S(2)}) collective-permute-start(f32[32,1152]{1,0:T(8,128)S(1)} %pad_maximum_fusion.1.refs_0_.refs_4_), channel_id=1, source_target_pairs={{0,8},{8,16},{16,24},{24,0},{1,9},{9,17},{17,25},{25,1},{2,10},{10... | collective-permute-start | bytes 442376 | tf_op jit(solution)/shard_map/ppermute | solution.py:119
  6.7 17.0 %collective-permute-start.4 = (f32[32,1152]{1,0:T(8,128)S(1)}, f32[32,1152]{1,0:T(8,128)S(1)}, u32[]{:S(2)}, u32[]{:S(2)}) collective-permute-start(f32[32,1152]{1,0:T(8,128)S(1)} %pad_maximum_fusion.1.refs_0_.refs_4_), channel_id=1, source_target_pairs={{0,16},{8,24},{16,0},{24,8},{1,17},{9,25},{17,1},{25,9},{2,18},{10... | collective-permute-start | bytes 442376 | tf_op jit(solution)/shard_map/ppermute | solution.py:119
  8.2 15.5 %collective-permute-start.3 = (f32[32,1152]{1,0:T(8,128)S(1)}, f32[32,1152]{1,0:T(8,128)S(1)}, u32[]{:S(2)}, u32[]{:S(2)}) collective-permute-start(f32[32,1152]{1,0:T(8,128)S(1)} %pad_maximum_fusion.1.refs_0_.refs_4_), channel_id=1, source_target_pairs={{0,24},{8,0},{16,8},{24,16},{1,25},{9,1},{17,9},{25,17},{2,26},{10... | collective-permute-start | bytes 442376 | tf_op jit(solution)/shard_map/ppermute | solution.py:119
  9.6 19.7 %collective-permute-start.2 = (f32[3,160,128]{2,1,0:T(8,128)S(1)}, f32[3,160,128]{2,1,0:T(8,128)S(1)}, u32[]{:S(2)}, u32[]{:S(2)}) collective-permute-start(f32[3,160,128]{2,1,0:T(8,128)S(1)} %copy-done.1), channel_id=1, source_target_pairs={{0,2},{1,3},{2,4},{3,5},{4,6},{5,7},{6,0},{7,1},{8,10},{9,11},{10,... | collective-permute-start | bytes 737288 | tf_op jit(solution)/shard_map/ppermute | solution.py:119
  11.2 18.2 %collective-permute-start.1 = (f32[3,160,128]{2,1,0:T(8,128)S(1)}, f32[3,160,128]{2,1,0:T(8,128)S(1)}, u32[]{:S(2)}, u32[]{:S(2)}) collective-permute-start(f32[3,160,128]{2,1,0:T(8,128)S(1)} %copy-done.1), channel_id=1, source_target_pairs={{0,4},{1,5},{2,6},{3,7},{4,0},{5,1},{6,2},{7,3},{8,12},{9,13},{10,... | collective-permute-start | bytes 737288 | tf_op jit(solution)/shard_map/ppermute | solution.py:119
  14.5 0.7 copy-start.4
  14.5 0.7 copy-start.5
  15.8 13.5 %all-to-all-start = ((s32[8,1,128]{2,1,0:T(1,128)}), s32[8,1,128]{2,1,0:T(1,128)S(1)}, u32[]{:S(2)}, u32[]{:S(2)}) async-start(s32[8,1,128]{2,1,0:T(1,128)} %broadcast_in_dim.107), calls=%async_computation | async-start | bytes 8192 | tf_op jit(solution)/shard_map/all_to_all | solution.py:157
  19.6 13.5 %collective-permute-start = (f32[3,160,128]{2,1,0:T(8,128)S(1)}, f32[3,160,128]{2,1,0:T(8,128)S(1)}, u32[]{:S(2)}, u32[]{:S(2)}) collective-permute-start(f32[3,160,128]{2,1,0:T(8,128)S(1)} %copy-done.1), channel_id=1, source_target_pairs={{0,6},{1,7},{2,0},{3,1},{4,2},{5,3},{6,4},{7,5},{8,14},{9,15},{10,... | collective-permute-start | bytes 737288 | tf_op jit(solution)/shard_map/ppermute | solution.py:119
  33.3 2.6 %collective-permute-start.6 = (f32[4,3,160,128]{3,2,1,0:T(8,128)S(1)}, f32[4,3,160,128]{3,2,1,0:T(8,128)S(1)}, u32[]{:S(2)}, u32[]{:S(2)}) collective-permute-start(f32[4,3,160,128]{3,2,1,0:T(8,128)S(1)} %pad_maximum_fusion.near), channel_id=1, source_target_pairs={{0,1},{1,0},{2,3},{3,2},{4,5},{5,4},{6,7},{7,6},{8,9},{9,8},{10,11... | collective-permute-start | bytes 2949128 | tf_op jit(solution)/shard_map/ppermute | solution.py:162
  40.2 5.6 %collective-permute-start.7 = (f32[6,1,32,128]{3,2,1,0:T(8,128)S(1)}, f32[6,1,32,128]{3,2,1,0:T(8,128)S(1)}, u32[]{:S(2)}, u32[]{:S(2)}) collective-permute-start(f32[6,1,32,128]{3,2,1,0:T(8,128)S(1)} %get-tuple-element.38), channel_id=1, source_target_pairs={{0,24},{8,0},{16,8},{24,16},{1,25},{9,1},{17,9},{25,17},{2,26},{10... | collective-permute-start | bytes 294920 | tf_op jit(solution)/shard_map/ppermute | solution.py:119
  40.7 5.8 %collective-permute-start.8 = (f32[6,1,32,128]{3,2,1,0:T(8,128)S(1)}, f32[6,1,32,128]{3,2,1,0:T(8,128)S(1)}, u32[]{:S(2)}, u32[]{:S(2)}) collective-permute-start(f32[6,1,32,128]{3,2,1,0:T(8,128)S(1)} %get-tuple-element.39), channel_id=1, source_target_pairs={{0,16},{8,24},{16,0},{24,8},{1,17},{9,25},{17,1},{25,9},{2,18},{10... | collective-permute-start | bytes 294920 | tf_op jit(solution)/shard_map/ppermute | solution.py:119
  42.3 5.5 %collective-permute-start.9 = (f32[6,1,32,128]{3,2,1,0:T(8,128)S(1)}, f32[6,1,32,128]{3,2,1,0:T(8,128)S(1)}, u32[]{:S(2)}, u32[]{:S(2)}) collective-permute-start(f32[6,1,32,128]{3,2,1,0:T(8,128)S(1)} %get-tuple-element.40), channel_id=1, source_target_pairs={{0,8},{8,16},{16,24},{24,0},{1,9},{9,17},{17,25},{25,1},{2,10},{10... | collective-permute-start | bytes 294920 | tf_op jit(solution)/shard_map/ppermute | solution.py:119
  50.2 14.6 %collective-permute-start.10 = (f32[6,1,32,128]{3,2,1,0:T(8,128)S(1)}, f32[6,1,32,128]{3,2,1,0:T(8,128)S(1)}, u32[]{:S(2)}, u32[]{:S(2)}) collective-permute-start(f32[6,1,32,128]{3,2,1,0:T(8,128)S(1)} %get-tuple-element.47), channel_id=1, source_target_pairs={{0,8},{8,16},{16,24},{24,0},{1,9},{9,17},{17,25},{25,1},{2,10},{10... | collective-permute-start | bytes 294920 | tf_op jit(solution)/shard_map/ppermute | solution.py:119
  51.1 13.7 %collective-permute-start.11 = (f32[6,1,32,128]{3,2,1,0:T(8,128)S(1)}, f32[6,1,32,128]{3,2,1,0:T(8,128)S(1)}, u32[]{:S(2)}, u32[]{:S(2)}) collective-permute-start(f32[6,1,32,128]{3,2,1,0:T(8,128)S(1)} %get-tuple-element.48), channel_id=1, source_target_pairs={{0,16},{8,24},{16,0},{24,8},{1,17},{9,25},{17,1},{25,9},{2,18},{10... | collective-permute-start | bytes 294920 | tf_op jit(solution)/shard_map/ppermute | solution.py:119
  51.7 13.1 %collective-permute-start.12 = (f32[6,1,32,128]{3,2,1,0:T(8,128)S(1)}, f32[6,1,32,128]{3,2,1,0:T(8,128)S(1)}, u32[]{:S(2)}, u32[]{:S(2)}) collective-permute-start(f32[6,1,32,128]{3,2,1,0:T(8,128)S(1)} %get-tuple-element.49), channel_id=1, source_target_pairs={{0,24},{8,0},{16,8},{24,16},{1,25},{9,1},{17,9},{25,17},{2,26},{10... | collective-permute-start | bytes 294920 | tf_op jit(solution)/shard_map/ppermute | solution.py:119

commit v3 on v2

--- a/solution.py
+++ b/solution.py
@@ -56,29 +56,27 @@
     return both[:tall] + (both[tall:] + plain_dot(high, rest))
 
 
-def pack_kernel(local, gradient, jacobi, tiles, packed, inverse, coupling, part, done):
+def pack_kernel(
+    local, gradient, jacobi, tiles, packed, blocks, whole, inverse, coupling, done
+):
     slots = packed.shape[0]
     contract = (((1,), (1,)), ((), ()))
-    copies = []
+    moves = [(local, blocks), (jacobi, inverse), (tiles, coupling), (gradient, whole)]
+    copies = [
+        pltpu.make_async_copy(source, target, done.at[i])
+        for i, (source, target) in enumerate(moves)
+    ]
+    for copy in copies:
+        copy.start()
+    for copy in copies:
+        copy.wait()
     for slot in range(slots):
-        block = local[slot]
-        columns = pl.ds(pl.multiple_of(block * BLOCK, BLOCK), BLOCK)
-        moves = [
-            (jacobi.at[block], inverse.at[slot]),
-            (tiles.at[slot], coupling.at[slot]),
-            (gradient.at[:, columns], part.at[slot]),
-        ]
-        for i, (source, target) in enumerate(moves):
-            copy = pltpu.make_async_copy(source, target, done.at[slot, i])
-            copy.start()
-            copies.append(copy)
-    for slot in range(slots):
-        for copy in copies[3 * slot : 3 * slot + 3]:
-            copy.wait()
-        halves = jnp.concatenate(split(inverse[slot]), 0)
+        block = blocks[slot]
+        halves = jnp.concatenate(split(inverse[block]), 0)
         both = lax.dot_general(halves, coupling[slot], contract, preferred_element_type=f32)
         packed[slot, :BLOCK, :] = both[:BLOCK] + both[BLOCK:]
-        packed[slot, BLOCK:, :] = part[slot]
+        columns = pl.ds(pl.multiple_of(block * BLOCK, BLOCK), BLOCK)
+        packed[slot, BLOCK:, :] = whole[:, columns]
 
 
 def chain_kernel(sources, give, near, far, *refs):
@@ -125,7 +123,7 @@
     return [piece] + [shift(piece, "cols", o) for o in others]
 
 
-def chain_gathered(gradient, factor, jacobi, tiles, whole_local, order, where, local, remote, live):
+def chain_gathered(gradient, factor, jacobi, tiles, whole_local, order, local, remote, live):
     width = gradient.shape[0]
     blocks, slots = jacobi.shape[0], local.shape[0]
     devices = lax.axis_size("rows")
@@ -138,12 +136,12 @@
         gradient,
         jacobi,
         tiles,
-        scalars=1,
         scratch=[
-            pltpu.VMEM((slots, BLOCK, BLOCK), f32),
-            pltpu.VMEM((slots, BLOCK, BLOCK), tiles.dtype),
-            pltpu.VMEM((slots, width, BLOCK), f32),
-            pltpu.SemaphoreType.DMA((slots, 3)),
+            pltpu.SMEM(whole_local.shape, jnp.int32),
+            pltpu.VMEM(gradient.shape, f32),
+            pltpu.VMEM(jacobi.shape, f32),
+            pltpu.VMEM(tiles.shape, tiles.dtype),
+            pltpu.SemaphoreType.DMA((4,)),
         ],
         place=pl.BlockSpec(memory_space=pl.ANY),
         grant=WHOLE_BYTES,
@@ -156,8 +154,8 @@
     told = jnp.broadcast_to(own[None, None, :], (devices, 1, BLOCK))
     told = lax.all_to_all(told, "rows", 0, 0, tiled=True)
     told = told[:, 0]
-    basis = make_basis(pieces, jacobi, where)
-    near, basis, told = lax.optimization_barrier((near, basis, told))
+    powers = make_powers(pieces)
+    near, pieces, powers, told = lax.optimization_barrier((near, pieces, powers, told))
     near = jnp.stack(near)
     far = lax.ppermute(near, "rows", [(i, i ^ 1) for i in range(devices)])
 
@@ -204,7 +202,7 @@
             pltpu.VMEM((total + 1, width, BLOCK), f32),
         ],
     )
-    return list(sends), pieces, basis
+    return list(sends), pieces, powers
 
 
 def chain_exchanged(gradient, jacobi, tiles, order, local, remote, live):
@@ -258,14 +256,10 @@
     return result
 
 
-def basis_kernel(turn, where, *refs):
-    devices = len(refs) - 5
-    pieces, jacobi = refs[:devices], refs[devices]
-    scaled, powers, gram, scale = refs[devices + 1 :]
+def powers_kernel(turn, *refs):
+    pieces, (scaled, powers, scale) = refs[:-3], refs[-3:]
     width = pieces[0].shape[0]
-    blocks = jacobi.shape[0]
-    rows = blocks * BLOCK
-    factor = jnp.concatenate([piece[:, rows:] for piece in pieces], 0)
+    factor = jnp.concatenate([piece[:, -BLOCK:] for piece in pieces], 0)
     factor = pltpu.roll(factor, turn[0], 1)
     norm = jnp.max(jnp.sum(jnp.abs(factor), axis=1, keepdims=True), axis=0, keepdims=True)
     power = factor / norm
@@ -285,55 +279,60 @@
     for k in range(ITERS):
         value = dot(kept[k], factor) - kept[k]
         kept.append(2.0 * value - kept[k - 1] if k else value)
-    first = jnp.concatenate(kept, 0)
-    powers[...] = first
+    powers[...] = jnp.concatenate(kept, 0)
+
+
+def basis_kernel(where, held, powers, jacobi, *refs):
+    pieces, (plain, smooth, gram, starts) = refs[:-4], refs[-4:]
+    width = pieces[0].shape[0]
+    for p in range(starts.shape[0]):
+        columns = pl.ds(pl.multiple_of(held[p] * BLOCK, BLOCK), BLOCK)
+        starts[p] = jnp.concatenate([piece[:, columns] for piece in pieces], 0)
     sums = {}
-    for b in range(blocks):
+    for b in range(jacobi.shape[0]):
         columns = slice(b * BLOCK, (b + 1) * BLOCK)
-        plain = dot(first, jnp.concatenate([piece[:, columns] for piece in pieces], 0))
-        smooth = dot(plain[: ITERS * width], jacobi[b])
+        whole = jnp.concatenate([piece[:, columns] for piece in pieces], 0)
+        s = dot(powers[...], whole)
+        y = dot(s[: ITERS * width], jacobi[b])
+        plain[b] = s[width:]
+        smooth[b] = y
         weight = jnp.where(where[b] < NOWHERE, 0.0, 1.0)
         for r in range(0, width, 8):
             gather_sums(
                 sums,
-                [plain[k * width + r : k * width + r + 8] for k in range(ITERS + 1)],
-                [smooth[k * width + r : k * width + r + 8] for k in range(ITERS)],
+                [s[k * width + r : k * width + r + 8] for k in range(ITERS + 1)],
+                [y[k * width + r : k * width + r + 8] for k in range(ITERS)],
                 weight,
             )
     gram[...] = flat_sums(sums)
 
 
-def make_basis(pieces, jacobi, where):
+def make_powers(pieces):
     width = pieces[0].shape[0]
     shape = jax.ShapeDtypeStruct
     turn = (BLOCK - width * lax.axis_index("cols")) % BLOCK
     return call(
-        basis_kernel,
+        powers_kernel,
         (
             shape((BLOCK, BLOCK), f32),
             shape(((ITERS + 1) * width, BLOCK), f32),
-            shape((1, BLOCK), f32),
             shape((8, BLOCK), f32),
         ),
         turn.astype(jnp.int32).reshape(1),
-        where,
         *pieces,
-        jacobi,
-        scalars=2,
+        scalars=1,
     )
 
 
 def mix_kernel(held, used, *refs):
-    devices = (len(refs) - 4) // 3
-    parts, pieces = refs[:devices], refs[devices : 2 * devices]
-    scaled, jacobi, others = refs[2 * devices : 2 * devices + 3]
-    gram, backs = refs[2 * devices + 3], refs[2 * devices + 4 :]
+    devices = (len(refs) - 5) // 2
+    parts = refs[:devices]
+    starts, scaled, jacobi, others, gram = refs[devices : devices + 5]
+    backs = refs[devices + 5 :]
     share, width = parts[0].shape[1:3]
     sums = {}
     for p in range(share):
-        block = held[p]
-        columns = pl.ds(pl.multiple_of(block * BLOCK, BLOCK), BLOCK)
-        now = [jnp.concatenate([piece[:, columns] for piece in pieces], 0)]
+        now = [starts[p]]
         for j in range(ITERS):
             now.append(jnp.concatenate([part[j, p] for part in parts], 0))
         past = None
@@ -352,7 +351,7 @@
         for o, back in enumerate(backs):
             for k in range(ITERS):
                 back[k, p] = chosen[k + 1][o * width : (o + 1) * width]
-        soft = dot3(jnp.concatenate(chosen[:ITERS], 0), jacobi[block])
+        soft = dot3(jnp.concatenate(chosen[:ITERS], 0), jacobi[held[p]])
         weight = jnp.where(used[p] > 0, 1.0, 0.0)
         for r in range(0, BLOCK, 8):
             gather_sums(
@@ -361,17 +360,15 @@
                 [soft[k * BLOCK + r : k * BLOCK + r + 8] for k in range(ITERS)],
                 weight,
             )
-    gram[...] = flat_sums(sums) + others[...]
-
-
-def finish_kernel(where, grams, scale, powers, jacobi, *refs):
-    devices = (len(refs) - 4) // 2
-    pieces, backs = refs[:devices], refs[devices : 2 * devices]
-    solution, residual, extra, less = refs[2 * devices :]
-    width = pieces[0].shape[0]
+    gram[...] = jnp.broadcast_to((flat_sums(sums) + others[...])[None], gram.shape)
+
+
+def finish_kernel(held, where, grams, scale, gradient, plain, smooth, jacobi, *refs):
+    backs, (solution, residual, extra, less) = refs[:-4], refs[-4:]
+    width = gradient.shape[0]
     blocks = jacobi.shape[0]
     share = backs[0].shape[1]
-    none = devices * share
+    none = len(backs) * share
     flat = jnp.sum(grams[:, 0, :], axis=0, keepdims=True)
     row = lax.broadcasted_iota(jnp.int32, (8, BLOCK), 0)
     lane = lax.broadcasted_iota(jnp.int32, (8, BLOCK), 1)
@@ -395,30 +392,27 @@
         takes.append(jnp.broadcast_to(value, (width, BLOCK)))
     longer = scale[0:1, 0:1]
     gives = [jnp.broadcast_to(longer * step, (width, BLOCK)) for step in steps]
-    pairs = [
-        sum(
-            weight * powers[k * width : (k + 1) * width, :]
-            for k, weight in enumerate(weights)
-        )
-        for weights in (gives, takes)
-    ]
-    pairs = jnp.concatenate(pairs, 0)
+
+    def combine(weights, values):
+        return sum(weight * value for weight, value in zip(weights, values))
+
+    def cut(ref, b):
+        return [ref[b, k * width : (k + 1) * width, :] for k in range(ITERS)]
+
     for n in range(none):
-        back = backs[n // share]
-        values = [back[k, n % share] for k in range(ITERS)]
-        extra[n] = sum(weight * value for weight, value in zip(gives[1:], values))
-        less[n] = sum(weight * value for weight, value in zip(takes[1:], values))
+        values = [backs[n // share][k, n % share] for k in range(ITERS)]
+        extra[n] = dot3(combine(gives[1:], values), jacobi[held[n]])
+        less[n] = combine(takes[1:], values)
     for b in range(blocks):
         columns = slice(b * BLOCK, (b + 1) * BLOCK)
-        whole = jnp.concatenate([piece[:, columns] for piece in pieces], 0)
-        start = whole[:width]
-        alone = dot(pairs, whole)
         n = jnp.minimum(where[b], none - 1)
         own = where[b] >= NOWHERE
-        total = jnp.where(own, alone[:width], gives[0] * start + extra[n])
-        solution[:, columns] = dot3(total, jacobi[b])
-        left = jnp.where(own, alone[width:], takes[0] * start + less[n])
-        residual[:, columns] = start - left
+        y = cut(smooth, b)
+        rest = jnp.where(own, combine(gives[1:], y[1:]), extra[n])
+        solution[:, columns] = gives[0] * y[0] + rest
+        rest = jnp.where(own, combine(takes[1:], cut(plain, b)), less[n])
+        start = gradient[:, columns]
+        residual[:, columns] = start - takes[0] * start - rest
 
 
 def on_device(
@@ -460,14 +454,13 @@
     mine = (held[None, :] == jnp.arange(blocks, dtype=jnp.int32)[:, None]) & (used > 0)[None, :]
     where = jnp.min(jnp.where(mine, numbers[None, :], NOWHERE), axis=1)
     if whole:
-        sends, pieces, basis = chain_gathered(
+        sends, pieces, powers = chain_gathered(
             gradient,
             width_factor,
             jacobi_inverse,
             coupling_tiles,
             tile_local,
             order,
-            where,
             *lists,
         )
     else:
@@ -475,44 +468,60 @@
             gradient, jacobi_inverse, coupling_tiles[:slots], order, *lists
         )
         pieces = whole_pieces(gradient, width_factor)
-        basis = make_basis(pieces, jacobi_inverse, where)
+        powers = make_powers(pieces)
+    scaled, powers, scale = powers
+    powers, sends = lax.optimization_barrier((powers, sends))
     parts = [sends[0]]
     for o in range(1, columns):
         parts.append(shift(sends[o], "cols", o))
 
     shape = jax.ShapeDtypeStruct
-    scaled, powers, others, scale = basis
+    plain, smooth, others, starts = call(
+        basis_kernel,
+        (
+            shape((blocks, ITERS * width, BLOCK), f32),
+            shape((blocks, ITERS * width, BLOCK), f32),
+            shape((1, BLOCK), f32),
+            shape((share, BLOCK, BLOCK), f32),
+        ),
+        where,
+        held,
+        powers,
+        jacobi_inverse,
+        *pieces,
+        scalars=2,
+    )
     gram, *backs = call(
         mix_kernel,
         tuple(
-            [shape((1, BLOCK), f32)]
+            [shape((columns * devices, 1, BLOCK), f32)]
             + [shape((ITERS, share, width, BLOCK), f32)] * columns
         ),
         held,
         used,
         *parts,
-        *pieces,
+        starts,
         scaled,
         jacobi_inverse,
         others,
         scalars=2,
     )
-    everyone = columns * devices
-    grams = jnp.broadcast_to(gram[None], (everyone, 1, BLOCK))
-    grams = lax.all_to_all(grams, ("cols", "rows"), 0, 0, tiled=True)
+    grams = lax.all_to_all(gram, ("cols", "rows"), 0, 0, tiled=True)
     for o in range(1, columns):
         backs[o] = shift(backs[o], "cols", -o)
     return call(
         finish_kernel,
         (shape((width, rows), f32), shape((width, rows), f32)),
+        held,
         where,
         grams,
         scale,
-        powers,
+        gradient,
+        plain,
+        smooth,
         jacobi_inverse,
-        *pieces,
         *backs,
-        scalars=1,
+        scalars=2,
         scratch=[pltpu.VMEM((columns * share, width, BLOCK), f32)] * 2,
     )
 

time: 68.9 us -> 66.5 us (0.965)
  starting transfers between devices: 24.1 us -> 21.4 us
  Pallas kernels: 19.1 us -> 17.2 us
  blocking collectives: 10.4 us -> 11.5 us
  waiting for transfers between devices: 10.5 us -> 11.6 us
    all_to_all x1, waiting for transfers between devices: 0.01 us -> 3.52 us  [chain_gathered(): told = lax.all_to_all(told, 'rows', 0, 0, tiled=True)]
    ppermute x12, starting transfers between devices: 20.7 us -> 17.2 us  [shift(): return lax.ppermute(x, axis, [(i, (i - by) % size) for i in range(size)])]
    ppermute x12, waiting for transfers between devices: 8.83 us -> 6.46 us  [shift(): return lax.ppermute(x, axis, [(i, (i - by) % size) for i in range(size)])]
    pallas_call x5 -> x6, Pallas kernels: 19.1 us -> 17.2 us  [call(): pl.pallas_call(kernel, out_shape=outs, in_specs=specs, out_specs=tuple([V...]
    all_to_all x1, blocking collectives: 10.4 us -> 11.5 us  [on_device(): grams = lax.all_to_all(gram, ('cols', 'rows'), 0, 0, tiled=True)]
    all_to_all x1, starting transfers between devices: 3.31 us -> 4.09 us  [chain_gathered(): told = lax.all_to_all(told, 'rows', 0, 0, tiled=True)]
  transfers between devices with their start and end apart: 14 -> 14, of which waited for: 5 -> 3; matrix products, arithmetic and copies ran while one was open for 3% -> 3% of each run, Pallas kernels for 8% -> 10%
where the time goes in v3:
time: 66.5 us; the launch traced here: 66.3 us
  starting transfers between devices  21.4 us (32%)
  Pallas kernels  17.2 us (26%)
  waiting for transfers between devices  11.6 us (17%)
  blocking collectives  11.5 us (17%)
  local copies, waits for them, and re-layouts  1.78 us (3%)
  between operations  1.48 us (2%)
  other arithmetic  1.26 us (2%)
    pallas_call x6, Pallas kernels, call(): pl.pallas_call(kernel, out_shape=outs, in_specs=specs, out_specs=tuple([V...  17.2 us
    ppermute x12, starting transfers between devices, shift(): return lax.ppermute(x, axis, [(i, (i - by) % size) for i in range(size)])  17.2 us
    all_to_all x1, blocking collectives, on_device(): grams = lax.all_to_all(gram, ('cols', 'rows'), 0, 0, tiled=True)  11.5 us
    ppermute x12, waiting for transfers between devices, shift(): return lax.ppermute(x, axis, [(i, (i - by) % size) for i in range(size)])  6.46 us
    all_to_all x1, starting transfers between devices, chain_gathered(): told = lax.all_to_all(told, 'rows', 0, 0, tiled=True)  4.09 us
    all_to_all x1, waiting for transfers between devices, chain_gathered(): told = lax.all_to_all(told, 'rows', 0, 0, tiled=True)  3.52 us
    ppermute x1, waiting for transfers between devices, chain_gathered(): far = lax.ppermute(near, 'rows', [(i, i ^ 1) for i in range(devices)])  1.63 us
  transfers between devices with their start and end apart: 14, of which 3 were waited for; matrix products, arithmetic and copies ran while one was open for 3% of the time, Pallas kernels for 10%

profile of v3, /device:TPU:0, one launch (start us, length us, event | category | flops | bytes accessed | tf_op | source)
XLA Modules:
  0.0 66.3 jit_solution(10227085139882846220)
XLA Ops:
  0.7 2.1 %shard_map.86 = f32[3,160,128]{2,1,0:T(8,128)} custom-call(s32[4]{0:T(128)} %local.1, f32[32,1024]{1,0:T(8,128)} %gradient.3, f32[8,128,128]{2,1,0:T(8,128)} %jacobi.5, bf16[4,128,128]{2,1,0:T(8,128)(2,1)} %tiles.1), custom_call_target="tpu_custom_call" | custom-call | tf_op jit(solution)/shard_map/pallas_call | solution.py:32
  2.8 4.0 %collective-permute-start.3 = (f32[32,1152]{1,0:T(8,128)S(1)}, f32[32,1152]{1,0:T(8,128)S(1)}, u32[]{:S(2)}, u32[]{:S(2)}) collective-permute-start(f32[32,1152]{1,0:T(8,128)S(1)} %pad_maximum_fusion.1.refs_0_), channel_id=1, source_target_pairs={{0,24},{8,0},{16,8},{24,16},{1,25},{9,1},{17,9},{25,17},{2,26},{10... | collective-permute-start | bytes 442376 | tf_op jit(solution)/shard_map/ppermute | solution.py:117
  6.8 0.5 collective-permute-start.4
  7.3 3.6 %collective-permute-start = (f32[3,160,128]{2,1,0:T(8,128)S(1)}, f32[3,160,128]{2,1,0:T(8,128)S(1)}, u32[]{:S(2)}, u32[]{:S(2)}) collective-permute-start(f32[3,160,128]{2,1,0:T(8,128)S(1)} %copy-done.2), channel_id=1, source_target_pairs={{0,6},{1,7},{2,0},{3,1},{4,2},{5,3},{6,4},{7,5},{8,14},{9,15},{10,... | collective-permute-start | bytes 737288 | tf_op jit(solution)/shard_map/ppermute | solution.py:117
  10.9 1.0 %collective-permute-start.2 = (f32[3,160,128]{2,1,0:T(8,128)S(1)}, f32[3,160,128]{2,1,0:T(8,128)S(1)}, u32[]{:S(2)}, u32[]{:S(2)}) collective-permute-start(f32[3,160,128]{2,1,0:T(8,128)S(1)} %copy-done.2), channel_id=1, source_target_pairs={{0,2},{1,3},{2,4},{3,5},{4,6},{5,7},{6,0},{7,1},{8,10},{9,11},{10,... | collective-permute-start | bytes 737288 | tf_op jit(solution)/shard_map/ppermute | solution.py:117
  12.6 0.6 copy-done.4
  13.3 0.6 broadcast_in_dim.99
  13.9 4.1 %all-to-all-start = ((s32[8,1,128]{2,1,0:T(1,128)}), s32[8,1,128]{2,1,0:T(1,128)S(1)}, u32[]{:S(2)}, u32[]{:S(2)}) async-start(s32[8,1,128]{2,1,0:T(1,128)} %broadcast_in_dim.99), calls=%async_computation | async-start | bytes 8192 | tf_op jit(solution)/shard_map/all_to_all | solution.py:155
  18.0 0.2 fusion.6
  18.3 0.2 select_reduce_fusion.2
  18.5 0.6 collective-permute-start.5
  19.3 6.4 %collective-permute-done.5.refs_3_ = f32[32,1152]{1,0:T(8,128)S(1)} collective-permute-done((f32[32,1152]{1,0:T(8,128)S(1)}, f32[32,1152]{1,0:T(8,128)S(1)}, u32[]{:S(2)}, u32[]{:S(2)}) %collective-permute-start.5) | collective-permute-done | bytes 147488 | tf_op jit(solution)/shard_map/ppermute | solution.py:117
  25.7 2.2 %shard_map.87 = (f32[128,128]{1,0:T(8,128)S(1)}, f32[224,128]{1,0:T(8,128)S(1)}, f32[8,128]{1,0:T(8,128)S(1)}) custom-call(s32[1]{0:T(128)} %bitcast.2.turn, f32[32,1152]{1,0:T(8,128)S(1)} %pad_maximum_fusion.1.refs_0_, f32[32,1152]{1,0:T(8,128)S(1)} %collective-permute-done.3.refs_1_, f32[32,1152]{1,0:T(8,128)S(1)} %collective-permute-done.4.refs_2_, ...), custom_call_target="tpu_custom_call" | custom-call | tf_op jit(solution)/shard_map/pallas_call | solution.py:32
  27.9 3.5 %all-to-all-done = s32[8,1,128]{2,1,0:T(1,128)S(1)} async-done(((s32[8,1,128]{2,1,0:T(1,128)}), s32[8,1,128]{2,1,0:T(1,128)S(1)}, u32[]{:S(2)}, u32[]{:S(2)}) %all-to-all-start) | async-done | bytes 4128 | tf_op jit(solution)/shard_map/all_to_all | solution.py:155
  31.6 0.1 multiply_reduce_fusion
  31.9 0.1 gt.39
  32.0 0.2 select_reduce_fusion
  32.3 0.1 and_select_fusion
  32.4 0.1 select_n.103.sources
  32.5 1.6 %collective-permute-done.6.far = f32[4,3,160,128]{3,2,1,0:T(8,128)S(1)} collective-permute-done((f32[4,3,160,128]{3,2,1,0:T(8,128)S(1)}, f32[4,3,160,128]{3,2,1,0:T(8,128)S(1)}, u32[]{:S(2)}, u32[]{:S(2)}) %collective-permute-start.6) | collective-permute-done | bytes 983072 | tf_op jit(solution)/shard_map/ppermute | solution.py:160
  34.1 4.3 %shard_map.88 = (f32[6,1,32,128]{3,2,1,0:T(8,128)S(1)}, f32[6,1,32,128]{3,2,1,0:T(8,128)S(1)}, f32[6,1,32,128]{3,2,1,0:T(8,128)S(1)}, f32[6,1,32,128]{3,2,1,0:T(8,128)S(1)}) custom-call(s32[72]{0:T(128)S(1)} %select_n.103.sources, s32[4]{0:T(128)S(1)} %compare_select_fusion.give, f32[4,3,160,128]{3,2,1,0:T(8,128)S(1)} %pad_maximum_fusion.near, ...), custom_call_target="tpu_custom_call" | custom-call | tf_op jit(solution)/shard_map/pallas_call | solution.py:32
  38.4 0.9 %collective-permute-start.7 = (f32[6,1,32,128]{3,2,1,0:T(8,128)S(1)}, f32[6,1,32,128]{3,2,1,0:T(8,128)S(1)}, u32[]{:S(2)}, u32[]{:S(2)}) collective-permute-start(f32[6,1,32,128]{3,2,1,0:T(8,128)S(1)} %get-tuple-element.53), channel_id=1, source_target_pairs={{0,24},{8,0},{16,8},{24,16},{1,25},{9,1},{17,9},{25,17},{2,26},{10... | collective-permute-start | bytes 294920 | tf_op jit(solution)/shard_map/ppermute | solution.py:117
  39.3 1.2 %collective-permute-start.8 = (f32[6,1,32,128]{3,2,1,0:T(8,128)S(1)}, f32[6,1,32,128]{3,2,1,0:T(8,128)S(1)}, u32[]{:S(2)}, u32[]{:S(2)}) collective-permute-start(f32[6,1,32,128]{3,2,1,0:T(8,128)S(1)} %get-tuple-element.54), channel_id=1, source_target_pairs={{0,16},{8,24},{16,0},{24,8},{1,17},{9,25},{17,1},{25,9},{2,18},{10... | collective-permute-start | bytes 294920 | tf_op jit(solution)/shard_map/ppermute | solution.py:117
  40.5 1.5 %collective-permute-start.9 = (f32[6,1,32,128]{3,2,1,0:T(8,128)S(1)}, f32[6,1,32,128]{3,2,1,0:T(8,128)S(1)}, u32[]{:S(2)}, u32[]{:S(2)}) collective-permute-start(f32[6,1,32,128]{3,2,1,0:T(8,128)S(1)} %get-tuple-element.55), channel_id=1, source_target_pairs={{0,8},{8,16},{16,24},{24,0},{1,9},{9,17},{17,25},{25,1},{2,10},{10... | collective-permute-start | bytes 294920 | tf_op jit(solution)/shard_map/ppermute | solution.py:117
  42.0 0.1 select_reduce_fusion.1.where
  42.1 4.2 %shard_map.89 = (f32[8,192,128]{2,1,0:T(8,128)S(1)}, f32[8,192,128]{2,1,0:T(8,128)S(1)}, f32[1,128]{1,0:T(1,128)S(1)}, f32[1,128,128]{2,1,0:T(8,128)S(1)}) custom-call(s32[8]{0:T(128)S(1)} %select_reduce_fusion.1.where, s32[4]{0:T(128)S(1)} %get-tuple-element.73.held, f32[224,128]{1,0:T(8,128)S(1)} %get-tuple-element.56.powers, f32[8,128,128]{2,1,0:T(8,128)S(1)} %copy-done, ...), custom_call_target="tpu_custom_call" | custom-call | tf_op jit(solution)/shard_map/pallas_call | solution.py:32
  46.3 2.4 %shard_map.90 = (f32[32,1,128]{2,1,0:T(1,128)S(1)}, f32[6,1,32,128]{3,2,1,0:T(8,128)S(1)}, f32[6,1,32,128]{3,2,1,0:T(8,128)S(1)}, f32[6,1,32,128]{3,2,1,0:T(8,128)S(1)}, f32[6,1,32,128]{3,2,1,0:T(8,128)S(1)}) custom-call(s32[4]{0:T(128)S(1)} %get-tuple-element.73.held, s32[4]{0:T(128)S(1)} %get-tuple-element.72.used, ...), custom_call_target="tpu_custom_call" | custom-call | tf_op jit(solution)/shard_map/pallas_call | solution.py:32
  48.8 0.9 %collective-permute-start.10 = (f32[6,1,32,128]{3,2,1,0:T(8,128)S(1)}, f32[6,1,32,128]{3,2,1,0:T(8,128)S(1)}, u32[]{:S(2)}, u32[]{:S(2)}) collective-permute-start(f32[6,1,32,128]{3,2,1,0:T(8,128)S(1)} %get-tuple-element.69), channel_id=1, source_target_pairs={{0,8},{8,16},{16,24},{24,0},{1,9},{9,17},{17,25},{25,1},{2,10},{10... | collective-permute-start | bytes 294920 | tf_op jit(solution)/shard_map/ppermute | solution.py:117
  49.6 1.2 %collective-permute-start.11 = (f32[6,1,32,128]{3,2,1,0:T(8,128)S(1)}, f32[6,1,32,128]{3,2,1,0:T(8,128)S(1)}, u32[]{:S(2)}, u32[]{:S(2)}) collective-permute-start(f32[6,1,32,128]{3,2,1,0:T(8,128)S(1)} %get-tuple-element.70), channel_id=1, source_target_pairs={{0,16},{8,24},{16,0},{24,8},{1,17},{9,25},{17,1},{25,9},{2,18},{10... | collective-permute-start | bytes 294920 | tf_op jit(solution)/shard_map/ppermute | solution.py:117
  50.8 1.8 %collective-permute-start.12 = (f32[6,1,32,128]{3,2,1,0:T(8,128)S(1)}, f32[6,1,32,128]{3,2,1,0:T(8,128)S(1)}, u32[]{:S(2)}, u32[]{:S(2)}) collective-permute-start(f32[6,1,32,128]{3,2,1,0:T(8,128)S(1)} %get-tuple-element.71), channel_id=1, source_target_pairs={{0,24},{8,0},{16,8},{24,16},{1,25},{9,1},{17,9},{25,17},{2,26},{10... | collective-permute-start | bytes 294920 | tf_op jit(solution)/shard_map/ppermute | solution.py:117
  52.6 11.5 %all_to_all.10.grams = f32[32,1,128]{2,1,0:T(1,128)S(1)} all-to-all(f32[32,1,128]{2,1,0:T(1,128)S(1)} %get-tuple-element.64), channel_id=1, replica_groups=mesh['cols'=4,'rows'=8] {'cols','rows'}, dimensions={0} | all-to-all | bytes 32768 | tf_op jit(solution)/shard_map/all_to_all | solution.py:509
  64.2 2.1 %shard_map.91 = (f32[32,1024]{1,0:T(8,128)}, f32[32,1024]{1,0:T(8,128)}) custom-call(s32[4]{0:T(128)S(1)} %get-tuple-element.73.held, s32[8]{0:T(128)S(1)} %select_reduce_fusion.1.where, f32[32,1,128]{2,1,0:T(1,128)S(1)} %all_to_all.10.grams, f32[8,128]{1,0:T(8,128)S(1)} %get-tuple-element.65.scale, f32[32,1024]{1,0:T(8,128)S(1)} %copy-done.1, ...), custom_call_target="tpu_custom_call" | custom-call | tf_op jit(solution)/shard_map/pallas_call | solution.py:32
  (41 shorter events, 0.9 us)
Async XLA Ops:
  0.6 2.1 %copy-start.1 = (f32[32,1024]{1,0:T(8,128)S(1)}, f32[32,1024]{1,0:T(8,128)}, u32[]{:S(2)}) copy-start(f32[32,1024]{1,0:T(8,128)} %gradient.3) | copy-start | bytes 393220
  0.6 2.1 %copy-start.3 = (f32[128,32]{0,1:T(8,128)S(1)}, f32[128,32]{0,1:T(8,128)}, u32[]{:S(2)}) copy-start(f32[128,32]{0,1:T(8,128)} %param.9) | copy-start | bytes 49156
  2.7 4.5 %copy-start.2 = (f32[3,160,128]{2,1,0:T(8,128)S(1)}, f32[3,160,128]{2,1,0:T(8,128)}, u32[]{:S(2)}) copy-start(f32[3,160,128]{2,1,0:T(8,128)} %shard_map.86) | copy-start | bytes 737284
  2.8 15.7 %collective-permute-start.3 = (f32[32,1152]{1,0:T(8,128)S(1)}, f32[32,1152]{1,0:T(8,128)S(1)}, u32[]{:S(2)}, u32[]{:S(2)}) collective-permute-start(f32[32,1152]{1,0:T(8,128)S(1)} %pad_maximum_fusion.1.refs_0_), channel_id=1, source_target_pairs={{0,24},{8,0},{16,8},{24,16},{1,25},{9,1},{17,9},{25,17},{2,26},{10... | collective-permute-start | bytes 442376 | tf_op jit(solution)/shard_map/ppermute | solution.py:117
  6.8 12.5 %collective-permute-start.4 = (f32[32,1152]{1,0:T(8,128)S(1)}, f32[32,1152]{1,0:T(8,128)S(1)}, u32[]{:S(2)}, u32[]{:S(2)}) collective-permute-start(f32[32,1152]{1,0:T(8,128)S(1)} %pad_maximum_fusion.1.refs_0_), channel_id=1, source_target_pairs={{0,16},{8,24},{16,0},{24,8},{1,17},{9,25},{17,1},{25,9},{2,18},{10... | collective-permute-start | bytes 442376 | tf_op jit(solution)/shard_map/ppermute | solution.py:117
  7.3 24.1 %collective-permute-start = (f32[3,160,128]{2,1,0:T(8,128)S(1)}, f32[3,160,128]{2,1,0:T(8,128)S(1)}, u32[]{:S(2)}, u32[]{:S(2)}) collective-permute-start(f32[3,160,128]{2,1,0:T(8,128)S(1)} %copy-done.2), channel_id=1, source_target_pairs={{0,6},{1,7},{2,0},{3,1},{4,2},{5,3},{6,4},{7,5},{8,14},{9,15},{10,... | collective-permute-start | bytes 737288 | tf_op jit(solution)/shard_map/ppermute | solution.py:117
  10.9 20.5 %collective-permute-start.1 = (f32[3,160,128]{2,1,0:T(8,128)S(1)}, f32[3,160,128]{2,1,0:T(8,128)S(1)}, u32[]{:S(2)}, u32[]{:S(2)}) collective-permute-start(f32[3,160,128]{2,1,0:T(8,128)S(1)} %copy-done.2), channel_id=1, source_target_pairs={{0,4},{1,5},{2,6},{3,7},{4,0},{5,1},{6,2},{7,3},{8,12},{9,13},{10,... | collective-permute-start | bytes 737288 | tf_op jit(solution)/shard_map/ppermute | solution.py:117
  10.9 20.5 %collective-permute-start.2 = (f32[3,160,128]{2,1,0:T(8,128)S(1)}, f32[3,160,128]{2,1,0:T(8,128)S(1)}, u32[]{:S(2)}, u32[]{:S(2)}) collective-permute-start(f32[3,160,128]{2,1,0:T(8,128)S(1)} %copy-done.2), channel_id=1, source_target_pairs={{0,2},{1,3},{2,4},{3,5},{4,6},{5,7},{6,0},{7,1},{8,10},{9,11},{10,... | collective-permute-start | bytes 737288 | tf_op jit(solution)/shard_map/ppermute | solution.py:117
  12.6 0.7 copy-start.4
  12.6 0.7 copy-start.5
  13.9 17.5 %all-to-all-start = ((s32[8,1,128]{2,1,0:T(1,128)}), s32[8,1,128]{2,1,0:T(1,128)S(1)}, u32[]{:S(2)}, u32[]{:S(2)}) async-start(s32[8,1,128]{2,1,0:T(1,128)} %broadcast_in_dim.99), calls=%async_computation | async-start | bytes 8192 | tf_op jit(solution)/shard_map/all_to_all | solution.py:155
  18.5 7.2 %collective-permute-start.5 = (f32[32,1152]{1,0:T(8,128)S(1)}, f32[32,1152]{1,0:T(8,128)S(1)}, u32[]{:S(2)}, u32[]{:S(2)}) collective-permute-start(f32[32,1152]{1,0:T(8,128)S(1)} %pad_maximum_fusion.1.refs_0_), channel_id=1, source_target_pairs={{0,8},{8,16},{16,24},{24,0},{1,9},{9,17},{17,25},{25,1},{2,10},{10... | collective-permute-start | bytes 442376 | tf_op jit(solution)/shard_map/ppermute | solution.py:117
  31.5 2.6 %collective-permute-start.6 = (f32[4,3,160,128]{3,2,1,0:T(8,128)S(1)}, f32[4,3,160,128]{3,2,1,0:T(8,128)S(1)}, u32[]{:S(2)}, u32[]{:S(2)}) collective-permute-start(f32[4,3,160,128]{3,2,1,0:T(8,128)S(1)} %pad_maximum_fusion.near), channel_id=1, source_target_pairs={{0,1},{1,0},{2,3},{3,2},{4,5},{5,4},{6,7},{7,6},{8,9},{9,8},{10,11... | collective-permute-start | bytes 2949128 | tf_op jit(solution)/shard_map/ppermute | solution.py:160
  32.5 9.6 %copy-start = (f32[8,128,128]{2,1,0:T(8,128)S(1)}, f32[8,128,128]{2,1,0:T(8,128)}, u32[]{:S(2)}) copy-start(f32[8,128,128]{2,1,0:T(8,128)} %jacobi.5) | copy-start | bytes 1572868
  38.4 7.9 %collective-permute-start.7 = (f32[6,1,32,128]{3,2,1,0:T(8,128)S(1)}, f32[6,1,32,128]{3,2,1,0:T(8,128)S(1)}, u32[]{:S(2)}, u32[]{:S(2)}) collective-permute-start(f32[6,1,32,128]{3,2,1,0:T(8,128)S(1)} %get-tuple-element.53), channel_id=1, source_target_pairs={{0,24},{8,0},{16,8},{24,16},{1,25},{9,1},{17,9},{25,17},{2,26},{10... | collective-permute-start | bytes 294920 | tf_op jit(solution)/shard_map/ppermute | solution.py:117
  39.3 7.0 %collective-permute-start.8 = (f32[6,1,32,128]{3,2,1,0:T(8,128)S(1)}, f32[6,1,32,128]{3,2,1,0:T(8,128)S(1)}, u32[]{:S(2)}, u32[]{:S(2)}) collective-permute-start(f32[6,1,32,128]{3,2,1,0:T(8,128)S(1)} %get-tuple-element.54), channel_id=1, source_target_pairs={{0,16},{8,24},{16,0},{24,8},{1,17},{9,25},{17,1},{25,9},{2,18},{10... | collective-permute-start | bytes 294920 | tf_op jit(solution)/shard_map/ppermute | solution.py:117
  40.5 5.8 %collective-permute-start.9 = (f32[6,1,32,128]{3,2,1,0:T(8,128)S(1)}, f32[6,1,32,128]{3,2,1,0:T(8,128)S(1)}, u32[]{:S(2)}, u32[]{:S(2)}) collective-permute-start(f32[6,1,32,128]{3,2,1,0:T(8,128)S(1)} %get-tuple-element.55), channel_id=1, source_target_pairs={{0,8},{8,16},{16,24},{24,0},{1,9},{9,17},{17,25},{25,1},{2,10},{10... | collective-permute-start | bytes 294920 | tf_op jit(solution)/shard_map/ppermute | solution.py:117
  48.8 15.4 %collective-permute-start.10 = (f32[6,1,32,128]{3,2,1,0:T(8,128)S(1)}, f32[6,1,32,128]{3,2,1,0:T(8,128)S(1)}, u32[]{:S(2)}, u32[]{:S(2)}) collective-permute-start(f32[6,1,32,128]{3,2,1,0:T(8,128)S(1)} %get-tuple-element.69), channel_id=1, source_target_pairs={{0,8},{8,16},{16,24},{24,0},{1,9},{9,17},{17,25},{25,1},{2,10},{10... | collective-permute-start | bytes 294920 | tf_op jit(solution)/shard_map/ppermute | solution.py:117
  49.6 14.5 %collective-permute-start.11 = (f32[6,1,32,128]{3,2,1,0:T(8,128)S(1)}, f32[6,1,32,128]{3,2,1,0:T(8,128)S(1)}, u32[]{:S(2)}, u32[]{:S(2)}) collective-permute-start(f32[6,1,32,128]{3,2,1,0:T(8,128)S(1)} %get-tuple-element.70), channel_id=1, source_target_pairs={{0,16},{8,24},{16,0},{24,8},{1,17},{9,25},{17,1},{25,9},{2,18},{10... | collective-permute-start | bytes 294920 | tf_op jit(solution)/shard_map/ppermute | solution.py:117
  50.8 13.4 %collective-permute-start.12 = (f32[6,1,32,128]{3,2,1,0:T(8,128)S(1)}, f32[6,1,32,128]{3,2,1,0:T(8,128)S(1)}, u32[]{:S(2)}, u32[]{:S(2)}) collective-permute-start(f32[6,1,32,128]{3,2,1,0:T(8,128)S(1)} %get-tuple-element.71), channel_id=1, source_target_pairs={{0,24},{8,0},{16,8},{24,16},{1,25},{9,1},{17,9},{25,17},{2,26},{10... | collective-permute-start | bytes 294920 | tf_op jit(solution)/shard_map/ppermute | solution.py:117

commit v4 on v3

--- a/solution.py
+++ b/solution.py
@@ -13,6 +13,7 @@
 
 
 NOWHERE = 2**20
+LEVELS = 32767.0
 GRANT_BYTES = 24 * 2**20
 WHOLE_BYTES = 60 * 2**20
 
@@ -56,10 +57,16 @@
     return both[:tall] + (both[tall:] + plain_dot(high, rest))
 
 
+def code(x, top):
+    unit = LEVELS / jnp.where(top > 0, top, 1.0)
+    return jnp.floor(x * unit + 0.5).astype(jnp.int32).astype(jnp.int16)
+
+
 def pack_kernel(
-    local, gradient, jacobi, tiles, packed, blocks, whole, inverse, coupling, done
+    local, gradient, jacobi, tiles, packed, marks, blocks, whole, inverse, coupling, done
 ):
     slots = packed.shape[0]
+    width = whole.shape[0]
     contract = (((1,), (1,)), ((), ()))
     moves = [(local, blocks), (jacobi, inverse), (tiles, coupling), (gradient, whole)]
     copies = [
@@ -70,35 +77,55 @@
         copy.start()
     for copy in copies:
         copy.wait()
+    lane = lax.broadcasted_iota(jnp.int32, (width, BLOCK), 1)
+    row = lax.broadcasted_iota(jnp.int32, (width, BLOCK), 0)
+    noted = jnp.zeros((width, BLOCK), f32)
     for slot in range(slots):
         block = blocks[slot]
         halves = jnp.concatenate(split(inverse[block]), 0)
         both = lax.dot_general(halves, coupling[slot], contract, preferred_element_type=f32)
-        packed[slot, :BLOCK, :] = both[:BLOCK] + both[BLOCK:]
+        operator = both[:BLOCK] + both[BLOCK:]
+        top = jnp.max(jnp.max(jnp.abs(operator), axis=0, keepdims=True), axis=1, keepdims=True)
+        packed[slot, :BLOCK, :] = code(operator, top)
+        noted = jnp.where((lane == 3 * slots + slot) & (row == 0), top, noted)
         columns = pl.ds(pl.multiple_of(block * BLOCK, BLOCK), BLOCK)
-        packed[slot, BLOCK:, :] = whole[:, columns]
-
-
-def chain_kernel(sources, give, near, far, *refs):
-    sends, (high, low, held, out) = refs[:-4], refs[-4:]
+        part = whole[:, columns]
+        top = jnp.max(jnp.abs(part), axis=1, keepdims=True)
+        packed[slot, BLOCK:, :] = code(part, top)
+        noted = jnp.where(lane == 4 * slots + slot * width + row, top, noted)
+    marks[...] = jnp.sum(noted, axis=0, keepdims=True)
+
+
+def chain_kernel(sources, give, tops, told, near, far, *refs):
+    sends, (operators, held, out) = refs[:-3], refs[-3:]
     groups, slots = near.shape[:2]
     half = groups * slots
     total = 2 * half
     width = held.shape[1]
     share = sends[0].shape[1]
+    lane = lax.broadcasted_iota(jnp.int32, (width, BLOCK), 1)
+    row = lax.broadcasted_iota(jnp.int32, (width, BLOCK), 0)
     for q in range(total):
         ref = near if q < half else far
-        group, slot = divmod(q % half, slots)
-        high[q], low[q] = split(ref[group, slot, :BLOCK, :])
-        held[q] = ref[group, slot, BLOCK:, :]
+        device, slot = divmod(q, slots)
+        group = device % groups
+        high, low = split(ref[group, slot, :BLOCK, :].astype(f32))
+        operators[q, :, :BLOCK] = high
+        operators[q, :, BLOCK:] = low
+        here = lane == 4 * slots + slot * width + row
+        top = jnp.where(here, told[device : device + 1, :], 0.0)
+        top = jnp.sum(top, axis=1, keepdims=True) * (1.0 / LEVELS)
+        held[q] = ref[group, slot, BLOCK:, :].astype(f32) * top
     held[total] = jnp.zeros((width, BLOCK), f32)
     out[total] = jnp.zeros((width, BLOCK), f32)
 
     def step(j, carry):
         for q in range(total):
-            first, second = split(held[q])
-            both = plain_dot(jnp.concatenate([first, second], 0), high[q])
-            out[q] = both[:width] + both[width:] + plain_dot(first, low[q])
+            four = plain_dot(jnp.concatenate(split(held[q]), 0), operators[q])
+            value = (four[:width, :BLOCK] + four[width:, :BLOCK]) + (
+                four[:width, BLOCK:] + four[width:, BLOCK:]
+            )
+            out[q] = value * (tops[q] * (1.0 / LEVELS))
         for q in range(total):
             value = out[sources[q * slots]]
             for i in range(1, slots):
@@ -129,9 +156,12 @@
     devices = lax.axis_size("rows")
     columns = lax.axis_size("cols")
     groups = devices // 2
-    packed = call(
+    packed, marks = call(
         pack_kernel,
-        jax.ShapeDtypeStruct((slots, BLOCK + width, BLOCK), f32),
+        (
+            jax.ShapeDtypeStruct((slots, BLOCK + width, BLOCK), jnp.int16),
+            jax.ShapeDtypeStruct((1, BLOCK), f32),
+        ),
         whole_local,
         gradient,
         jacobi,
@@ -150,7 +180,7 @@
     gradient, factor, _ = lax.optimization_barrier((gradient, factor, packed))
     pieces = whole_pieces(gradient, factor)
     own = jnp.concatenate([local, remote, live.astype(jnp.int32)])
-    own = jnp.pad(own, (0, BLOCK - own.shape[0]))
+    own = jnp.pad(own.astype(f32), (0, BLOCK - own.shape[0])) + marks[0]
     told = jnp.broadcast_to(own[None, None, :], (devices, 1, BLOCK))
     told = lax.all_to_all(told, "rows", 0, 0, tiled=True)
     told = told[:, 0]
@@ -163,11 +193,12 @@
     position = jnp.arange(devices, dtype=jnp.int32)
     base = me ^ (position // groups)
     device = (base + 2 * (position % groups)) % devices
-    pick = (device[:, None] == jnp.arange(devices, dtype=jnp.int32)[None, :]).astype(jnp.int32)
-    told = jnp.sum(pick[:, :, None] * told[None, :, :], axis=1)
+    pick = (device[:, None] == jnp.arange(devices, dtype=jnp.int32)[None, :])
+    told = jnp.sum(jnp.where(pick[:, :, None], told[None, :, :], 0.0), axis=1)
     locals_, remotes, lives = (
-        told[:, i * slots : (i + 1) * slots] for i in range(3)
-    )
+        told[:, i * slots : (i + 1) * slots].astype(jnp.int32) for i in range(3)
+    )
+    tops = told[:, 3 * slots : 4 * slots].reshape(-1)
     owner = (remotes // blocks).reshape(-1)
     holder = jnp.broadcast_to(device[:, None], locals_.shape).reshape(-1)
     alive = lives.reshape(-1) > 0
@@ -192,12 +223,13 @@
         tuple([shape((ITERS, share, width, BLOCK), f32)] * columns),
         sources,
         jnp.where(order < slots, order, total),
+        tops,
+        told,
         near,
         far,
-        scalars=2,
+        scalars=3,
         scratch=[
-            pltpu.VMEM((total, BLOCK, BLOCK), jnp.bfloat16),
-            pltpu.VMEM((total, BLOCK, BLOCK), jnp.bfloat16),
+            pltpu.VMEM((total, BLOCK, 2 * BLOCK), jnp.bfloat16),
             pltpu.VMEM((total + 1, width, BLOCK), f32),
             pltpu.VMEM((total + 1, width, BLOCK), f32),
         ],
@@ -434,8 +466,9 @@
     live = jnp.arange(slots, dtype=jnp.int32) < tile_count[0]
     lists = (tile_local[:slots], tile_remote[:slots], live)
 
-    gathered = devices * slots * BLOCK * (BLOCK + width) * 4
-    whole = gathered <= GATHER_BYTES and devices % 2 == 0 and not exchange
+    gathered = devices * slots * BLOCK * (BLOCK + width) * 2
+    noted = slots * (4 + width) <= BLOCK
+    whole = gathered <= GATHER_BYTES and noted and devices % 2 == 0 and not exchange
     units = slots if whole else blocks
     share = -(-units // columns)
     numbers = jnp.arange(columns * share, dtype=jnp.int32)

time: 66.5 us -> 63 us (0.947)
  waiting for transfers between devices: 11.6 us -> 7.58 us
  local copies, waits for them, and re-layouts: 1.78 us -> 2.51 us
    all_to_all x1, waiting for transfers between devices: 3.52 us -> 0.01 us  [chain_gathered(): told = lax.all_to_all(told, 'rows', 0, 0, tiled=True)]
    ppermute x12, starting transfers between devices: 17.2 us -> 18.4 us  [shift(): return lax.ppermute(x, axis, [(i, (i - by) % size) for i in range(size)])]
    all_to_all x1, starting transfers between devices: 4.09 us -> 3.31 us  [chain_gathered(): told = lax.all_to_all(told, 'rows', 0, 0, tiled=True)]
    unnamed x12 -> x14, local copies, waits for them, and re-layouts: 0.68 us -> 1.33 us
where the time goes in v4:
time: 63 us; the launch traced here: 62.8 us
  starting transfers between devices  21.8 us (35%)
  Pallas kernels  16.6 us (26%)
  blocking collectives  11.4 us (18%)
  waiting for transfers between devices  7.58 us (12%)
  local copies, waits for them, and re-layouts  2.51 us (4%)
  between operations  1.48 us (2%)
  other arithmetic  1.32 us (2%)
    ppermute x12, starting transfers between devices, shift(): return lax.ppermute(x, axis, [(i, (i - by) % size) for i in range(size)])  18.4 us
    pallas_call x6, Pallas kernels, call(): pl.pallas_call(kernel, out_shape=outs, in_specs=specs, out_specs=tuple([V...  16.6 us
    all_to_all x1, blocking collectives, on_device(): grams = lax.all_to_all(gram, ('cols', 'rows'), 0, 0, tiled=True)  11.4 us
    ppermute x12, waiting for transfers between devices, shift(): return lax.ppermute(x, axis, [(i, (i - by) % size) for i in range(size)])  6.34 us
    all_to_all x1, starting transfers between devices, chain_gathered(): told = lax.all_to_all(told, 'rows', 0, 0, tiled=True)  3.31 us
    unnamed x14, local copies, waits for them, and re-layouts  1.33 us
  transfers between devices with their start and end apart: 14, of which 3 were waited for; matrix products, arithmetic and copies ran while one was open for 3% of the time, Pallas kernels for 10%

profile of v4, /device:TPU:0, one launch (start us, length us, event | category | flops | bytes accessed | tf_op | source)
XLA Modules:
  0.0 62.8 jit_solution(9722828840418803092)
XLA Ops:
  0.6 2.2 %shard_map.86 = (s16[3,160,128]{2,1,0:T(8,128)(2,1)}, f32[1,128]{1,0:T(1,128)}) custom-call(s32[4]{0:T(128)} %local.1, f32[32,1024]{1,0:T(8,128)} %gradient.3, f32[8,128,128]{2,1,0:T(8,128)} %jacobi.5, bf16[4,128,128]{2,1,0:T(8,128)(2,1)} %tiles.1), custom_call_target="tpu_custom_call" | custom-call | tf_op jit(solution)/shard_map/pallas_call | solution.py:33
  2.8 3.1 %collective-permute-start.2 = (s16[3,160,128]{2,1,0:T(8,128)(2,1)}, s16[3,160,128]{2,1,0:T(8,128)(2,1)S(1)}, u32[]{:S(2)}, u32[]{:S(2)}) collective-permute-start(s16[3,160,128]{2,1,0:T(8,128)(2,1)} %get-tuple-element.48), channel_id=1, source_target_pairs={{0,2},{1,3},{2,4},{3,5},{4,6},{5,7},{6,0},{7,1},{8,10},{9,11},{10,... | collective-permute-start | bytes 368648 | tf_op jit(solution)/shard_map/ppermute | solution.py:144
  5.9 2.6 %collective-permute-start.1 = (s16[3,160,128]{2,1,0:T(8,128)(2,1)}, s16[3,160,128]{2,1,0:T(8,128)(2,1)S(1)}, u32[]{:S(2)}, u32[]{:S(2)}) collective-permute-start(s16[3,160,128]{2,1,0:T(8,128)(2,1)} %get-tuple-element.48), channel_id=1, source_target_pairs={{0,4},{1,5},{2,6},{3,7},{4,0},{5,1},{6,2},{7,3},{8,12},{9,13},{10,... | collective-permute-start | bytes 368648 | tf_op jit(solution)/shard_map/ppermute | solution.py:144
  8.5 1.3 %collective-permute-start = (s16[3,160,128]{2,1,0:T(8,128)(2,1)}, s16[3,160,128]{2,1,0:T(8,128)(2,1)S(1)}, u32[]{:S(2)}, u32[]{:S(2)}) collective-permute-start(s16[3,160,128]{2,1,0:T(8,128)(2,1)} %get-tuple-element.48), channel_id=1, source_target_pairs={{0,6},{1,7},{2,0},{3,1},{4,2},{5,3},{6,4},{7,5},{8,14},{9,15},{10,... | collective-permute-start | bytes 368648 | tf_op jit(solution)/shard_map/ppermute | solution.py:144
  9.9 1.5 %collective-permute-start.5 = (f32[32,1152]{1,0:T(8,128)S(1)}, f32[32,1152]{1,0:T(8,128)S(1)}, u32[]{:S(2)}, u32[]{:S(2)}) collective-permute-start(f32[32,1152]{1,0:T(8,128)S(1)} %pad_maximum_fusion.refs_0_), channel_id=1, source_target_pairs={{0,8},{8,16},{16,24},{24,0},{1,9},{9,17},{17,25},{25,1},{2,10},{10... | collective-permute-start | bytes 442376 | tf_op jit(solution)/shard_map/ppermute | solution.py:144
  11.4 1.5 %collective-permute-start.4 = (f32[32,1152]{1,0:T(8,128)S(1)}, f32[32,1152]{1,0:T(8,128)S(1)}, u32[]{:S(2)}, u32[]{:S(2)}) collective-permute-start(f32[32,1152]{1,0:T(8,128)S(1)} %pad_maximum_fusion.refs_0_), channel_id=1, source_target_pairs={{0,16},{8,24},{16,0},{24,8},{1,17},{9,25},{17,1},{25,9},{2,18},{10... | collective-permute-start | bytes 442376 | tf_op jit(solution)/shard_map/ppermute | solution.py:144
  13.6 0.6 %copy-done.4 = s32[4]{0:T(128)S(1)} copy-done((s32[4]{0:T(128)S(1)}, s32[4]{0:T(128)}, u32[]{:S(2)}) %copy-start.4) | copy-done | bytes 40
  14.4 0.7 %copy-done.6 = f32[1,128]{1,0:T(1,128)S(1)} copy-done((f32[1,128]{1,0:T(1,128)S(1)}, f32[1,128]{1,0:T(1,128)}, u32[]{:S(2)}) %copy-start.6) | copy-done | bytes 536
  15.0 0.6 broadcast_in_dim.119
  15.6 3.3 %all-to-all-start = ((f32[8,1,128]{2,1,0:T(1,128)}), f32[8,1,128]{2,1,0:T(1,128)S(1)}, u32[]{:S(2)}, u32[]{:S(2)}) async-start(f32[8,1,128]{2,1,0:T(1,128)} %broadcast_in_dim.119), calls=%async_computation | async-start | bytes 8192 | tf_op jit(solution)/shard_map/all_to_all | solution.py:185
  18.9 0.2 fusion.5
  19.2 0.2 select_reduce_fusion.3
  19.4 1.5 %collective-permute-start.3 = (f32[32,1152]{1,0:T(8,128)S(1)}, f32[32,1152]{1,0:T(8,128)S(1)}, u32[]{:S(2)}, u32[]{:S(2)}) collective-permute-start(f32[32,1152]{1,0:T(8,128)S(1)} %pad_maximum_fusion.refs_0_), channel_id=1, source_target_pairs={{0,24},{8,0},{16,8},{24,16},{1,25},{9,1},{17,9},{25,17},{2,26},{10... | collective-permute-start | bytes 442376 | tf_op jit(solution)/shard_map/ppermute | solution.py:144
  21.1 4.5 %collective-permute-done.3.refs_1_ = f32[32,1152]{1,0:T(8,128)S(1)} collective-permute-done((f32[32,1152]{1,0:T(8,128)S(1)}, f32[32,1152]{1,0:T(8,128)S(1)}, u32[]{:S(2)}, u32[]{:S(2)}) %collective-permute-start.3) | collective-permute-done | bytes 147488 | tf_op jit(solution)/shard_map/ppermute | solution.py:144
  25.6 2.2 %shard_map.87 = (f32[128,128]{1,0:T(8,128)S(1)}, f32[224,128]{1,0:T(8,128)S(1)}, f32[8,128]{1,0:T(8,128)S(1)}) custom-call(s32[1]{0:T(128)} %bitcast.2.turn, f32[32,1152]{1,0:T(8,128)S(1)} %pad_maximum_fusion.refs_0_, f32[32,1152]{1,0:T(8,128)S(1)} %collective-permute-done.3.refs_1_, f32[32,1152]{1,0:T(8,128)S(1)} %collective-permute-done.4.refs_2_, ...), custom_call_target="tpu_custom_call" | custom-call | tf_op jit(solution)/shard_map/pallas_call | solution.py:33
  28.4 0.2 select_reduce_fusion.1
  28.8 0.1 and_select_fusion
  28.9 0.1 select_n.108.sources
  29.0 1.2 %collective-permute-done.6.far = s16[4,3,160,128]{3,2,1,0:T(8,128)(2,1)S(1)} collective-permute-done((s16[4,3,160,128]{3,2,1,0:T(8,128)(2,1)S(1)}, s16[4,3,160,128]{3,2,1,0:T(8,128)(2,1)S(1)}, u32[]{:S(2)}, u32[]{:S(2)}) %collective-permute-start.6) | collective-permute-done | bytes 491552 | tf_op jit(solution)/shard_map/ppermute | solution.py:190
  30.3 3.6 %shard_map.88 = (f32[6,1,32,128]{3,2,1,0:T(8,128)S(1)}, f32[6,1,32,128]{3,2,1,0:T(8,128)S(1)}, f32[6,1,32,128]{3,2,1,0:T(8,128)S(1)}, f32[6,1,32,128]{3,2,1,0:T(8,128)S(1)}) custom-call(s32[72]{0:T(128)S(1)} %select_n.108.sources, s32[4]{0:T(128)S(1)} %compare_select_fusion.give, f32[24]{0:T(128)S(1)} %reshape.128.tops, ...), custom_call_target="tpu_custom_call" | custom-call | tf_op jit(solution)/shard_map/pallas_call | solution.py:33
  33.9 2.4 %collective-permute-start.7 = (f32[6,1,32,128]{3,2,1,0:T(8,128)S(1)}, f32[6,1,32,128]{3,2,1,0:T(8,128)S(1)}, u32[]{:S(2)}, u32[]{:S(2)}) collective-permute-start(f32[6,1,32,128]{3,2,1,0:T(8,128)S(1)} %get-tuple-element.57), channel_id=1, source_target_pairs={{0,24},{8,0},{16,8},{24,16},{1,25},{9,1},{17,9},{25,17},{2,26},{10... | collective-permute-start | bytes 294920 | tf_op jit(solution)/shard_map/ppermute | solution.py:144
  36.3 0.5 collective-permute-start.8
  36.8 0.1 collective-permute-start.9
  36.9 0.1 select_reduce_fusion.2.where
  37.0 4.2 %shard_map.89 = (f32[8,192,128]{2,1,0:T(8,128)S(1)}, f32[8,192,128]{2,1,0:T(8,128)S(1)}, f32[1,128]{1,0:T(1,128)S(1)}, f32[1,128,128]{2,1,0:T(8,128)S(1)}) custom-call(s32[8]{0:T(128)S(1)} %select_reduce_fusion.2.where, s32[4]{0:T(128)S(1)} %get-tuple-element.77.held, f32[224,128]{1,0:T(8,128)S(1)} %get-tuple-element.60.powers, f32[8,128,128]{2,1,0:T(8,128)S(1)} %copy-done, ...), custom_call_target="tpu_custom_call" | custom-call | tf_op jit(solution)/shard_map/pallas_call | solution.py:33
  41.2 1.8 %collective-permute-done.8.refs_2_ = f32[6,1,32,128]{3,2,1,0:T(8,128)S(1)} collective-permute-done((f32[6,1,32,128]{3,2,1,0:T(8,128)S(1)}, f32[6,1,32,128]{3,2,1,0:T(8,128)S(1)}, u32[]{:S(2)}, u32[]{:S(2)}) %collective-permute-start.8) | collective-permute-done | bytes 98336 | tf_op jit(solution)/shard_map/ppermute | solution.py:144
  43.0 2.4 %shard_map.90 = (f32[32,1,128]{2,1,0:T(1,128)S(1)}, f32[6,1,32,128]{3,2,1,0:T(8,128)S(1)}, f32[6,1,32,128]{3,2,1,0:T(8,128)S(1)}, f32[6,1,32,128]{3,2,1,0:T(8,128)S(1)}, f32[6,1,32,128]{3,2,1,0:T(8,128)S(1)}) custom-call(s32[4]{0:T(128)S(1)} %get-tuple-element.77.held, s32[4]{0:T(128)S(1)} %get-tuple-element.76.used, ...), custom_call_target="tpu_custom_call" | custom-call | tf_op jit(solution)/shard_map/pallas_call | solution.py:33
  45.4 1.1 %collective-permute-start.10 = (f32[6,1,32,128]{3,2,1,0:T(8,128)S(1)}, f32[6,1,32,128]{3,2,1,0:T(8,128)S(1)}, u32[]{:S(2)}, u32[]{:S(2)}) collective-permute-start(f32[6,1,32,128]{3,2,1,0:T(8,128)S(1)} %get-tuple-element.73), channel_id=1, source_target_pairs={{0,8},{8,16},{16,24},{24,0},{1,9},{9,17},{17,25},{25,1},{2,10},{10... | collective-permute-start | bytes 294920 | tf_op jit(solution)/shard_map/ppermute | solution.py:144
  46.6 0.5 collective-permute-start.11
  47.1 2.2 %collective-permute-start.12 = (f32[6,1,32,128]{3,2,1,0:T(8,128)S(1)}, f32[6,1,32,128]{3,2,1,0:T(8,128)S(1)}, u32[]{:S(2)}, u32[]{:S(2)}) collective-permute-start(f32[6,1,32,128]{3,2,1,0:T(8,128)S(1)} %get-tuple-element.75), channel_id=1, source_target_pairs={{0,24},{8,0},{16,8},{24,16},{1,25},{9,1},{17,9},{25,17},{2,26},{10... | collective-permute-start | bytes 294920 | tf_op jit(solution)/shard_map/ppermute | solution.py:144
  49.2 11.4 %all_to_all.10.grams = f32[32,1,128]{2,1,0:T(1,128)S(1)} all-to-all(f32[32,1,128]{2,1,0:T(1,128)S(1)} %get-tuple-element.68), channel_id=1, replica_groups=mesh['cols'=4,'rows'=8] {'cols','rows'}, dimensions={0} | all-to-all | bytes 32768 | tf_op jit(solution)/shard_map/all_to_all | solution.py:542
  60.7 2.1 %shard_map.91 = (f32[32,1024]{1,0:T(8,128)}, f32[32,1024]{1,0:T(8,128)}) custom-call(s32[4]{0:T(128)S(1)} %get-tuple-element.77.held, s32[8]{0:T(128)S(1)} %select_reduce_fusion.2.where, f32[32,1,128]{2,1,0:T(1,128)S(1)} %all_to_all.10.grams, f32[8,128]{1,0:T(8,128)S(1)} %get-tuple-element.69.scale, f32[32,1024]{1,0:T(8,128)S(1)} %copy-done.1, ...), custom_call_target="tpu_custom_call" | custom-call | tf_op jit(solution)/shard_map/pallas_call | solution.py:33
  (45 shorter events, 1.2 us)
Async XLA Ops:
  0.6 9.2 %copy-start.1 = (f32[32,1024]{1,0:T(8,128)S(1)}, f32[32,1024]{1,0:T(8,128)}, u32[]{:S(2)}) copy-start(f32[32,1024]{1,0:T(8,128)} %gradient.3) | copy-start | bytes 393220
  0.6 9.2 %copy-start.3 = (f32[128,32]{0,1:T(8,128)S(1)}, f32[128,32]{0,1:T(8,128)}, u32[]{:S(2)}) copy-start(f32[128,32]{0,1:T(8,128)} %param.9) | copy-start | bytes 49156
  2.8 25.0 %collective-permute-start.2 = (s16[3,160,128]{2,1,0:T(8,128)(2,1)}, s16[3,160,128]{2,1,0:T(8,128)(2,1)S(1)}, u32[]{:S(2)}, u32[]{:S(2)}) collective-permute-start(s16[3,160,128]{2,1,0:T(8,128)(2,1)} %get-tuple-element.48), channel_id=1, source_target_pairs={{0,2},{1,3},{2,4},{3,5},{4,6},{5,7},{6,0},{7,1},{8,10},{9,11},{10,... | collective-permute-start | bytes 368648 | tf_op jit(solution)/shard_map/ppermute | solution.py:144
  5.9 21.9 %collective-permute-start.1 = (s16[3,160,128]{2,1,0:T(8,128)(2,1)}, s16[3,160,128]{2,1,0:T(8,128)(2,1)S(1)}, u32[]{:S(2)}, u32[]{:S(2)}) collective-permute-start(s16[3,160,128]{2,1,0:T(8,128)(2,1)} %get-tuple-element.48), channel_id=1, source_target_pairs={{0,4},{1,5},{2,6},{3,7},{4,0},{5,1},{6,2},{7,3},{8,12},{9,13},{10,... | collective-permute-start | bytes 368648 | tf_op jit(solution)/shard_map/ppermute | solution.py:144
  8.5 19.3 %collective-permute-start = (s16[3,160,128]{2,1,0:T(8,128)(2,1)}, s16[3,160,128]{2,1,0:T(8,128)(2,1)S(1)}, u32[]{:S(2)}, u32[]{:S(2)}) collective-permute-start(s16[3,160,128]{2,1,0:T(8,128)(2,1)} %get-tuple-element.48), channel_id=1, source_target_pairs={{0,6},{1,7},{2,0},{3,1},{4,2},{5,3},{6,4},{7,5},{8,14},{9,15},{10,... | collective-permute-start | bytes 368648 | tf_op jit(solution)/shard_map/ppermute | solution.py:144
  9.9 9.5 %collective-permute-start.5 = (f32[32,1152]{1,0:T(8,128)S(1)}, f32[32,1152]{1,0:T(8,128)S(1)}, u32[]{:S(2)}, u32[]{:S(2)}) collective-permute-start(f32[32,1152]{1,0:T(8,128)S(1)} %pad_maximum_fusion.refs_0_), channel_id=1, source_target_pairs={{0,8},{8,16},{16,24},{24,0},{1,9},{9,17},{17,25},{25,1},{2,10},{10... | collective-permute-start | bytes 442376 | tf_op jit(solution)/shard_map/ppermute | solution.py:144
  11.4 9.7 %collective-permute-start.4 = (f32[32,1152]{1,0:T(8,128)S(1)}, f32[32,1152]{1,0:T(8,128)S(1)}, u32[]{:S(2)}, u32[]{:S(2)}) collective-permute-start(f32[32,1152]{1,0:T(8,128)S(1)} %pad_maximum_fusion.refs_0_), channel_id=1, source_target_pairs={{0,16},{8,24},{16,0},{24,8},{1,17},{9,25},{17,1},{25,9},{2,18},{10... | collective-permute-start | bytes 442376 | tf_op jit(solution)/shard_map/ppermute | solution.py:144
  13.6 0.7 %copy-start.4 = (s32[4]{0:T(128)S(1)}, s32[4]{0:T(128)}, u32[]{:S(2)}) copy-start(s32[4]{0:T(128)} %local.1) | copy-start | bytes 52
  13.6 0.7 %copy-start.5 = (s32[4]{0:T(128)S(1)}, s32[4]{0:T(128)}, u32[]{:S(2)}) copy-start(s32[4]{0:T(128)} %param.13) | copy-start | bytes 52
  14.4 0.7 %copy-start.6 = (f32[1,128]{1,0:T(1,128)S(1)}, f32[1,128]{1,0:T(1,128)}, u32[]{:S(2)}) copy-start(f32[1,128]{1,0:T(1,128)} %get-tuple-element.45) | copy-start | bytes 1540
  15.6 12.2 %all-to-all-start = ((f32[8,1,128]{2,1,0:T(1,128)}), f32[8,1,128]{2,1,0:T(1,128)S(1)}, u32[]{:S(2)}, u32[]{:S(2)}) async-start(f32[8,1,128]{2,1,0:T(1,128)} %broadcast_in_dim.119), calls=%async_computation | async-start | bytes 8192 | tf_op jit(solution)/shard_map/all_to_all | solution.py:185
  19.4 6.2 %collective-permute-start.3 = (f32[32,1152]{1,0:T(8,128)S(1)}, f32[32,1152]{1,0:T(8,128)S(1)}, u32[]{:S(2)}, u32[]{:S(2)}) collective-permute-start(f32[32,1152]{1,0:T(8,128)S(1)} %pad_maximum_fusion.refs_0_), channel_id=1, source_target_pairs={{0,24},{8,0},{16,8},{24,16},{1,25},{9,1},{17,9},{25,17},{2,26},{10... | collective-permute-start | bytes 442376 | tf_op jit(solution)/shard_map/ppermute | solution.py:144
  25.6 2.6 %copy-start.2 = (s16[3,160,128]{2,1,0:T(8,128)(2,1)S(1)}, s16[3,160,128]{2,1,0:T(8,128)(2,1)}, u32[]{:S(2)}) copy-start(s16[3,160,128]{2,1,0:T(8,128)(2,1)} %get-tuple-element.48) | copy-start | bytes 368644
  28.3 1.9 %collective-permute-start.6 = (s16[4,3,160,128]{3,2,1,0:T(8,128)(2,1)S(1)}, s16[4,3,160,128]{3,2,1,0:T(8,128)(2,1)S(1)}, u32[]{:S(2)}, u32[]{:S(2)}) collective-permute-start(s16[4,3,160,128]{3,2,1,0:T(8,128)(2,1)S(1)} %pad_add_fusion.near), channel_id=1, source_target_pairs={{0,1},{1,0},{2,3},{3,2},{4,5},{5,4},{6,7},{7,6},{8,9},{9,8},{10,11... | collective-permute-start | bytes 1474568 | tf_op jit(solution)/shard_map/ppermute | solution.py:190
  28.8 8.2 %copy-start = (f32[8,128,128]{2,1,0:T(8,128)S(1)}, f32[8,128,128]{2,1,0:T(8,128)}, u32[]{:S(2)}) copy-start(f32[8,128,128]{2,1,0:T(8,128)} %jacobi.5) | copy-start | bytes 1572868
  33.9 7.3 %collective-permute-start.7 = (f32[6,1,32,128]{3,2,1,0:T(8,128)S(1)}, f32[6,1,32,128]{3,2,1,0:T(8,128)S(1)}, u32[]{:S(2)}, u32[]{:S(2)}) collective-permute-start(f32[6,1,32,128]{3,2,1,0:T(8,128)S(1)} %get-tuple-element.57), channel_id=1, source_target_pairs={{0,24},{8,0},{16,8},{24,16},{1,25},{9,1},{17,9},{25,17},{2,26},{10... | collective-permute-start | bytes 294920 | tf_op jit(solution)/shard_map/ppermute | solution.py:144
  36.3 6.7 %collective-permute-start.8 = (f32[6,1,32,128]{3,2,1,0:T(8,128)S(1)}, f32[6,1,32,128]{3,2,1,0:T(8,128)S(1)}, u32[]{:S(2)}, u32[]{:S(2)}) collective-permute-start(f32[6,1,32,128]{3,2,1,0:T(8,128)S(1)} %get-tuple-element.58), channel_id=1, source_target_pairs={{0,16},{8,24},{16,0},{24,8},{1,17},{9,25},{17,1},{25,9},{2,18},{10... | collective-permute-start | bytes 294920 | tf_op jit(solution)/shard_map/ppermute | solution.py:144
  36.8 6.2 %collective-permute-start.9 = (f32[6,1,32,128]{3,2,1,0:T(8,128)S(1)}, f32[6,1,32,128]{3,2,1,0:T(8,128)S(1)}, u32[]{:S(2)}, u32[]{:S(2)}) collective-permute-start(f32[6,1,32,128]{3,2,1,0:T(8,128)S(1)} %get-tuple-element.59), channel_id=1, source_target_pairs={{0,8},{8,16},{16,24},{24,0},{1,9},{9,17},{17,25},{25,1},{2,10},{10... | collective-permute-start | bytes 294920 | tf_op jit(solution)/shard_map/ppermute | solution.py:144
  45.4 15.2 %collective-permute-start.10 = (f32[6,1,32,128]{3,2,1,0:T(8,128)S(1)}, f32[6,1,32,128]{3,2,1,0:T(8,128)S(1)}, u32[]{:S(2)}, u32[]{:S(2)}) collective-permute-start(f32[6,1,32,128]{3,2,1,0:T(8,128)S(1)} %get-tuple-element.73), channel_id=1, source_target_pairs={{0,8},{8,16},{16,24},{24,0},{1,9},{9,17},{17,25},{25,1},{2,10},{10... | collective-permute-start | bytes 294920 | tf_op jit(solution)/shard_map/ppermute | solution.py:144
  46.6 14.1 %collective-permute-start.11 = (f32[6,1,32,128]{3,2,1,0:T(8,128)S(1)}, f32[6,1,32,128]{3,2,1,0:T(8,128)S(1)}, u32[]{:S(2)}, u32[]{:S(2)}) collective-permute-start(f32[6,1,32,128]{3,2,1,0:T(8,128)S(1)} %get-tuple-element.74), channel_id=1, source_target_pairs={{0,16},{8,24},{16,0},{24,8},{1,17},{9,25},{17,1},{25,9},{2,18},{10... | collective-permute-start | bytes 294920 | tf_op jit(solution)/shard_map/ppermute | solution.py:144
  47.1 13.6 %collective-permute-start.12 = (f32[6,1,32,128]{3,2,1,0:T(8,128)S(1)}, f32[6,1,32,128]{3,2,1,0:T(8,128)S(1)}, u32[]{:S(2)}, u32[]{:S(2)}) collective-permute-start(f32[6,1,32,128]{3,2,1,0:T(8,128)S(1)} %get-tuple-element.75), channel_id=1, source_target_pairs={{0,24},{8,0},{16,8},{24,16},{1,25},{9,1},{17,9},{25,17},{2,26},{10... | collective-permute-start | bytes 294920 | tf_op jit(solution)/shard_map/ppermute | solution.py:144

commit v5 on v4

--- a/solution.py
+++ b/solution.py
@@ -13,7 +13,9 @@
 
 
 NOWHERE = 2**20
-LEVELS = 32767.0
+LEVELS = 32700.0
+NOTES = 256 / 0.6931471805599453
+NOTE_ROWS = 16
 GRANT_BYTES = 24 * 2**20
 WHOLE_BYTES = 60 * 2**20
 
@@ -57,21 +59,30 @@
     return both[:tall] + (both[tall:] + plain_dot(high, rest))
 
 
-def code(x, top):
-    unit = LEVELS / jnp.where(top > 0, top, 1.0)
+def note(top):
+    return jnp.floor(jnp.log(jnp.maximum(top, 1e-30)) * NOTES).astype(jnp.int32) + 1
+
+
+def noted_range(number):
+    return jnp.exp(number.astype(f32) * (1.0 / NOTES))
+
+
+def code(x, number):
+    unit = LEVELS / noted_range(number)
     return jnp.floor(x * unit + 0.5).astype(jnp.int32).astype(jnp.int16)
 
 
-def pack_kernel(
-    local, gradient, jacobi, tiles, packed, marks, blocks, whole, inverse, coupling, done
-):
-    slots = packed.shape[0]
+def pack_kernel(local, remote, count, gradient, jacobi, tiles, packed, *scratch):
+    blocks, others, lives, whole, inverse, coupling, done = scratch
     width = whole.shape[0]
+    height = BLOCK + width
+    slots = packed.shape[0] // height
     contract = (((1,), (1,)), ((), ()))
-    moves = [(local, blocks), (jacobi, inverse), (tiles, coupling), (gradient, whole)]
+    sources = [local, remote, count, jacobi, tiles, gradient]
+    targets = [blocks, others, lives, inverse, coupling, whole]
     copies = [
         pltpu.make_async_copy(source, target, done.at[i])
-        for i, (source, target) in enumerate(moves)
+        for i, (source, target) in enumerate(zip(sources, targets))
     ]
     for copy in copies:
         copy.start()
@@ -79,43 +90,56 @@
         copy.wait()
     lane = lax.broadcasted_iota(jnp.int32, (width, BLOCK), 1)
     row = lax.broadcasted_iota(jnp.int32, (width, BLOCK), 0)
-    noted = jnp.zeros((width, BLOCK), f32)
+    notes = jnp.zeros((width, BLOCK), jnp.int32)
     for slot in range(slots):
         block = blocks[slot]
         halves = jnp.concatenate(split(inverse[block]), 0)
         both = lax.dot_general(halves, coupling[slot], contract, preferred_element_type=f32)
         operator = both[:BLOCK] + both[BLOCK:]
         top = jnp.max(jnp.max(jnp.abs(operator), axis=0, keepdims=True), axis=1, keepdims=True)
-        packed[slot, :BLOCK, :] = code(operator, top)
-        noted = jnp.where((lane == 3 * slots + slot) & (row == 0), top, noted)
         columns = pl.ds(pl.multiple_of(block * BLOCK, BLOCK), BLOCK)
         part = whole[:, columns]
-        top = jnp.max(jnp.abs(part), axis=1, keepdims=True)
-        packed[slot, BLOCK:, :] = code(part, top)
-        noted = jnp.where(lane == 4 * slots + slot * width + row, top, noted)
-    marks[...] = jnp.sum(noted, axis=0, keepdims=True)
-
-
-def chain_kernel(sources, give, tops, told, near, far, *refs):
-    sends, (operators, held, out) = refs[:-3], refs[-3:]
-    groups, slots = near.shape[:2]
+        tops = jnp.max(jnp.abs(part), axis=1, keepdims=True)
+        at = slot * height
+        packed[at : at + BLOCK, :] = code(operator, note(top))
+        packed[at + BLOCK : at + height, :] = code(part, note(tops))
+        live = jnp.where(slot < lives[0], 1, 0)
+        for place, value in enumerate((block, others[slot], live, note(top))):
+            here = (lane == place * slots + slot) & (row == 0)
+            notes = jnp.where(here, value, notes)
+        notes = jnp.where(lane == 4 * slots + slot * width + row, note(tops), notes)
+    notes = jnp.sum(notes, axis=0, keepdims=True)
+    packed[slots * height :, :] = jnp.broadcast_to(notes, (NOTE_ROWS, BLOCK)).astype(jnp.int16)
+
+
+def chain_kernel(sources, give, near, far, *refs):
+    sends, (operators, tops, held, out) = refs[:-4], refs[-4:]
+    groups = near.shape[0]
+    width = held.shape[1]
+    height = BLOCK + width
+    slots = near.shape[1] // height
     half = groups * slots
     total = 2 * half
-    width = held.shape[1]
     share = sends[0].shape[1]
     lane = lax.broadcasted_iota(jnp.int32, (width, BLOCK), 1)
     row = lax.broadcasted_iota(jnp.int32, (width, BLOCK), 0)
     for q in range(total):
         ref = near if q < half else far
-        device, slot = divmod(q, slots)
-        group = device % groups
-        high, low = split(ref[group, slot, :BLOCK, :].astype(f32))
+        group, slot = divmod(q % half, slots)
+        at = slot * height
+        high, low = split(ref[group, at : at + BLOCK, :].astype(f32))
         operators[q, :, :BLOCK] = high
         operators[q, :, BLOCK:] = low
+        notes = ref[group, slots * height :, :].astype(f32)
+        notes = jnp.concatenate([notes] * (width // NOTE_ROWS), 0)
+        scale = noted_range(
+            jnp.sum(jnp.where(lane == 3 * slots + slot, notes, 0.0), axis=1, keepdims=True)
+        )
+        tops[q] = jnp.broadcast_to(scale * (1.0 / LEVELS), (width, BLOCK))
         here = lane == 4 * slots + slot * width + row
-        top = jnp.where(here, told[device : device + 1, :], 0.0)
-        top = jnp.sum(top, axis=1, keepdims=True) * (1.0 / LEVELS)
-        held[q] = ref[group, slot, BLOCK:, :].astype(f32) * top
+        scale = noted_range(jnp.sum(jnp.where(here, notes, 0.0), axis=1, keepdims=True))
+        part = ref[group, at + BLOCK : at + height, :].astype(f32)
+        held[q] = part * (scale * (1.0 / LEVELS))
     held[total] = jnp.zeros((width, BLOCK), f32)
     out[total] = jnp.zeros((width, BLOCK), f32)
 
@@ -125,7 +149,7 @@
             value = (four[:width, :BLOCK] + four[width:, :BLOCK]) + (
                 four[:width, BLOCK:] + four[width:, BLOCK:]
             )
-            out[q] = value * (tops[q] * (1.0 / LEVELS))
+            out[q] = value * tops[q]
         for q in range(total):
             value = out[sources[q * slots]]
             for i in range(1, slots):
@@ -150,28 +174,32 @@
     return [piece] + [shift(piece, "cols", o) for o in others]
 
 
-def chain_gathered(gradient, factor, jacobi, tiles, whole_local, order, local, remote, live):
+def chain_gathered(
+    gradient, factor, jacobi, tiles, whole_local, whole_remote, count, order, slots
+):
     width = gradient.shape[0]
-    blocks, slots = jacobi.shape[0], local.shape[0]
+    blocks = jacobi.shape[0]
     devices = lax.axis_size("rows")
     columns = lax.axis_size("cols")
     groups = devices // 2
-    packed, marks = call(
+    height = BLOCK + width
+    packed = call(
         pack_kernel,
-        (
-            jax.ShapeDtypeStruct((slots, BLOCK + width, BLOCK), jnp.int16),
-            jax.ShapeDtypeStruct((1, BLOCK), f32),
-        ),
+        jax.ShapeDtypeStruct((slots * height + NOTE_ROWS, BLOCK), jnp.int16),
         whole_local,
+        whole_remote,
+        count,
         gradient,
         jacobi,
         tiles,
         scratch=[
             pltpu.SMEM(whole_local.shape, jnp.int32),
+            pltpu.SMEM(whole_remote.shape, jnp.int32),
+            pltpu.SMEM(count.shape, jnp.int32),
             pltpu.VMEM(gradient.shape, f32),
             pltpu.VMEM(jacobi.shape, f32),
             pltpu.VMEM(tiles.shape, tiles.dtype),
-            pltpu.SemaphoreType.DMA((4,)),
+            pltpu.SemaphoreType.DMA((6,)),
         ],
         place=pl.BlockSpec(memory_space=pl.ANY),
         grant=WHOLE_BYTES,
@@ -179,13 +207,8 @@
     near = [packed] + [shift(packed, "rows", 2 * o) for o in range(1, groups)]
     gradient, factor, _ = lax.optimization_barrier((gradient, factor, packed))
     pieces = whole_pieces(gradient, factor)
-    own = jnp.concatenate([local, remote, live.astype(jnp.int32)])
-    own = jnp.pad(own.astype(f32), (0, BLOCK - own.shape[0])) + marks[0]
-    told = jnp.broadcast_to(own[None, None, :], (devices, 1, BLOCK))
-    told = lax.all_to_all(told, "rows", 0, 0, tiled=True)
-    told = told[:, 0]
     powers = make_powers(pieces)
-    near, pieces, powers, told = lax.optimization_barrier((near, pieces, powers, told))
+    near, pieces, powers = lax.optimization_barrier((near, pieces, powers))
     near = jnp.stack(near)
     far = lax.ppermute(near, "rows", [(i, i ^ 1) for i in range(devices)])
 
@@ -193,12 +216,10 @@
     position = jnp.arange(devices, dtype=jnp.int32)
     base = me ^ (position // groups)
     device = (base + 2 * (position % groups)) % devices
-    pick = (device[:, None] == jnp.arange(devices, dtype=jnp.int32)[None, :])
-    told = jnp.sum(jnp.where(pick[:, :, None], told[None, :, :], 0.0), axis=1)
+    told = jnp.concatenate([x[:, slots * height, :] for x in (near, far)], 0)
     locals_, remotes, lives = (
         told[:, i * slots : (i + 1) * slots].astype(jnp.int32) for i in range(3)
     )
-    tops = told[:, 3 * slots : 4 * slots].reshape(-1)
     owner = (remotes // blocks).reshape(-1)
     holder = jnp.broadcast_to(device[:, None], locals_.shape).reshape(-1)
     alive = lives.reshape(-1) > 0
@@ -223,13 +244,12 @@
         tuple([shape((ITERS, share, width, BLOCK), f32)] * columns),
         sources,
         jnp.where(order < slots, order, total),
-        tops,
-        told,
         near,
         far,
-        scalars=3,
+        scalars=2,
         scratch=[
             pltpu.VMEM((total, BLOCK, 2 * BLOCK), jnp.bfloat16),
+            pltpu.VMEM((total, width, BLOCK), f32),
             pltpu.VMEM((total + 1, width, BLOCK), f32),
             pltpu.VMEM((total + 1, width, BLOCK), f32),
         ],
@@ -467,7 +487,7 @@
     lists = (tile_local[:slots], tile_remote[:slots], live)
 
     gathered = devices * slots * BLOCK * (BLOCK + width) * 2
-    noted = slots * (4 + width) <= BLOCK
+    noted = slots * (4 + width) <= BLOCK and width % NOTE_ROWS == 0 and devices * blocks < 2**15
     whole = gathered <= GATHER_BYTES and noted and devices % 2 == 0 and not exchange
     units = slots if whole else blocks
     share = -(-units // columns)
@@ -493,8 +513,10 @@
             jacobi_inverse,
             coupling_tiles,
             tile_local,
+            tile_remote,
+            tile_count,
             order,
-            *lists,
+            slots,
         )
     else:
         sends = chain_exchanged(

time: 63 us -> 57.2 us (0.908)
  starting transfers between devices: 21.8 us -> 19.1 us
  blocking collectives: 11.4 us -> 8.85 us
  local copies, waits for them, and re-layouts: 2.51 us -> 1.19 us
  waiting for transfers between devices: 7.58 us -> 8.58 us
    all_to_all x1 -> x0, starting transfers between devices: 3.31 us -> none  [chain_gathered(): told = lax.all_to_all(told, 'rows', 0, 0, tiled=True)]
    all_to_all x1, blocking collectives: 11.4 us -> 8.85 us  [on_device(): grams = lax.all_to_all(gram, ('cols', 'rows'), 0, 0, tiled=True)]
    unnamed x14 -> x12, local copies, waits for them, and re-layouts: 1.33 us -> 0.69 us
  transfers between devices with their start and end apart: 14 -> 13, of which waited for: 3 -> 5; matrix products, arithmetic and copies ran while one was open for 3% -> 1% of each run, Pallas kernels for 10% -> 11%
where the time goes in v5:
time: 57.2 us; the launch traced here: 57 us
  starting transfers between devices  19.1 us (33%)
  Pallas kernels  16.7 us (29%)
  blocking collectives  8.85 us (15%)
  waiting for transfers between devices  8.58 us (15%)
  between operations  1.46 us (3%)
  local copies, waits for them, and re-layouts  1.19 us (2%)
  other arithmetic  1.04 us (2%)
    ppermute x12, starting transfers between devices, shift(): return lax.ppermute(x, axis, [(i, (i - by) % size) for i in range(size)])  19 us
    pallas_call x6, Pallas kernels, call(): pl.pallas_call(kernel, out_shape=outs, in_specs=specs, out_specs=tuple([V...  16.7 us
    all_to_all x1, blocking collectives, on_device(): grams = lax.all_to_all(gram, ('cols', 'rows'), 0, 0, tiled=True)  8.85 us
    ppermute x12, waiting for transfers between devices, shift(): return lax.ppermute(x, axis, [(i, (i - by) % size) for i in range(size)])  6.93 us
    ppermute x1, waiting for transfers between devices, chain_gathered(): far = lax.ppermute(near, 'rows', [(i, i ^ 1) for i in range(devices)])  1.64 us
  transfers between devices with their start and end apart: 13, of which 5 were waited for; matrix products, arithmetic and copies ran while one was open for 1% of the time, Pallas kernels for 11%

profile of v5, /device:TPU:0, one launch (start us, length us, event | category | flops | bytes accessed | tf_op | source)
XLA Modules:
  0.0 57.0 jit_solution(963324052981075805)
XLA Ops:
  1.3 2.2 %shard_map.86 = s16[496,128]{1,0:T(8,128)(2,1)} custom-call(s32[4]{0:T(128)} %local.1, s32[4]{0:T(128)} %remote.1, s32[1]{0:T(128)} %copy.17.count, f32[32,1024]{1,0:T(8,128)} %gradient.3, f32[8,128,128]{2,1,0:T(8,128)} %jacobi.5, bf16[4,128,128]{2,1,0:T(8,128)(2,1)} %tiles.1), custom_call_target="tpu_custom_call" | custom-call | tf_op jit(solution)/shard_map/pallas_call | solution.py:35
  3.5 3.1 %collective-permute-start.2 = (s16[496,128]{1,0:T(8,128)(2,1)}, s16[496,128]{1,0:T(8,128)(2,1)S(1)}, u32[]{:S(2)}, u32[]{:S(2)}) collective-permute-start(s16[496,128]{1,0:T(8,128)(2,1)} %shard_map.86), channel_id=1, source_target_pairs={{0,2},{1,3},{2,4},{3,5},{4,6},{5,7},{6,0},{7,1},{8,10},{9,11},{10,... | collective-permute-start | bytes 380936 | tf_op jit(solution)/shard_map/ppermute | solution.py:168
  6.6 2.6 %collective-permute-start.1 = (s16[496,128]{1,0:T(8,128)(2,1)}, s16[496,128]{1,0:T(8,128)(2,1)S(1)}, u32[]{:S(2)}, u32[]{:S(2)}) collective-permute-start(s16[496,128]{1,0:T(8,128)(2,1)} %shard_map.86), channel_id=1, source_target_pairs={{0,4},{1,5},{2,6},{3,7},{4,0},{5,1},{6,2},{7,3},{8,12},{9,13},{10,... | collective-permute-start | bytes 380936 | tf_op jit(solution)/shard_map/ppermute | solution.py:168
  9.2 1.3 %collective-permute-start = (s16[496,128]{1,0:T(8,128)(2,1)}, s16[496,128]{1,0:T(8,128)(2,1)S(1)}, u32[]{:S(2)}, u32[]{:S(2)}) collective-permute-start(s16[496,128]{1,0:T(8,128)(2,1)} %shard_map.86), channel_id=1, source_target_pairs={{0,6},{1,7},{2,0},{3,1},{4,2},{5,3},{6,4},{7,5},{8,14},{9,15},{10,... | collective-permute-start | bytes 380936 | tf_op jit(solution)/shard_map/ppermute | solution.py:168
  10.6 1.5 %collective-permute-start.5 = (f32[32,1152]{1,0:T(8,128)S(1)}, f32[32,1152]{1,0:T(8,128)S(1)}, u32[]{:S(2)}, u32[]{:S(2)}) collective-permute-start(f32[32,1152]{1,0:T(8,128)S(1)} %pad_maximum_fusion.refs_0_), channel_id=1, source_target_pairs={{0,8},{8,16},{16,24},{24,0},{1,9},{9,17},{17,25},{25,1},{2,10},{10... | collective-permute-start | bytes 442376 | tf_op jit(solution)/shard_map/ppermute | solution.py:168
  12.1 1.5 %collective-permute-start.4 = (f32[32,1152]{1,0:T(8,128)S(1)}, f32[32,1152]{1,0:T(8,128)S(1)}, u32[]{:S(2)}, u32[]{:S(2)}) collective-permute-start(f32[32,1152]{1,0:T(8,128)S(1)} %pad_maximum_fusion.refs_0_), channel_id=1, source_target_pairs={{0,16},{8,24},{16,0},{24,8},{1,17},{9,25},{17,1},{25,9},{2,18},{10... | collective-permute-start | bytes 442376 | tf_op jit(solution)/shard_map/ppermute | solution.py:168
  13.7 3.0 %collective-permute-done.5.refs_3_ = f32[32,1152]{1,0:T(8,128)S(1)} collective-permute-done((f32[32,1152]{1,0:T(8,128)S(1)}, f32[32,1152]{1,0:T(8,128)S(1)}, u32[]{:S(2)}, u32[]{:S(2)}) %collective-permute-start.5) | collective-permute-done | bytes 147488 | tf_op jit(solution)/shard_map/ppermute | solution.py:168
  16.7 1.5 %collective-permute-start.3 = (f32[32,1152]{1,0:T(8,128)S(1)}, f32[32,1152]{1,0:T(8,128)S(1)}, u32[]{:S(2)}, u32[]{:S(2)}) collective-permute-start(f32[32,1152]{1,0:T(8,128)S(1)} %pad_maximum_fusion.refs_0_), channel_id=1, source_target_pairs={{0,24},{8,0},{16,8},{24,16},{1,25},{9,1},{17,9},{25,17},{2,26},{10... | collective-permute-start | bytes 442376 | tf_op jit(solution)/shard_map/ppermute | solution.py:168
  18.4 0.7 %copy-done.4 = s32[4]{0:T(128)S(1)} copy-done((s32[4]{0:T(128)S(1)}, s32[4]{0:T(128)}, u32[]{:S(2)}) %copy-start.4) | copy-done | bytes 40
  19.1 0.2 fusion.8
  19.2 0.2 collective-permute-done.4.refs_2_
  19.4 2.4 %collective-permute-done.3.refs_1_ = f32[32,1152]{1,0:T(8,128)S(1)} collective-permute-done((f32[32,1152]{1,0:T(8,128)S(1)}, f32[32,1152]{1,0:T(8,128)S(1)}, u32[]{:S(2)}, u32[]{:S(2)}) %collective-permute-start.3) | collective-permute-done | bytes 147488 | tf_op jit(solution)/shard_map/ppermute | solution.py:168
  21.8 2.2 %shard_map.87 = (f32[128,128]{1,0:T(8,128)S(1)}, f32[224,128]{1,0:T(8,128)S(1)}, f32[8,128]{1,0:T(8,128)S(1)}) custom-call(s32[1]{0:T(128)} %bitcast.2.turn, f32[32,1152]{1,0:T(8,128)S(1)} %pad_maximum_fusion.refs_0_, f32[32,1152]{1,0:T(8,128)S(1)} %collective-permute-done.3.refs_1_, f32[32,1152]{1,0:T(8,128)S(1)} %collective-permute-done.4.refs_2_, ...), custom_call_target="tpu_custom_call" | custom-call | tf_op jit(solution)/shard_map/pallas_call | solution.py:35
  24.2 0.2 select_reduce_fusion.2
  24.4 1.6 %collective-permute-done.6.far = s16[4,496,128]{2,1,0:T(8,128)(2,1)S(1)} collective-permute-done((s16[4,496,128]{2,1,0:T(8,128)(2,1)S(1)}, s16[4,496,128]{2,1,0:T(8,128)(2,1)S(1)}, u32[]{:S(2)}, u32[]{:S(2)}) %collective-permute-start.6) | collective-permute-done | bytes 507936 | tf_op jit(solution)/shard_map/ppermute | solution.py:213
  26.3 0.1 gt.39
  26.4 0.2 select_reduce_fusion
  26.7 0.1 and_select_fusion
  26.8 0.1 select_n.103.sources
  26.9 3.7 %shard_map.88 = (f32[6,1,32,128]{3,2,1,0:T(8,128)S(1)}, f32[6,1,32,128]{3,2,1,0:T(8,128)S(1)}, f32[6,1,32,128]{3,2,1,0:T(8,128)S(1)}, f32[6,1,32,128]{3,2,1,0:T(8,128)S(1)}) custom-call(s32[72]{0:T(128)S(1)} %select_n.103.sources, s32[4]{0:T(128)S(1)} %compare_select_fusion.give, s16[4,496,128]{2,1,0:T(8,128)(2,1)S(1)} %pad_add_fusion.near, ...), custom_call_target="tpu_custom_call" | custom-call | tf_op jit(solution)/shard_map/pallas_call | solution.py:35
  30.6 2.5 %collective-permute-start.7 = (f32[6,1,32,128]{3,2,1,0:T(8,128)S(1)}, f32[6,1,32,128]{3,2,1,0:T(8,128)S(1)}, u32[]{:S(2)}, u32[]{:S(2)}) collective-permute-start(f32[6,1,32,128]{3,2,1,0:T(8,128)S(1)} %get-tuple-element.51), channel_id=1, source_target_pairs={{0,24},{8,0},{16,8},{24,16},{1,25},{9,1},{17,9},{25,17},{2,26},{10... | collective-permute-start | bytes 294920 | tf_op jit(solution)/shard_map/ppermute | solution.py:168
  33.1 0.5 collective-permute-start.8
  33.6 0.6 %collective-permute-start.9 = (f32[6,1,32,128]{3,2,1,0:T(8,128)S(1)}, f32[6,1,32,128]{3,2,1,0:T(8,128)S(1)}, u32[]{:S(2)}, u32[]{:S(2)}) collective-permute-start(f32[6,1,32,128]{3,2,1,0:T(8,128)S(1)} %get-tuple-element.53), channel_id=1, source_target_pairs={{0,8},{8,16},{16,24},{24,0},{1,9},{9,17},{17,25},{25,1},{2,10},{10... | collective-permute-start | bytes 294920 | tf_op jit(solution)/shard_map/ppermute | solution.py:168
  34.2 0.1 select_reduce_fusion.1.where
  34.3 4.2 %shard_map.89 = (f32[8,192,128]{2,1,0:T(8,128)S(1)}, f32[8,192,128]{2,1,0:T(8,128)S(1)}, f32[1,128]{1,0:T(1,128)S(1)}, f32[1,128,128]{2,1,0:T(8,128)S(1)}) custom-call(s32[8]{0:T(128)S(1)} %select_reduce_fusion.1.where, s32[4]{0:T(128)S(1)} %get-tuple-element.71.held, f32[224,128]{1,0:T(8,128)S(1)} %get-tuple-element.54.powers, f32[8,128,128]{2,1,0:T(8,128)S(1)} %copy-done, ...), custom_call_target="tpu_custom_call" | custom-call | tf_op jit(solution)/shard_map/pallas_call | solution.py:35
  38.5 1.3 %collective-permute-done.8.refs_2_ = f32[6,1,32,128]{3,2,1,0:T(8,128)S(1)} collective-permute-done((f32[6,1,32,128]{3,2,1,0:T(8,128)S(1)}, f32[6,1,32,128]{3,2,1,0:T(8,128)S(1)}, u32[]{:S(2)}, u32[]{:S(2)}) %collective-permute-start.8) | collective-permute-done | bytes 98336 | tf_op jit(solution)/shard_map/ppermute | solution.py:168
  39.8 2.4 %shard_map.90 = (f32[32,1,128]{2,1,0:T(1,128)S(1)}, f32[6,1,32,128]{3,2,1,0:T(8,128)S(1)}, f32[6,1,32,128]{3,2,1,0:T(8,128)S(1)}, f32[6,1,32,128]{3,2,1,0:T(8,128)S(1)}, f32[6,1,32,128]{3,2,1,0:T(8,128)S(1)}) custom-call(s32[4]{0:T(128)S(1)} %get-tuple-element.71.held, s32[4]{0:T(128)S(1)} %get-tuple-element.70.used, ...), custom_call_target="tpu_custom_call" | custom-call | tf_op jit(solution)/shard_map/pallas_call | solution.py:35
  42.2 1.1 %collective-permute-start.10 = (f32[6,1,32,128]{3,2,1,0:T(8,128)S(1)}, f32[6,1,32,128]{3,2,1,0:T(8,128)S(1)}, u32[]{:S(2)}, u32[]{:S(2)}) collective-permute-start(f32[6,1,32,128]{3,2,1,0:T(8,128)S(1)} %get-tuple-element.67), channel_id=1, source_target_pairs={{0,8},{8,16},{16,24},{24,0},{1,9},{9,17},{17,25},{25,1},{2,10},{10... | collective-permute-start | bytes 294920 | tf_op jit(solution)/shard_map/ppermute | solution.py:168
  43.4 0.5 collective-permute-start.11
  43.9 2.2 %collective-permute-start.12 = (f32[6,1,32,128]{3,2,1,0:T(8,128)S(1)}, f32[6,1,32,128]{3,2,1,0:T(8,128)S(1)}, u32[]{:S(2)}, u32[]{:S(2)}) collective-permute-start(f32[6,1,32,128]{3,2,1,0:T(8,128)S(1)} %get-tuple-element.69), channel_id=1, source_target_pairs={{0,24},{8,0},{16,8},{24,16},{1,25},{9,1},{17,9},{25,17},{2,26},{10... | collective-permute-start | bytes 294920 | tf_op jit(solution)/shard_map/ppermute | solution.py:168
  46.0 8.8 %all_to_all.5.grams = f32[32,1,128]{2,1,0:T(1,128)S(1)} all-to-all(f32[32,1,128]{2,1,0:T(1,128)S(1)} %get-tuple-element.62), channel_id=1, replica_groups=mesh['cols'=4,'rows'=8] {'cols','rows'}, dimensions={0} | all-to-all | bytes 32768 | tf_op jit(solution)/shard_map/all_to_all | solution.py:564
  54.9 2.1 %shard_map.91 = (f32[32,1024]{1,0:T(8,128)}, f32[32,1024]{1,0:T(8,128)}) custom-call(s32[4]{0:T(128)S(1)} %get-tuple-element.71.held, s32[8]{0:T(128)S(1)} %select_reduce_fusion.1.where, f32[32,1,128]{2,1,0:T(1,128)S(1)} %all_to_all.5.grams, f32[8,128]{1,0:T(8,128)S(1)} %get-tuple-element.63.scale, f32[32,1024]{1,0:T(8,128)S(1)} %copy-done.1, ...), custom_call_target="tpu_custom_call" | custom-call | tf_op jit(solution)/shard_map/pallas_call | solution.py:35
  (37 shorter events, 0.7 us)
Async XLA Ops:
  1.3 9.3 %copy-start.1 = (f32[32,1024]{1,0:T(8,128)S(1)}, f32[32,1024]{1,0:T(8,128)}, u32[]{:S(2)}) copy-start(f32[32,1024]{1,0:T(8,128)} %gradient.3) | copy-start | bytes 393220
  1.3 9.3 %copy-start.3 = (f32[128,32]{0,1:T(8,128)S(1)}, f32[128,32]{0,1:T(8,128)}, u32[]{:S(2)}) copy-start(f32[128,32]{0,1:T(8,128)} %param.9) | copy-start | bytes 49156
  3.5 20.5 %collective-permute-start.2 = (s16[496,128]{1,0:T(8,128)(2,1)}, s16[496,128]{1,0:T(8,128)(2,1)S(1)}, u32[]{:S(2)}, u32[]{:S(2)}) collective-permute-start(s16[496,128]{1,0:T(8,128)(2,1)} %shard_map.86), channel_id=1, source_target_pairs={{0,2},{1,3},{2,4},{3,5},{4,6},{5,7},{6,0},{7,1},{8,10},{9,11},{10,... | collective-permute-start | bytes 380936 | tf_op jit(solution)/shard_map/ppermute | solution.py:168
  6.6 17.4 %collective-permute-start.1 = (s16[496,128]{1,0:T(8,128)(2,1)}, s16[496,128]{1,0:T(8,128)(2,1)S(1)}, u32[]{:S(2)}, u32[]{:S(2)}) collective-permute-start(s16[496,128]{1,0:T(8,128)(2,1)} %shard_map.86), channel_id=1, source_target_pairs={{0,4},{1,5},{2,6},{3,7},{4,0},{5,1},{6,2},{7,3},{8,12},{9,13},{10,... | collective-permute-start | bytes 380936 | tf_op jit(solution)/shard_map/ppermute | solution.py:168
  9.2 14.8 %collective-permute-start = (s16[496,128]{1,0:T(8,128)(2,1)}, s16[496,128]{1,0:T(8,128)(2,1)S(1)}, u32[]{:S(2)}, u32[]{:S(2)}) collective-permute-start(s16[496,128]{1,0:T(8,128)(2,1)} %shard_map.86), channel_id=1, source_target_pairs={{0,6},{1,7},{2,0},{3,1},{4,2},{5,3},{6,4},{7,5},{8,14},{9,15},{10,... | collective-permute-start | bytes 380936 | tf_op jit(solution)/shard_map/ppermute | solution.py:168
  10.6 6.1 %collective-permute-start.5 = (f32[32,1152]{1,0:T(8,128)S(1)}, f32[32,1152]{1,0:T(8,128)S(1)}, u32[]{:S(2)}, u32[]{:S(2)}) collective-permute-start(f32[32,1152]{1,0:T(8,128)S(1)} %pad_maximum_fusion.refs_0_), channel_id=1, source_target_pairs={{0,8},{8,16},{16,24},{24,0},{1,9},{9,17},{17,25},{25,1},{2,10},{10... | collective-permute-start | bytes 442376 | tf_op jit(solution)/shard_map/ppermute | solution.py:168
  12.1 7.3 %collective-permute-start.4 = (f32[32,1152]{1,0:T(8,128)S(1)}, f32[32,1152]{1,0:T(8,128)S(1)}, u32[]{:S(2)}, u32[]{:S(2)}) collective-permute-start(f32[32,1152]{1,0:T(8,128)S(1)} %pad_maximum_fusion.refs_0_), channel_id=1, source_target_pairs={{0,16},{8,24},{16,0},{24,8},{1,17},{9,25},{17,1},{25,9},{2,18},{10... | collective-permute-start | bytes 442376 | tf_op jit(solution)/shard_map/ppermute | solution.py:168
  16.7 5.1 %collective-permute-start.3 = (f32[32,1152]{1,0:T(8,128)S(1)}, f32[32,1152]{1,0:T(8,128)S(1)}, u32[]{:S(2)}, u32[]{:S(2)}) collective-permute-start(f32[32,1152]{1,0:T(8,128)S(1)} %pad_maximum_fusion.refs_0_), channel_id=1, source_target_pairs={{0,24},{8,0},{16,8},{24,16},{1,25},{9,1},{17,9},{25,17},{2,26},{10... | collective-permute-start | bytes 442376 | tf_op jit(solution)/shard_map/ppermute | solution.py:168
  18.4 0.7 %copy-start.4 = (s32[4]{0:T(128)S(1)}, s32[4]{0:T(128)}, u32[]{:S(2)}) copy-start(s32[4]{0:T(128)} %local.1) | copy-start | bytes 52
  21.8 2.2 %copy-start.2 = (s16[496,128]{1,0:T(8,128)(2,1)S(1)}, s16[496,128]{1,0:T(8,128)(2,1)}, u32[]{:S(2)}) copy-start(s16[496,128]{1,0:T(8,128)(2,1)} %shard_map.86) | copy-start | bytes 380932
  24.1 2.0 %collective-permute-start.6 = (s16[4,496,128]{2,1,0:T(8,128)(2,1)S(1)}, s16[4,496,128]{2,1,0:T(8,128)(2,1)S(1)}, u32[]{:S(2)}, u32[]{:S(2)}) collective-permute-start(s16[4,496,128]{2,1,0:T(8,128)(2,1)S(1)} %pad_add_fusion.near), channel_id=1, source_target_pairs={{0,1},{1,0},{2,3},{3,2},{4,5},{5,4},{6,7},{7,6},{8,9},{9,8},{10,11... | collective-permute-start | bytes 1523720 | tf_op jit(solution)/shard_map/ppermute | solution.py:213
  26.8 7.5 %copy-start = (f32[8,128,128]{2,1,0:T(8,128)S(1)}, f32[8,128,128]{2,1,0:T(8,128)}, u32[]{:S(2)}) copy-start(f32[8,128,128]{2,1,0:T(8,128)} %jacobi.5) | copy-start | bytes 1572868
  30.6 7.9 %collective-permute-start.7 = (f32[6,1,32,128]{3,2,1,0:T(8,128)S(1)}, f32[6,1,32,128]{3,2,1,0:T(8,128)S(1)}, u32[]{:S(2)}, u32[]{:S(2)}) collective-permute-start(f32[6,1,32,128]{3,2,1,0:T(8,128)S(1)} %get-tuple-element.51), channel_id=1, source_target_pairs={{0,24},{8,0},{16,8},{24,16},{1,25},{9,1},{17,9},{25,17},{2,26},{10... | collective-permute-start | bytes 294920 | tf_op jit(solution)/shard_map/ppermute | solution.py:168
  33.1 6.7 %collective-permute-start.8 = (f32[6,1,32,128]{3,2,1,0:T(8,128)S(1)}, f32[6,1,32,128]{3,2,1,0:T(8,128)S(1)}, u32[]{:S(2)}, u32[]{:S(2)}) collective-permute-start(f32[6,1,32,128]{3,2,1,0:T(8,128)S(1)} %get-tuple-element.52), channel_id=1, source_target_pairs={{0,16},{8,24},{16,0},{24,8},{1,17},{9,25},{17,1},{25,9},{2,18},{10... | collective-permute-start | bytes 294920 | tf_op jit(solution)/shard_map/ppermute | solution.py:168
  33.6 6.2 %collective-permute-start.9 = (f32[6,1,32,128]{3,2,1,0:T(8,128)S(1)}, f32[6,1,32,128]{3,2,1,0:T(8,128)S(1)}, u32[]{:S(2)}, u32[]{:S(2)}) collective-permute-start(f32[6,1,32,128]{3,2,1,0:T(8,128)S(1)} %get-tuple-element.53), channel_id=1, source_target_pairs={{0,8},{8,16},{16,24},{24,0},{1,9},{9,17},{17,25},{25,1},{2,10},{10... | collective-permute-start | bytes 294920 | tf_op jit(solution)/shard_map/ppermute | solution.py:168
  42.2 12.6 %collective-permute-start.10 = (f32[6,1,32,128]{3,2,1,0:T(8,128)S(1)}, f32[6,1,32,128]{3,2,1,0:T(8,128)S(1)}, u32[]{:S(2)}, u32[]{:S(2)}) collective-permute-start(f32[6,1,32,128]{3,2,1,0:T(8,128)S(1)} %get-tuple-element.67), channel_id=1, source_target_pairs={{0,8},{8,16},{16,24},{24,0},{1,9},{9,17},{17,25},{25,1},{2,10},{10... | collective-permute-start | bytes 294920 | tf_op jit(solution)/shard_map/ppermute | solution.py:168
  43.4 11.5 %collective-permute-start.11 = (f32[6,1,32,128]{3,2,1,0:T(8,128)S(1)}, f32[6,1,32,128]{3,2,1,0:T(8,128)S(1)}, u32[]{:S(2)}, u32[]{:S(2)}) collective-permute-start(f32[6,1,32,128]{3,2,1,0:T(8,128)S(1)} %get-tuple-element.68), channel_id=1, source_target_pairs={{0,16},{8,24},{16,0},{24,8},{1,17},{9,25},{17,1},{25,9},{2,18},{10... | collective-permute-start | bytes 294920 | tf_op jit(solution)/shard_map/ppermute | solution.py:168
  43.9 11.0 %collective-permute-start.12 = (f32[6,1,32,128]{3,2,1,0:T(8,128)S(1)}, f32[6,1,32,128]{3,2,1,0:T(8,128)S(1)}, u32[]{:S(2)}, u32[]{:S(2)}) collective-permute-start(f32[6,1,32,128]{3,2,1,0:T(8,128)S(1)} %get-tuple-element.69), channel_id=1, source_target_pairs={{0,24},{8,0},{16,8},{24,16},{1,25},{9,1},{17,9},{25,17},{2,26},{10... | collective-permute-start | bytes 294920 | tf_op jit(solution)/shard_map/ppermute | solution.py:168

commit v6 on v5

--- a/solution.py
+++ b/solution.py
@@ -207,10 +207,10 @@
     near = [packed] + [shift(packed, "rows", 2 * o) for o in range(1, groups)]
     gradient, factor, _ = lax.optimization_barrier((gradient, factor, packed))
     pieces = whole_pieces(gradient, factor)
-    powers = make_powers(pieces)
-    near, pieces, powers = lax.optimization_barrier((near, pieces, powers))
     near = jnp.stack(near)
     far = lax.ppermute(near, "rows", [(i, i ^ 1) for i in range(devices)])
+    powers = make_powers(pieces)
+    far, pieces, powers = lax.optimization_barrier((far, pieces, powers))
 
     me = lax.axis_index("rows")
     position = jnp.arange(devices, dtype=jnp.int32)
@@ -316,7 +316,7 @@
     norm = jnp.max(jnp.sum(jnp.abs(factor), axis=1, keepdims=True), axis=0, keepdims=True)
     power = factor / norm
     for _ in range(3):
-        power = dot(power, power)
+        power = dot3(power, power)
     bound = jnp.sum(jnp.sum(power * power, axis=1, keepdims=True), axis=0, keepdims=True)
     for _ in range(4):
         bound = jnp.sqrt(bound)
@@ -344,8 +344,8 @@
     for b in range(jacobi.shape[0]):
         columns = slice(b * BLOCK, (b + 1) * BLOCK)
         whole = jnp.concatenate([piece[:, columns] for piece in pieces], 0)
-        s = dot(powers[...], whole)
-        y = dot(s[: ITERS * width], jacobi[b])
+        s = dot3(powers[...], whole)
+        y = dot3(s[: ITERS * width], jacobi[b])
         plain[b] = s[width:]
         smooth[b] = y
         weight = jnp.where(where[b] < NOWHERE, 0.0, 1.0)

time: 57.2 us -> 57.5 us (level)
  blocking collectives: 8.85 us -> 13.7 us
  waiting for transfers between devices: 8.58 us -> 5.68 us
  Pallas kernels: 16.7 us -> 15.3 us
  local copies, waits for them, and re-layouts: 1.19 us -> 0.53 us
    all_to_all x1, blocking collectives: 8.85 us -> 13.7 us  [on_device(): grams = lax.all_to_all(gram, ('cols', 'rows'), 0, 0, tiled=True)]
    ppermute x1, waiting for transfers between devices: 1.64 us -> 0.01 us  [chain_gathered(): far = lax.ppermute(near, 'rows', [(i, i ^ 1) for i in range(devices)])]
    pallas_call x6, Pallas kernels: 16.7 us -> 15.3 us  [call(): pl.pallas_call(kernel, out_shape=outs, in_specs=specs, out_specs=tuple([V...]
    ppermute x12, waiting for transfers between devices: 6.93 us -> 5.67 us  [shift(): return lax.ppermute(x, axis, [(i, (i - by) % size) for i in range(size)])]
    unnamed x12, local copies, waits for them, and re-layouts: 0.69 us -> 0.03 us
  transfers between devices with their start and end apart: 13 -> 13, of which waited for: 5 -> 5; matrix products, arithmetic and copies ran while one was open for 1% -> 1% of each run, Pallas kernels for 11% -> 9%
where the time goes in v6:
time: 57.5 us; the launch traced here: 57.4 us
  starting transfers between devices  19.6 us (34%)
  Pallas kernels  15.3 us (27%)
  blocking collectives  13.7 us (24%)
  waiting for transfers between devices  5.68 us (10%)
  between operations  1.48 us (3%)
  other arithmetic  1.03 us (2%)
    ppermute x12, starting transfers between devices, shift(): return lax.ppermute(x, axis, [(i, (i - by) % size) for i in range(size)])  19.6 us
    pallas_call x6, Pallas kernels, call(): pl.pallas_call(kernel, out_shape=outs, in_specs=specs, out_specs=tuple([V...  15.3 us
    all_to_all x1, blocking collectives, on_device(): grams = lax.all_to_all(gram, ('cols', 'rows'), 0, 0, tiled=True)  13.7 us
    ppermute x12, waiting for transfers between devices, shift(): return lax.ppermute(x, axis, [(i, (i - by) % size) for i in range(size)])  5.67 us
  transfers between devices with their start and end apart: 13, of which 5 were waited for; matrix products, arithmetic and copies ran while one was open for 1% of the time, Pallas kernels for 9%

profile of v6, /device:TPU:0, one launch (start us, length us, event | category | flops | bytes accessed | tf_op | source)
XLA Modules:
  0.0 57.4 jit_solution(14478077502803393650)
XLA Ops:
  1.3 2.2 %shard_map.86 = s16[496,128]{1,0:T(8,128)(2,1)} custom-call(s32[4]{0:T(128)} %local.1, s32[4]{0:T(128)} %remote.1, s32[1]{0:T(128)} %copy.17.count, f32[32,1024]{1,0:T(8,128)} %gradient.3, f32[8,128,128]{2,1,0:T(8,128)} %jacobi.5, bf16[4,128,128]{2,1,0:T(8,128)(2,1)} %tiles.1), custom_call_target="tpu_custom_call" | custom-call | tf_op jit(solution)/shard_map/pallas_call | solution.py:35
  3.5 3.1 %collective-permute-start.2 = (s16[496,128]{1,0:T(8,128)(2,1)}, s16[496,128]{1,0:T(8,128)(2,1)S(1)}, u32[]{:S(2)}, u32[]{:S(2)}) collective-permute-start(s16[496,128]{1,0:T(8,128)(2,1)} %shard_map.86), channel_id=1, source_target_pairs={{0,2},{1,3},{2,4},{3,5},{4,6},{5,7},{6,0},{7,1},{8,10},{9,11},{10,... | collective-permute-start | bytes 380936 | tf_op jit(solution)/shard_map/ppermute | solution.py:168
  6.6 2.6 %collective-permute-start.1 = (s16[496,128]{1,0:T(8,128)(2,1)}, s16[496,128]{1,0:T(8,128)(2,1)S(1)}, u32[]{:S(2)}, u32[]{:S(2)}) collective-permute-start(s16[496,128]{1,0:T(8,128)(2,1)} %shard_map.86), channel_id=1, source_target_pairs={{0,4},{1,5},{2,6},{3,7},{4,0},{5,1},{6,2},{7,3},{8,12},{9,13},{10,... | collective-permute-start | bytes 380936 | tf_op jit(solution)/shard_map/ppermute | solution.py:168
  9.2 1.3 %collective-permute-start = (s16[496,128]{1,0:T(8,128)(2,1)}, s16[496,128]{1,0:T(8,128)(2,1)S(1)}, u32[]{:S(2)}, u32[]{:S(2)}) collective-permute-start(s16[496,128]{1,0:T(8,128)(2,1)} %shard_map.86), channel_id=1, source_target_pairs={{0,6},{1,7},{2,0},{3,1},{4,2},{5,3},{6,4},{7,5},{8,14},{9,15},{10,... | collective-permute-start | bytes 380936 | tf_op jit(solution)/shard_map/ppermute | solution.py:168
  10.6 1.5 %collective-permute-start.6 = (f32[32,1152]{1,0:T(8,128)S(1)}, f32[32,1152]{1,0:T(8,128)S(1)}, u32[]{:S(2)}, u32[]{:S(2)}) collective-permute-start(f32[32,1152]{1,0:T(8,128)S(1)} %pad_maximum_fusion.refs_0_), channel_id=1, source_target_pairs={{0,8},{8,16},{16,24},{24,0},{1,9},{9,17},{17,25},{25,1},{2,10},{10... | collective-permute-start | bytes 442376 | tf_op jit(solution)/shard_map/ppermute | solution.py:168
  12.1 1.5 %collective-permute-start.5 = (f32[32,1152]{1,0:T(8,128)S(1)}, f32[32,1152]{1,0:T(8,128)S(1)}, u32[]{:S(2)}, u32[]{:S(2)}) collective-permute-start(f32[32,1152]{1,0:T(8,128)S(1)} %pad_maximum_fusion.refs_0_), channel_id=1, source_target_pairs={{0,16},{8,24},{16,0},{24,8},{1,17},{9,25},{17,1},{25,9},{2,18},{10... | collective-permute-start | bytes 442376 | tf_op jit(solution)/shard_map/ppermute | solution.py:168
  13.7 0.2 fusion.8
  13.9 2.0 %collective-permute-start.4 = (f32[32,1152]{1,0:T(8,128)S(1)}, f32[32,1152]{1,0:T(8,128)S(1)}, u32[]{:S(2)}, u32[]{:S(2)}) collective-permute-start(f32[32,1152]{1,0:T(8,128)S(1)} %pad_maximum_fusion.refs_0_), channel_id=1, source_target_pairs={{0,24},{8,0},{16,8},{24,16},{1,25},{9,1},{17,9},{25,17},{2,26},{10... | collective-permute-start | bytes 442376 | tf_op jit(solution)/shard_map/ppermute | solution.py:168
  15.9 1.9 %collective-permute-done.1 = s16[496,128]{1,0:T(8,128)(2,1)S(1)} collective-permute-done((s16[496,128]{1,0:T(8,128)(2,1)}, s16[496,128]{1,0:T(8,128)(2,1)S(1)}, u32[]{:S(2)}, u32[]{:S(2)}) %collective-permute-start.1) | collective-permute-done | bytes 127008 | tf_op jit(solution)/shard_map/ppermute | solution.py:168
  17.9 0.2 select_reduce_fusion.2
  18.2 0.1 eq.106
  18.4 1.1 %collective-permute-done.5.refs_2_ = f32[32,1152]{1,0:T(8,128)S(1)} collective-permute-done((f32[32,1152]{1,0:T(8,128)S(1)}, f32[32,1152]{1,0:T(8,128)S(1)}, u32[]{:S(2)}, u32[]{:S(2)}) %collective-permute-start.5) | collective-permute-done | bytes 147488 | tf_op jit(solution)/shard_map/ppermute | solution.py:168
  19.5 0.3 collective-permute-done.4.refs_1_
  19.7 2.0 %shard_map.87 = (f32[128,128]{1,0:T(8,128)S(1)}, f32[224,128]{1,0:T(8,128)S(1)}, f32[8,128]{1,0:T(8,128)S(1)}) custom-call(s32[1]{0:T(128)} %bitcast.6.turn, f32[32,1152]{1,0:T(8,128)S(1)} %pad_maximum_fusion.refs_0_, f32[32,1152]{1,0:T(8,128)S(1)} %collective-permute-done.4.refs_1_, f32[32,1152]{1,0:T(8,128)S(1)} %collective-permute-done.5.refs_2_, ...), custom_call_target="tpu_custom_call" | custom-call | tf_op jit(solution)/shard_map/pallas_call | solution.py:35
  22.0 0.1 gt.39
  22.1 0.2 select_reduce_fusion
  22.4 0.1 and_select_fusion
  22.5 0.1 select_n.103.sources
  22.6 3.7 %shard_map.88 = (f32[6,1,32,128]{3,2,1,0:T(8,128)S(1)}, f32[6,1,32,128]{3,2,1,0:T(8,128)S(1)}, f32[6,1,32,128]{3,2,1,0:T(8,128)S(1)}, f32[6,1,32,128]{3,2,1,0:T(8,128)S(1)}) custom-call(s32[72]{0:T(128)S(1)} %select_n.103.sources, s32[4]{0:T(128)S(1)} %compare_select_fusion.give, s16[4,496,128]{2,1,0:T(8,128)(2,1)S(1)} %pad_add_fusion.near, ...), custom_call_target="tpu_custom_call" | custom-call | tf_op jit(solution)/shard_map/pallas_call | solution.py:35
  26.3 2.3 %collective-permute-start.7 = (f32[6,1,32,128]{3,2,1,0:T(8,128)S(1)}, f32[6,1,32,128]{3,2,1,0:T(8,128)S(1)}, u32[]{:S(2)}, u32[]{:S(2)}) collective-permute-start(f32[6,1,32,128]{3,2,1,0:T(8,128)S(1)} %get-tuple-element.45), channel_id=1, source_target_pairs={{0,24},{8,0},{16,8},{24,16},{1,25},{9,1},{17,9},{25,17},{2,26},{10... | collective-permute-start | bytes 294920 | tf_op jit(solution)/shard_map/ppermute | solution.py:168
  28.6 0.9 %collective-permute-start.8 = (f32[6,1,32,128]{3,2,1,0:T(8,128)S(1)}, f32[6,1,32,128]{3,2,1,0:T(8,128)S(1)}, u32[]{:S(2)}, u32[]{:S(2)}) collective-permute-start(f32[6,1,32,128]{3,2,1,0:T(8,128)S(1)} %get-tuple-element.46), channel_id=1, source_target_pairs={{0,16},{8,24},{16,0},{24,8},{1,17},{9,25},{17,1},{25,9},{2,18},{10... | collective-permute-start | bytes 294920 | tf_op jit(solution)/shard_map/ppermute | solution.py:168
  29.5 0.2 collective-permute-start.9
  29.7 0.1 select_reduce_fusion.1.where
  29.8 2.8 %shard_map.89 = (f32[8,192,128]{2,1,0:T(8,128)S(1)}, f32[8,192,128]{2,1,0:T(8,128)S(1)}, f32[1,128]{1,0:T(1,128)S(1)}, f32[1,128,128]{2,1,0:T(8,128)S(1)}) custom-call(s32[8]{0:T(128)S(1)} %select_reduce_fusion.1.where, s32[4]{0:T(128)S(1)} %get-tuple-element.65.held, f32[224,128]{1,0:T(8,128)S(1)} %get-tuple-element.48.powers, f32[8,128,128]{2,1,0:T(8,128)S(1)} %copy-done, ...), custom_call_target="tpu_custom_call" | custom-call | tf_op jit(solution)/shard_map/pallas_call | solution.py:35
  32.6 1.2 %collective-permute-done.8.refs_2_ = f32[6,1,32,128]{3,2,1,0:T(8,128)S(1)} collective-permute-done((f32[6,1,32,128]{3,2,1,0:T(8,128)S(1)}, f32[6,1,32,128]{3,2,1,0:T(8,128)S(1)}, u32[]{:S(2)}, u32[]{:S(2)}) %collective-permute-start.8) | collective-permute-done | bytes 98336 | tf_op jit(solution)/shard_map/ppermute | solution.py:168
  33.8 1.2 %collective-permute-done.9.refs_3_ = f32[6,1,32,128]{3,2,1,0:T(8,128)S(1)} collective-permute-done((f32[6,1,32,128]{3,2,1,0:T(8,128)S(1)}, f32[6,1,32,128]{3,2,1,0:T(8,128)S(1)}, u32[]{:S(2)}, u32[]{:S(2)}) %collective-permute-start.9) | collective-permute-done | bytes 98336 | tf_op jit(solution)/shard_map/ppermute | solution.py:168
  35.0 2.4 %shard_map.90 = (f32[32,1,128]{2,1,0:T(1,128)S(1)}, f32[6,1,32,128]{3,2,1,0:T(8,128)S(1)}, f32[6,1,32,128]{3,2,1,0:T(8,128)S(1)}, f32[6,1,32,128]{3,2,1,0:T(8,128)S(1)}, f32[6,1,32,128]{3,2,1,0:T(8,128)S(1)}) custom-call(s32[4]{0:T(128)S(1)} %get-tuple-element.65.held, s32[4]{0:T(128)S(1)} %get-tuple-element.64.used, ...), custom_call_target="tpu_custom_call" | custom-call | tf_op jit(solution)/shard_map/pallas_call | solution.py:35
  37.4 0.1 collective-permute-start.10
  37.5 1.2 %collective-permute-start.11 = (f32[6,1,32,128]{3,2,1,0:T(8,128)S(1)}, f32[6,1,32,128]{3,2,1,0:T(8,128)S(1)}, u32[]{:S(2)}, u32[]{:S(2)}) collective-permute-start(f32[6,1,32,128]{3,2,1,0:T(8,128)S(1)} %get-tuple-element.62), channel_id=1, source_target_pairs={{0,16},{8,24},{16,0},{24,8},{1,17},{9,25},{17,1},{25,9},{2,18},{10... | collective-permute-start | bytes 294920 | tf_op jit(solution)/shard_map/ppermute | solution.py:168
  38.7 2.8 %collective-permute-start.12 = (f32[6,1,32,128]{3,2,1,0:T(8,128)S(1)}, f32[6,1,32,128]{3,2,1,0:T(8,128)S(1)}, u32[]{:S(2)}, u32[]{:S(2)}) collective-permute-start(f32[6,1,32,128]{3,2,1,0:T(8,128)S(1)} %get-tuple-element.63), channel_id=1, source_target_pairs={{0,24},{8,0},{16,8},{24,16},{1,25},{9,1},{17,9},{25,17},{2,26},{10... | collective-permute-start | bytes 294920 | tf_op jit(solution)/shard_map/ppermute | solution.py:168
  41.5 13.7 %all_to_all.5.grams = f32[32,1,128]{2,1,0:T(1,128)S(1)} all-to-all(f32[32,1,128]{2,1,0:T(1,128)S(1)} %get-tuple-element.56), channel_id=1, replica_groups=mesh['cols'=4,'rows'=8] {'cols','rows'}, dimensions={0} | all-to-all | bytes 32768 | tf_op jit(solution)/shard_map/all_to_all | solution.py:564
  55.3 2.1 %shard_map.91 = (f32[32,1024]{1,0:T(8,128)}, f32[32,1024]{1,0:T(8,128)}) custom-call(s32[4]{0:T(128)S(1)} %get-tuple-element.65.held, s32[8]{0:T(128)S(1)} %select_reduce_fusion.1.where, f32[32,1,128]{2,1,0:T(1,128)S(1)} %all_to_all.5.grams, f32[8,128]{1,0:T(8,128)S(1)} %get-tuple-element.57.scale, f32[32,1024]{1,0:T(8,128)S(1)} %copy-done.1, ...), custom_call_target="tpu_custom_call" | custom-call | tf_op jit(solution)/shard_map/pallas_call | solution.py:35
  (37 shorter events, 0.7 us)
Async XLA Ops:
  1.3 9.3 %copy-start.1 = (f32[32,1024]{1,0:T(8,128)S(1)}, f32[32,1024]{1,0:T(8,128)}, u32[]{:S(2)}) copy-start(f32[32,1024]{1,0:T(8,128)} %gradient.3) | copy-start | bytes 393220
  1.3 9.3 %copy-start.3 = (f32[128,32]{0,1:T(8,128)S(1)}, f32[128,32]{0,1:T(8,128)}, u32[]{:S(2)}) copy-start(f32[128,32]{0,1:T(8,128)} %param.9) | copy-start | bytes 49156
  3.5 10.4 %collective-permute-start.2 = (s16[496,128]{1,0:T(8,128)(2,1)}, s16[496,128]{1,0:T(8,128)(2,1)S(1)}, u32[]{:S(2)}, u32[]{:S(2)}) collective-permute-start(s16[496,128]{1,0:T(8,128)(2,1)} %shard_map.86), channel_id=1, source_target_pairs={{0,2},{1,3},{2,4},{3,5},{4,6},{5,7},{6,0},{7,1},{8,10},{9,11},{10,... | collective-permute-start | bytes 380936 | tf_op jit(solution)/shard_map/ppermute | solution.py:168
  6.6 11.2 %collective-permute-start.1 = (s16[496,128]{1,0:T(8,128)(2,1)}, s16[496,128]{1,0:T(8,128)(2,1)S(1)}, u32[]{:S(2)}, u32[]{:S(2)}) collective-permute-start(s16[496,128]{1,0:T(8,128)(2,1)} %shard_map.86), channel_id=1, source_target_pairs={{0,4},{1,5},{2,6},{3,7},{4,0},{5,1},{6,2},{7,3},{8,12},{9,13},{10,... | collective-permute-start | bytes 380936 | tf_op jit(solution)/shard_map/ppermute | solution.py:168
  9.2 8.6 %collective-permute-start = (s16[496,128]{1,0:T(8,128)(2,1)}, s16[496,128]{1,0:T(8,128)(2,1)S(1)}, u32[]{:S(2)}, u32[]{:S(2)}) collective-permute-start(s16[496,128]{1,0:T(8,128)(2,1)} %shard_map.86), channel_id=1, source_target_pairs={{0,6},{1,7},{2,0},{3,1},{4,2},{5,3},{6,4},{7,5},{8,14},{9,15},{10,... | collective-permute-start | bytes 380936 | tf_op jit(solution)/shard_map/ppermute | solution.py:168
  10.6 7.2 %copy-start.2 = (s16[496,128]{1,0:T(8,128)(2,1)S(1)}, s16[496,128]{1,0:T(8,128)(2,1)}, u32[]{:S(2)}) copy-start(s16[496,128]{1,0:T(8,128)(2,1)} %shard_map.86) | copy-start | bytes 380932
  10.6 3.1 %copy-start.4 = (s32[4]{0:T(128)S(1)}, s32[4]{0:T(128)}, u32[]{:S(2)}) copy-start(s32[4]{0:T(128)} %local.1) | copy-start | bytes 52
  10.6 7.8 %collective-permute-start.6 = (f32[32,1152]{1,0:T(8,128)S(1)}, f32[32,1152]{1,0:T(8,128)S(1)}, u32[]{:S(2)}, u32[]{:S(2)}) collective-permute-start(f32[32,1152]{1,0:T(8,128)S(1)} %pad_maximum_fusion.refs_0_), channel_id=1, source_target_pairs={{0,8},{8,16},{16,24},{24,0},{1,9},{9,17},{17,25},{25,1},{2,10},{10... | collective-permute-start | bytes 442376 | tf_op jit(solution)/shard_map/ppermute | solution.py:168
  12.1 7.3 %collective-permute-start.5 = (f32[32,1152]{1,0:T(8,128)S(1)}, f32[32,1152]{1,0:T(8,128)S(1)}, u32[]{:S(2)}, u32[]{:S(2)}) collective-permute-start(f32[32,1152]{1,0:T(8,128)S(1)} %pad_maximum_fusion.refs_0_), channel_id=1, source_target_pairs={{0,16},{8,24},{16,0},{24,8},{1,17},{9,25},{17,1},{25,9},{2,18},{10... | collective-permute-start | bytes 442376 | tf_op jit(solution)/shard_map/ppermute | solution.py:168
  13.9 5.8 %collective-permute-start.4 = (f32[32,1152]{1,0:T(8,128)S(1)}, f32[32,1152]{1,0:T(8,128)S(1)}, u32[]{:S(2)}, u32[]{:S(2)}) collective-permute-start(f32[32,1152]{1,0:T(8,128)S(1)} %pad_maximum_fusion.refs_0_), channel_id=1, source_target_pairs={{0,24},{8,0},{16,8},{24,16},{1,25},{9,1},{17,9},{25,17},{2,26},{10... | collective-permute-start | bytes 442376 | tf_op jit(solution)/shard_map/ppermute | solution.py:168
  17.9 3.9 %collective-permute-start.3 = (s16[4,496,128]{2,1,0:T(8,128)(2,1)S(1)}, s16[4,496,128]{2,1,0:T(8,128)(2,1)S(1)}, u32[]{:S(2)}, u32[]{:S(2)}) collective-permute-start(s16[4,496,128]{2,1,0:T(8,128)(2,1)S(1)} %pad_add_fusion.near), channel_id=1, source_target_pairs={{0,1},{1,0},{2,3},{3,2},{4,5},{5,4},{6,7},{7,6},{8,9},{9,8},{10,11... | collective-permute-start | bytes 1523720 | tf_op jit(solution)/shard_map/ppermute | solution.py:211
  22.5 7.2 %copy-start = (f32[8,128,128]{2,1,0:T(8,128)S(1)}, f32[8,128,128]{2,1,0:T(8,128)}, u32[]{:S(2)}) copy-start(f32[8,128,128]{2,1,0:T(8,128)} %jacobi.5) | copy-start | bytes 1572868
  26.3 6.3 %collective-permute-start.7 = (f32[6,1,32,128]{3,2,1,0:T(8,128)S(1)}, f32[6,1,32,128]{3,2,1,0:T(8,128)S(1)}, u32[]{:S(2)}, u32[]{:S(2)}) collective-permute-start(f32[6,1,32,128]{3,2,1,0:T(8,128)S(1)} %get-tuple-element.45), channel_id=1, source_target_pairs={{0,24},{8,0},{16,8},{24,16},{1,25},{9,1},{17,9},{25,17},{2,26},{10... | collective-permute-start | bytes 294920 | tf_op jit(solution)/shard_map/ppermute | solution.py:168
  28.6 5.2 %collective-permute-start.8 = (f32[6,1,32,128]{3,2,1,0:T(8,128)S(1)}, f32[6,1,32,128]{3,2,1,0:T(8,128)S(1)}, u32[]{:S(2)}, u32[]{:S(2)}) collective-permute-start(f32[6,1,32,128]{3,2,1,0:T(8,128)S(1)} %get-tuple-element.46), channel_id=1, source_target_pairs={{0,16},{8,24},{16,0},{24,8},{1,17},{9,25},{17,1},{25,9},{2,18},{10... | collective-permute-start | bytes 294920 | tf_op jit(solution)/shard_map/ppermute | solution.py:168
  29.5 5.5 %collective-permute-start.9 = (f32[6,1,32,128]{3,2,1,0:T(8,128)S(1)}, f32[6,1,32,128]{3,2,1,0:T(8,128)S(1)}, u32[]{:S(2)}, u32[]{:S(2)}) collective-permute-start(f32[6,1,32,128]{3,2,1,0:T(8,128)S(1)} %get-tuple-element.47), channel_id=1, source_target_pairs={{0,8},{8,16},{16,24},{24,0},{1,9},{9,17},{17,25},{25,1},{2,10},{10... | collective-permute-start | bytes 294920 | tf_op jit(solution)/shard_map/ppermute | solution.py:168
  37.4 17.8 %collective-permute-start.10 = (f32[6,1,32,128]{3,2,1,0:T(8,128)S(1)}, f32[6,1,32,128]{3,2,1,0:T(8,128)S(1)}, u32[]{:S(2)}, u32[]{:S(2)}) collective-permute-start(f32[6,1,32,128]{3,2,1,0:T(8,128)S(1)} %get-tuple-element.61), channel_id=1, source_target_pairs={{0,8},{8,16},{16,24},{24,0},{1,9},{9,17},{17,25},{25,1},{2,10},{10... | collective-permute-start | bytes 294920 | tf_op jit(solution)/shard_map/ppermute | solution.py:168
  37.5 17.7 %collective-permute-start.11 = (f32[6,1,32,128]{3,2,1,0:T(8,128)S(1)}, f32[6,1,32,128]{3,2,1,0:T(8,128)S(1)}, u32[]{:S(2)}, u32[]{:S(2)}) collective-permute-start(f32[6,1,32,128]{3,2,1,0:T(8,128)S(1)} %get-tuple-element.62), channel_id=1, source_target_pairs={{0,16},{8,24},{16,0},{24,8},{1,17},{9,25},{17,1},{25,9},{2,18},{10... | collective-permute-start | bytes 294920 | tf_op jit(solution)/shard_map/ppermute | solution.py:168
  38.7 16.6 %collective-permute-start.12 = (f32[6,1,32,128]{3,2,1,0:T(8,128)S(1)}, f32[6,1,32,128]{3,2,1,0:T(8,128)S(1)}, u32[]{:S(2)}, u32[]{:S(2)}) collective-permute-start(f32[6,1,32,128]{3,2,1,0:T(8,128)S(1)} %get-tuple-element.63), channel_id=1, source_target_pairs={{0,24},{8,0},{16,8},{24,16},{1,25},{9,1},{17,9},{25,17},{2,26},{10... | collective-permute-start | bytes 294920 | tf_op jit(solution)/shard_map/ppermute | solution.py:168

commit v7 on v6

--- a/solution.py
+++ b/solution.py
@@ -168,10 +168,9 @@
     return lax.ppermute(x, axis, [(i, (i - by) % size) for i in range(size)])
 
 
-def whole_pieces(gradient, factor):
-    piece = jnp.concatenate([gradient, factor.T], axis=1)
+def whole_pieces(x):
     others = range(1, lax.axis_size("cols"))
-    return [piece] + [shift(piece, "cols", o) for o in others]
+    return [x] + [shift(x, "cols", o) for o in others]
 
 
 def chain_gathered(
@@ -206,17 +205,21 @@
     )
     near = [packed] + [shift(packed, "rows", 2 * o) for o in range(1, groups)]
     gradient, factor, _ = lax.optimization_barrier((gradient, factor, packed))
-    pieces = whole_pieces(gradient, factor)
+    factors = whole_pieces(factor.T)
+    pieces = whole_pieces(gradient)
+    powers = make_powers(factors)
+    near, powers = lax.optimization_barrier((near, powers))
     near = jnp.stack(near)
-    far = lax.ppermute(near, "rows", [(i, i ^ 1) for i in range(devices)])
-    powers = make_powers(pieces)
-    far, pieces, powers = lax.optimization_barrier((far, pieces, powers))
+    swap = [(i, i ^ 1) for i in range(devices)]
+    noted = near[:, slots * height :, :]
+    told = lax.ppermute(noted, "rows", swap)
+    far = lax.ppermute(near, "rows", swap)
+    told = jnp.concatenate([noted[:, 0], told[:, 0]], 0)
 
     me = lax.axis_index("rows")
     position = jnp.arange(devices, dtype=jnp.int32)
     base = me ^ (position // groups)
     device = (base + 2 * (position % groups)) % devices
-    told = jnp.concatenate([x[:, slots * height, :] for x in (near, far)], 0)
     locals_, remotes, lives = (
         told[:, i * slots : (i + 1) * slots].astype(jnp.int32) for i in range(3)
     )
@@ -311,7 +314,7 @@
 def powers_kernel(turn, *refs):
     pieces, (scaled, powers, scale) = refs[:-3], refs[-3:]
     width = pieces[0].shape[0]
-    factor = jnp.concatenate([piece[:, -BLOCK:] for piece in pieces], 0)
+    factor = jnp.concatenate([piece[...] for piece in pieces], 0)
     factor = pltpu.roll(factor, turn[0], 1)
     norm = jnp.max(jnp.sum(jnp.abs(factor), axis=1, keepdims=True), axis=0, keepdims=True)
     power = factor / norm
@@ -522,8 +525,8 @@
         sends = chain_exchanged(
             gradient, jacobi_inverse, coupling_tiles[:slots], order, *lists
         )
-        pieces = whole_pieces(gradient, width_factor)
-        powers = make_powers(pieces)
+        pieces = whole_pieces(gradient)
+        powers = make_powers(whole_pieces(width_factor.T))
     scaled, powers, scale = powers
     powers, sends = lax.optimization_barrier((powers, sends))
     parts = [sends[0]]

time: 57.5 us -> 55.5 us (0.965)
  blocking collectives: 13.7 us -> 10.1 us
  starting transfers between devices: 19.6 us -> 22.9 us
  waiting for transfers between devices: 5.68 us -> 4 us
    all_to_all x1, blocking collectives: 13.7 us -> 10.1 us  [on_device(): grams = lax.all_to_all(gram, ('cols', 'rows'), 0, 0, tiled=True)]
    ppermute x12 -> x15, starting transfers between devices: 19.6 us -> 22.2 us  [shift(): return lax.ppermute(x, axis, [(i, (i - by) % size) for i in range(size)])]
    ppermute x12 -> x15, waiting for transfers between devices: 5.67 us -> 3.34 us  [shift(): return lax.ppermute(x, axis, [(i, (i - by) % size) for i in range(size)])]
    ppermute x1 -> x2, waiting for transfers between devices: 0.01 us -> 0.67 us  [the longest x1 0.43 us: chain_gathered(): told = lax.ppermute(noted, 'rows', swap)]
  transfers between devices with their start and end apart: 13 -> 17, of which waited for: 5 -> 4; matrix products, arithmetic and copies ran while one was open for 1% -> 3% of each run, Pallas kernels for 9% -> 15%
where the time goes in v7:
time: 55.5 us; the launch traced here: 55.3 us
  starting transfers between devices  22.9 us (41%)
  Pallas kernels  15.3 us (28%)
  blocking collectives  10.1 us (18%)
  waiting for transfers between devices  4 us (7%)
  between operations  1.5 us (3%)
  other arithmetic  1.03 us (2%)
    ppermute x15, starting transfers between devices, shift(): return lax.ppermute(x, axis, [(i, (i - by) % size) for i in range(size)])  22.2 us
    pallas_call x6, Pallas kernels, call(): pl.pallas_call(kernel, out_shape=outs, in_specs=specs, out_specs=tuple([V...  15.3 us
    all_to_all x1, blocking collectives, on_device(): grams = lax.all_to_all(gram, ('cols', 'rows'), 0, 0, tiled=True)  10.1 us
    ppermute x15, waiting for transfers between devices, shift(): return lax.ppermute(x, axis, [(i, (i - by) % size) for i in range(size)])  3.34 us
  transfers between devices with their start and end apart: 17, of which 4 were waited for; matrix products, arithmetic and copies ran while one was open for 3% of the time, Pallas kernels for 15%

profile of v7, /device:TPU:0, one launch (start us, length us, event | category | flops | bytes accessed | tf_op | source)
XLA Modules:
  0.0 55.3 jit_solution(11411644609153354514)
XLA Ops:
  1.3 2.2 %shard_map.86 = s16[496,128]{1,0:T(8,128)(2,1)} custom-call(s32[4]{0:T(128)} %local.1, s32[4]{0:T(128)} %remote.1, s32[1]{0:T(128)} %copy.16.count, f32[32,1024]{1,0:T(8,128)} %gradient.3, f32[8,128,128]{2,1,0:T(8,128)} %jacobi.5, bf16[4,128,128]{2,1,0:T(8,128)(2,1)} %tiles.1), custom_call_target="tpu_custom_call" | custom-call | tf_op jit(solution)/shard_map/pallas_call | solution.py:35
  3.6 3.0 %collective-permute-start.5 = (f32[32,128]{1,0:T(8,128)S(1)}, f32[32,128]{1,0:T(8,128)S(1)}, u32[]{:S(2)}, u32[]{:S(2)}) collective-permute-start(f32[32,128]{1,0:T(8,128)S(1)} %bitcast.15), channel_id=1, source_target_pairs={{0,8},{8,16},{16,24},{24,0},{1,9},{9,17},{17,25},{25,1},{2,10},{10... | collective-permute-start | bytes 49160 | tf_op jit(solution)/shard_map/ppermute | solution.py:168
  6.6 1.5 %collective-permute-start.4 = (f32[32,128]{1,0:T(8,128)S(1)}, f32[32,128]{1,0:T(8,128)S(1)}, u32[]{:S(2)}, u32[]{:S(2)}) collective-permute-start(f32[32,128]{1,0:T(8,128)S(1)} %bitcast.16), channel_id=1, source_target_pairs={{0,16},{8,24},{16,0},{24,8},{1,17},{9,25},{17,1},{25,9},{2,18},{10... | collective-permute-start | bytes 49160 | tf_op jit(solution)/shard_map/ppermute | solution.py:168
  8.1 1.6 %collective-permute-start.2 = (s16[496,128]{1,0:T(8,128)(2,1)}, s16[496,128]{1,0:T(8,128)(2,1)S(1)}, u32[]{:S(2)}, u32[]{:S(2)}) collective-permute-start(s16[496,128]{1,0:T(8,128)(2,1)} %shard_map.86), channel_id=1, source_target_pairs={{0,2},{1,3},{2,4},{3,5},{4,6},{5,7},{6,0},{7,1},{8,10},{9,11},{10,... | collective-permute-start | bytes 380936 | tf_op jit(solution)/shard_map/ppermute | solution.py:168
  9.7 2.6 %collective-permute-start.1 = (s16[496,128]{1,0:T(8,128)(2,1)}, s16[496,128]{1,0:T(8,128)(2,1)S(1)}, u32[]{:S(2)}, u32[]{:S(2)}) collective-permute-start(s16[496,128]{1,0:T(8,128)(2,1)} %shard_map.86), channel_id=1, source_target_pairs={{0,4},{1,5},{2,6},{3,7},{4,0},{5,1},{6,2},{7,3},{8,12},{9,13},{10,... | collective-permute-start | bytes 380936 | tf_op jit(solution)/shard_map/ppermute | solution.py:168
  12.3 1.3 %collective-permute-start = (s16[496,128]{1,0:T(8,128)(2,1)}, s16[496,128]{1,0:T(8,128)(2,1)S(1)}, u32[]{:S(2)}, u32[]{:S(2)}) collective-permute-start(s16[496,128]{1,0:T(8,128)(2,1)} %shard_map.86), channel_id=1, source_target_pairs={{0,6},{1,7},{2,0},{3,1},{4,2},{5,3},{6,4},{7,5},{8,14},{9,15},{10,... | collective-permute-start | bytes 380936 | tf_op jit(solution)/shard_map/ppermute | solution.py:168
  13.6 0.2 fusion.8
  13.8 0.2 select_reduce_fusion.2
  14.0 1.5 %collective-permute-start.3 = (f32[32,128]{1,0:T(8,128)S(1)}, f32[32,128]{1,0:T(8,128)S(1)}, u32[]{:S(2)}, u32[]{:S(2)}) collective-permute-start(f32[32,128]{1,0:T(8,128)S(1)} %bitcast.17), channel_id=1, source_target_pairs={{0,24},{8,0},{16,8},{24,16},{1,25},{9,1},{17,9},{25,17},{2,26},{10... | collective-permute-start | bytes 49160 | tf_op jit(solution)/shard_map/ppermute | solution.py:168
  15.6 0.6 %collective-permute-start.13 = (f32[32,1024]{1,0:T(8,128)S(1)}, f32[32,1024]{1,0:T(8,128)S(1)}, u32[]{:S(2)}, u32[]{:S(2)}) collective-permute-start(f32[32,1024]{1,0:T(8,128)S(1)} %copy-done.1), channel_id=1, source_target_pairs={{0,8},{8,16},{16,24},{24,0},{1,9},{9,17},{17,25},{25,1},{2,10},{10... | collective-permute-start | bytes 393224 | tf_op jit(solution)/shard_map/ppermute | solution.py:168
  16.2 1.7 %collective-permute-done.3.refs_1_ = f32[32,128]{1,0:T(8,128)S(1)} collective-permute-done((f32[32,128]{1,0:T(8,128)S(1)}, f32[32,128]{1,0:T(8,128)S(1)}, u32[]{:S(2)}, u32[]{:S(2)}) %collective-permute-start.3) | collective-permute-done | bytes 16416 | tf_op jit(solution)/shard_map/ppermute | solution.py:168
  17.9 0.6 %collective-permute-start.12 = (f32[32,1024]{1,0:T(8,128)S(1)}, f32[32,1024]{1,0:T(8,128)S(1)}, u32[]{:S(2)}, u32[]{:S(2)}) collective-permute-start(f32[32,1024]{1,0:T(8,128)S(1)} %copy-done.1), channel_id=1, source_target_pairs={{0,16},{8,24},{16,0},{24,8},{1,17},{9,25},{17,1},{25,9},{2,18},{10... | collective-permute-start | bytes 393224 | tf_op jit(solution)/shard_map/ppermute | solution.py:168
  18.5 2.0 %shard_map.87 = (f32[128,128]{1,0:T(8,128)S(1)}, f32[224,128]{1,0:T(8,128)S(1)}, f32[8,128]{1,0:T(8,128)S(1)}) custom-call(s32[1]{0:T(128)} %bitcast.1.turn, f32[32,128]{1,0:T(8,128)S(1)} %bitcast.18, f32[32,128]{1,0:T(8,128)S(1)} %collective-permute-done.3.refs_1_, f32[32,128]{1,0:T(8,128)S(1)} %collective-permute-done.4.refs_2_, ...), custom_call_target="tpu_custom_call" | custom-call | tf_op jit(solution)/shard_map/pallas_call | solution.py:35
  20.6 2.2 %collective-permute-start.11 = (f32[32,1024]{1,0:T(8,128)S(1)}, f32[32,1024]{1,0:T(8,128)S(1)}, u32[]{:S(2)}, u32[]{:S(2)}) collective-permute-start(f32[32,1024]{1,0:T(8,128)S(1)} %copy-done.1), channel_id=1, source_target_pairs={{0,24},{8,0},{16,8},{24,16},{1,25},{9,1},{17,9},{25,17},{2,26},{10... | collective-permute-start | bytes 393224 | tf_op jit(solution)/shard_map/ppermute | solution.py:168
  23.1 0.6 %collective-permute-start.7 = (s16[4,496,128]{2,1,0:T(8,128)(2,1)S(1)}, s16[4,496,128]{2,1,0:T(8,128)(2,1)S(1)}, u32[]{:S(2)}, u32[]{:S(2)}) collective-permute-start(s16[4,496,128]{2,1,0:T(8,128)(2,1)S(1)} %pad_add_fusion.near), channel_id=1, source_target_pairs={{0,1},{1,0},{2,3},{3,2},{4,5},{5,4},{6,7},{7,6},{8,9},{9,8},{10,11... | collective-permute-start | bytes 1523720 | tf_op jit(solution)/shard_map/ppermute | solution.py:216
  23.7 0.4 collective-permute-done.6
  24.5 0.2 select_reduce_fusion
  24.7 0.1 and_select_fusion
  24.9 0.1 select_n.103.sources
  25.0 0.2 collective-permute-done.7.far
  25.2 3.7 %shard_map.88 = (f32[6,1,32,128]{3,2,1,0:T(8,128)S(1)}, f32[6,1,32,128]{3,2,1,0:T(8,128)S(1)}, f32[6,1,32,128]{3,2,1,0:T(8,128)S(1)}, f32[6,1,32,128]{3,2,1,0:T(8,128)S(1)}) custom-call(s32[72]{0:T(128)S(1)} %select_n.103.sources, s32[4]{0:T(128)S(1)} %compare_select_fusion.give, s16[4,496,128]{2,1,0:T(8,128)(2,1)S(1)} %pad_add_fusion.near, ...), custom_call_target="tpu_custom_call" | custom-call | tf_op jit(solution)/shard_map/pallas_call | solution.py:35
  28.9 0.8 %collective-permute-start.8 = (f32[6,1,32,128]{3,2,1,0:T(8,128)S(1)}, f32[6,1,32,128]{3,2,1,0:T(8,128)S(1)}, u32[]{:S(2)}, u32[]{:S(2)}) collective-permute-start(f32[6,1,32,128]{3,2,1,0:T(8,128)S(1)} %get-tuple-element.46), channel_id=1, source_target_pairs={{0,24},{8,0},{16,8},{24,16},{1,25},{9,1},{17,9},{25,17},{2,26},{10... | collective-permute-start | bytes 294920 | tf_op jit(solution)/shard_map/ppermute | solution.py:168
  29.6 0.9 %collective-permute-start.9 = (f32[6,1,32,128]{3,2,1,0:T(8,128)S(1)}, f32[6,1,32,128]{3,2,1,0:T(8,128)S(1)}, u32[]{:S(2)}, u32[]{:S(2)}) collective-permute-start(f32[6,1,32,128]{3,2,1,0:T(8,128)S(1)} %get-tuple-element.47), channel_id=1, source_target_pairs={{0,16},{8,24},{16,0},{24,8},{1,17},{9,25},{17,1},{25,9},{2,18},{10... | collective-permute-start | bytes 294920 | tf_op jit(solution)/shard_map/ppermute | solution.py:168
  30.5 1.9 %collective-permute-start.10 = (f32[6,1,32,128]{3,2,1,0:T(8,128)S(1)}, f32[6,1,32,128]{3,2,1,0:T(8,128)S(1)}, u32[]{:S(2)}, u32[]{:S(2)}) collective-permute-start(f32[6,1,32,128]{3,2,1,0:T(8,128)S(1)} %get-tuple-element.48), channel_id=1, source_target_pairs={{0,8},{8,16},{16,24},{24,0},{1,9},{9,17},{17,25},{25,1},{2,10},{10... | collective-permute-start | bytes 294920 | tf_op jit(solution)/shard_map/ppermute | solution.py:168
  32.6 2.8 %shard_map.89 = (f32[8,192,128]{2,1,0:T(8,128)S(1)}, f32[8,192,128]{2,1,0:T(8,128)S(1)}, f32[1,128]{1,0:T(1,128)S(1)}, f32[1,128,128]{2,1,0:T(8,128)S(1)}) custom-call(s32[8]{0:T(128)S(1)} %select_reduce_fusion.1.where, s32[4]{0:T(128)S(1)} %get-tuple-element.63.held, f32[224,128]{1,0:T(8,128)S(1)} %get-tuple-element.49.powers, f32[8,128,128]{2,1,0:T(8,128)S(1)} %copy-done, ...), custom_call_target="tpu_custom_call" | custom-call | tf_op jit(solution)/shard_map/pallas_call | solution.py:35
  35.4 1.6 %collective-permute-done.10.refs_3_ = f32[6,1,32,128]{3,2,1,0:T(8,128)S(1)} collective-permute-done((f32[6,1,32,128]{3,2,1,0:T(8,128)S(1)}, f32[6,1,32,128]{3,2,1,0:T(8,128)S(1)}, u32[]{:S(2)}, u32[]{:S(2)}) %collective-permute-start.10) | collective-permute-done | bytes 98336 | tf_op jit(solution)/shard_map/ppermute | solution.py:168
  37.0 2.4 %shard_map.90 = (f32[32,1,128]{2,1,0:T(1,128)S(1)}, f32[6,1,32,128]{3,2,1,0:T(8,128)S(1)}, f32[6,1,32,128]{3,2,1,0:T(8,128)S(1)}, f32[6,1,32,128]{3,2,1,0:T(8,128)S(1)}, f32[6,1,32,128]{3,2,1,0:T(8,128)S(1)}) custom-call(s32[4]{0:T(128)S(1)} %get-tuple-element.63.held, s32[4]{0:T(128)S(1)} %get-tuple-element.62.used, ...), custom_call_target="tpu_custom_call" | custom-call | tf_op jit(solution)/shard_map/pallas_call | solution.py:35
  39.5 0.4 collective-permute-start.14
  39.8 0.9 %collective-permute-start.15 = (f32[6,1,32,128]{3,2,1,0:T(8,128)S(1)}, f32[6,1,32,128]{3,2,1,0:T(8,128)S(1)}, u32[]{:S(2)}, u32[]{:S(2)}) collective-permute-start(f32[6,1,32,128]{3,2,1,0:T(8,128)S(1)} %get-tuple-element.60), channel_id=1, source_target_pairs={{0,16},{8,24},{16,0},{24,8},{1,17},{9,25},{17,1},{25,9},{2,18},{10... | collective-permute-start | bytes 294920 | tf_op jit(solution)/shard_map/ppermute | solution.py:168
  40.8 2.3 %collective-permute-start.16 = (f32[6,1,32,128]{3,2,1,0:T(8,128)S(1)}, f32[6,1,32,128]{3,2,1,0:T(8,128)S(1)}, u32[]{:S(2)}, u32[]{:S(2)}) collective-permute-start(f32[6,1,32,128]{3,2,1,0:T(8,128)S(1)} %get-tuple-element.61), channel_id=1, source_target_pairs={{0,24},{8,0},{16,8},{24,16},{1,25},{9,1},{17,9},{25,17},{2,26},{10... | collective-permute-start | bytes 294920 | tf_op jit(solution)/shard_map/ppermute | solution.py:168
  43.1 10.1 %all_to_all.5.grams = f32[32,1,128]{2,1,0:T(1,128)S(1)} all-to-all(f32[32,1,128]{2,1,0:T(1,128)S(1)} %get-tuple-element.54), channel_id=1, replica_groups=mesh['cols'=4,'rows'=8] {'cols','rows'}, dimensions={0} | all-to-all | bytes 32768 | tf_op jit(solution)/shard_map/all_to_all | solution.py:567
  53.2 2.1 %shard_map.91 = (f32[32,1024]{1,0:T(8,128)}, f32[32,1024]{1,0:T(8,128)}) custom-call(s32[4]{0:T(128)S(1)} %get-tuple-element.63.held, s32[8]{0:T(128)S(1)} %select_reduce_fusion.1.where, f32[32,1,128]{2,1,0:T(1,128)S(1)} %all_to_all.5.grams, f32[8,128]{1,0:T(8,128)S(1)} %get-tuple-element.55.scale, f32[32,1024]{1,0:T(8,128)S(1)} %copy-done.1, ...), custom_call_target="tpu_custom_call" | custom-call | tf_op jit(solution)/shard_map/pallas_call | solution.py:35
  (45 shorter events, 0.9 us)
Async XLA Ops:
  1.3 2.3 %copy-start.2 = (f32[128,32]{0,1:T(8,128)S(1)}, f32[128,32]{0,1:T(8,128)}, u32[]{:S(2)}) copy-start(f32[128,32]{0,1:T(8,128)} %param.9) | copy-start | bytes 49156
  1.3 12.3 %copy-start.4 = (s32[4]{0:T(128)S(1)}, s32[4]{0:T(128)}, u32[]{:S(2)}) copy-start(s32[4]{0:T(128)} %local.1) | copy-start | bytes 52
  1.3 14.2 %copy-start.1 = (f32[32,1024]{1,0:T(8,128)S(1)}, f32[32,1024]{1,0:T(8,128)}, u32[]{:S(2)}) copy-start(f32[32,1024]{1,0:T(8,128)} %gradient.3) | copy-start | bytes 393220
  3.5 19.3 %copy-start.3 = (s16[496,128]{1,0:T(8,128)(2,1)S(1)}, s16[496,128]{1,0:T(8,128)(2,1)}, u32[]{:S(2)}) copy-start(s16[496,128]{1,0:T(8,128)(2,1)} %shard_map.86) | copy-start | bytes 380932
  3.6 10.5 %collective-permute-start.5 = (f32[32,128]{1,0:T(8,128)S(1)}, f32[32,128]{1,0:T(8,128)S(1)}, u32[]{:S(2)}, u32[]{:S(2)}) collective-permute-start(f32[32,128]{1,0:T(8,128)S(1)} %bitcast.15), channel_id=1, source_target_pairs={{0,8},{8,16},{16,24},{24,0},{1,9},{9,17},{17,25},{25,1},{2,10},{10... | collective-permute-start | bytes 49160 | tf_op jit(solution)/shard_map/ppermute | solution.py:168
  6.6 9.0 %collective-permute-start.4 = (f32[32,128]{1,0:T(8,128)S(1)}, f32[32,128]{1,0:T(8,128)S(1)}, u32[]{:S(2)}, u32[]{:S(2)}) collective-permute-start(f32[32,128]{1,0:T(8,128)S(1)} %bitcast.16), channel_id=1, source_target_pairs={{0,16},{8,24},{16,0},{24,8},{1,17},{9,25},{17,1},{25,9},{2,18},{10... | collective-permute-start | bytes 49160 | tf_op jit(solution)/shard_map/ppermute | solution.py:168
  8.1 12.5 %collective-permute-start.2 = (s16[496,128]{1,0:T(8,128)(2,1)}, s16[496,128]{1,0:T(8,128)(2,1)S(1)}, u32[]{:S(2)}, u32[]{:S(2)}) collective-permute-start(s16[496,128]{1,0:T(8,128)(2,1)} %shard_map.86), channel_id=1, source_target_pairs={{0,2},{1,3},{2,4},{3,5},{4,6},{5,7},{6,0},{7,1},{8,10},{9,11},{10,... | collective-permute-start | bytes 380936 | tf_op jit(solution)/shard_map/ppermute | solution.py:168
  9.7 13.1 %collective-permute-start.1 = (s16[496,128]{1,0:T(8,128)(2,1)}, s16[496,128]{1,0:T(8,128)(2,1)S(1)}, u32[]{:S(2)}, u32[]{:S(2)}) collective-permute-start(s16[496,128]{1,0:T(8,128)(2,1)} %shard_map.86), channel_id=1, source_target_pairs={{0,4},{1,5},{2,6},{3,7},{4,0},{5,1},{6,2},{7,3},{8,12},{9,13},{10,... | collective-permute-start | bytes 380936 | tf_op jit(solution)/shard_map/ppermute | solution.py:168
  12.3 10.5 %collective-permute-start = (s16[496,128]{1,0:T(8,128)(2,1)}, s16[496,128]{1,0:T(8,128)(2,1)S(1)}, u32[]{:S(2)}, u32[]{:S(2)}) collective-permute-start(s16[496,128]{1,0:T(8,128)(2,1)} %shard_map.86), channel_id=1, source_target_pairs={{0,6},{1,7},{2,0},{3,1},{4,2},{5,3},{6,4},{7,5},{8,14},{9,15},{10,... | collective-permute-start | bytes 380936 | tf_op jit(solution)/shard_map/ppermute | solution.py:168
  14.0 3.9 %collective-permute-start.3 = (f32[32,128]{1,0:T(8,128)S(1)}, f32[32,128]{1,0:T(8,128)S(1)}, u32[]{:S(2)}, u32[]{:S(2)}) collective-permute-start(f32[32,128]{1,0:T(8,128)S(1)} %bitcast.17), channel_id=1, source_target_pairs={{0,24},{8,0},{16,8},{24,16},{1,25},{9,1},{17,9},{25,17},{2,26},{10... | collective-permute-start | bytes 49160 | tf_op jit(solution)/shard_map/ppermute | solution.py:168
  15.6 15.0 %collective-permute-start.13 = (f32[32,1024]{1,0:T(8,128)S(1)}, f32[32,1024]{1,0:T(8,128)S(1)}, u32[]{:S(2)}, u32[]{:S(2)}) collective-permute-start(f32[32,1024]{1,0:T(8,128)S(1)} %copy-done.1), channel_id=1, source_target_pairs={{0,8},{8,16},{16,24},{24,0},{1,9},{9,17},{17,25},{25,1},{2,10},{10... | collective-permute-start | bytes 393224 | tf_op jit(solution)/shard_map/ppermute | solution.py:168
  17.9 14.7 %collective-permute-start.12 = (f32[32,1024]{1,0:T(8,128)S(1)}, f32[32,1024]{1,0:T(8,128)S(1)}, u32[]{:S(2)}, u32[]{:S(2)}) collective-permute-start(f32[32,1024]{1,0:T(8,128)S(1)} %copy-done.1), channel_id=1, source_target_pairs={{0,16},{8,24},{16,0},{24,8},{1,17},{9,25},{17,1},{25,9},{2,18},{10... | collective-permute-start | bytes 393224 | tf_op jit(solution)/shard_map/ppermute | solution.py:168
  20.6 12.0 %collective-permute-start.11 = (f32[32,1024]{1,0:T(8,128)S(1)}, f32[32,1024]{1,0:T(8,128)S(1)}, u32[]{:S(2)}, u32[]{:S(2)}) collective-permute-start(f32[32,1024]{1,0:T(8,128)S(1)} %copy-done.1), channel_id=1, source_target_pairs={{0,24},{8,0},{16,8},{24,16},{1,25},{9,1},{17,9},{25,17},{2,26},{10... | collective-permute-start | bytes 393224 | tf_op jit(solution)/shard_map/ppermute | solution.py:168
  22.9 1.2 %collective-permute-start.6 = (s16[4,16,128]{2,1,0:T(8,128)(2,1)S(1)}, s16[4,16,128]{2,1,0:T(8,128)(2,1)S(1)}, u32[]{:S(2)}, u32[]{:S(2)}) collective-permute-start(s16[4,16,128]{2,1,0:T(8,128)(2,1)S(1)} %slice.30), channel_id=1, source_target_pairs={{0,1},{1,0},{2,3},{3,2},{4,5},{5,4},{6,7},{7,6},{8,9},{9,8},{10,11... | collective-permute-start | bytes 49160 | tf_op jit(solution)/shard_map/ppermute | solution.py:215
  23.1 2.1 %collective-permute-start.7 = (s16[4,496,128]{2,1,0:T(8,128)(2,1)S(1)}, s16[4,496,128]{2,1,0:T(8,128)(2,1)S(1)}, u32[]{:S(2)}, u32[]{:S(2)}) collective-permute-start(s16[4,496,128]{2,1,0:T(8,128)(2,1)S(1)} %pad_add_fusion.near), channel_id=1, source_target_pairs={{0,1},{1,0},{2,3},{3,2},{4,5},{5,4},{6,7},{7,6},{8,9},{9,8},{10,11... | collective-permute-start | bytes 1523720 | tf_op jit(solution)/shard_map/ppermute | solution.py:216
  24.8 7.7 %copy-start = (f32[8,128,128]{2,1,0:T(8,128)S(1)}, f32[8,128,128]{2,1,0:T(8,128)}, u32[]{:S(2)}) copy-start(f32[8,128,128]{2,1,0:T(8,128)} %jacobi.5) | copy-start | bytes 1572868
  28.9 6.6 %collective-permute-start.8 = (f32[6,1,32,128]{3,2,1,0:T(8,128)S(1)}, f32[6,1,32,128]{3,2,1,0:T(8,128)S(1)}, u32[]{:S(2)}, u32[]{:S(2)}) collective-permute-start(f32[6,1,32,128]{3,2,1,0:T(8,128)S(1)} %get-tuple-element.46), channel_id=1, source_target_pairs={{0,24},{8,0},{16,8},{24,16},{1,25},{9,1},{17,9},{25,17},{2,26},{10... | collective-permute-start | bytes 294920 | tf_op jit(solution)/shard_map/ppermute | solution.py:168
  29.6 5.8 %collective-permute-start.9 = (f32[6,1,32,128]{3,2,1,0:T(8,128)S(1)}, f32[6,1,32,128]{3,2,1,0:T(8,128)S(1)}, u32[]{:S(2)}, u32[]{:S(2)}) collective-permute-start(f32[6,1,32,128]{3,2,1,0:T(8,128)S(1)} %get-tuple-element.47), channel_id=1, source_target_pairs={{0,16},{8,24},{16,0},{24,8},{1,17},{9,25},{17,1},{25,9},{2,18},{10... | collective-permute-start | bytes 294920 | tf_op jit(solution)/shard_map/ppermute | solution.py:168
  30.5 6.5 %collective-permute-start.10 = (f32[6,1,32,128]{3,2,1,0:T(8,128)S(1)}, f32[6,1,32,128]{3,2,1,0:T(8,128)S(1)}, u32[]{:S(2)}, u32[]{:S(2)}) collective-permute-start(f32[6,1,32,128]{3,2,1,0:T(8,128)S(1)} %get-tuple-element.48), channel_id=1, source_target_pairs={{0,8},{8,16},{16,24},{24,0},{1,9},{9,17},{17,25},{25,1},{2,10},{10... | collective-permute-start | bytes 294920 | tf_op jit(solution)/shard_map/ppermute | solution.py:168
  39.5 13.7 %collective-permute-start.14 = (f32[6,1,32,128]{3,2,1,0:T(8,128)S(1)}, f32[6,1,32,128]{3,2,1,0:T(8,128)S(1)}, u32[]{:S(2)}, u32[]{:S(2)}) collective-permute-start(f32[6,1,32,128]{3,2,1,0:T(8,128)S(1)} %get-tuple-element.59), channel_id=1, source_target_pairs={{0,8},{8,16},{16,24},{24,0},{1,9},{9,17},{17,25},{25,1},{2,10},{10... | collective-permute-start | bytes 294920 | tf_op jit(solution)/shard_map/ppermute | solution.py:168
  39.8 13.4 %collective-permute-start.15 = (f32[6,1,32,128]{3,2,1,0:T(8,128)S(1)}, f32[6,1,32,128]{3,2,1,0:T(8,128)S(1)}, u32[]{:S(2)}, u32[]{:S(2)}) collective-permute-start(f32[6,1,32,128]{3,2,1,0:T(8,128)S(1)} %get-tuple-element.60), channel_id=1, source_target_pairs={{0,16},{8,24},{16,0},{24,8},{1,17},{9,25},{17,1},{25,9},{2,18},{10... | collective-permute-start | bytes 294920 | tf_op jit(solution)/shard_map/ppermute | solution.py:168
  40.8 12.5 %collective-permute-start.16 = (f32[6,1,32,128]{3,2,1,0:T(8,128)S(1)}, f32[6,1,32,128]{3,2,1,0:T(8,128)S(1)}, u32[]{:S(2)}, u32[]{:S(2)}) collective-permute-start(f32[6,1,32,128]{3,2,1,0:T(8,128)S(1)} %get-tuple-element.61), channel_id=1, source_target_pairs={{0,24},{8,0},{16,8},{24,16},{1,25},{9,1},{17,9},{25,17},{2,26},{10... | collective-permute-start | bytes 294920 | tf_op jit(solution)/shard_map/ppermute | solution.py:168

commit v8 on v7

--- a/solution.py
+++ b/solution.py
@@ -113,14 +113,15 @@
 
 
 def chain_kernel(sources, give, near, far, *refs):
-    sends, (operators, tops, held, out) = refs[:-4], refs[-4:]
+    sends, (operators, tops, held, out, kept) = refs[:-5], refs[-5:]
     groups = near.shape[0]
     width = held.shape[1]
     height = BLOCK + width
     slots = near.shape[1] // height
     half = groups * slots
     total = 2 * half
-    share = sends[0].shape[1]
+    count = kept.shape[0] // len(sends)
+    share = count // ITERS
     lane = lax.broadcasted_iota(jnp.int32, (width, BLOCK), 1)
     row = lax.broadcasted_iota(jnp.int32, (width, BLOCK), 0)
     for q in range(total):
@@ -155,12 +156,24 @@
             for i in range(1, slots):
                 value += out[sources[q * slots + i]]
             held[q] = value
-        for o, send in enumerate(sends):
+        for o in range(len(sends)):
             for p in range(share):
-                send[j, p] = held[give[o * share + p]]
+                kept[o * count + j * share + p] = held[give[o * share + p]]
         return carry
 
     lax.fori_loop(0, ITERS, step, 0)
+    line = lax.broadcasted_iota(jnp.int32, (NOTE_ROWS, BLOCK), 0)
+    for o, send in enumerate(sends):
+        notes = jnp.zeros((NOTE_ROWS, BLOCK), jnp.int32)
+        for n in range(count):
+            at = n * width
+            value = kept[o * count + n]
+            number = note(jnp.max(jnp.abs(value), axis=1, keepdims=True))
+            send[at : at + width, :] = code(value, number)
+            number = jnp.where(lane == at % BLOCK + row, number, 0)
+            number = jnp.sum(number, axis=0, keepdims=True)
+            notes = jnp.where(line == at // BLOCK, notes + number, notes)
+        send[count * width :, :] = notes.astype(jnp.int16)
 
 
 def shift(x, axis, by):
@@ -244,7 +257,7 @@
     shape = jax.ShapeDtypeStruct
     sends = call(
         chain_kernel,
-        tuple([shape((ITERS, share, width, BLOCK), f32)] * columns),
+        tuple([shape((ITERS * share * width + NOTE_ROWS, BLOCK), jnp.int16)] * columns),
         sources,
         jnp.where(order < slots, order, total),
         near,
@@ -255,6 +268,7 @@
             pltpu.VMEM((total, width, BLOCK), f32),
             pltpu.VMEM((total + 1, width, BLOCK), f32),
             pltpu.VMEM((total + 1, width, BLOCK), f32),
+            pltpu.VMEM((columns * ITERS * share, width, BLOCK), f32),
         ],
     )
     return list(sends), pieces, powers
@@ -384,12 +398,26 @@
     parts = refs[:devices]
     starts, scaled, jacobi, others, gram = refs[devices : devices + 5]
     backs = refs[devices + 5 :]
-    share, width = parts[0].shape[1:3]
+    share = starts.shape[0]
+    width = BLOCK // devices
+    lane = lax.broadcasted_iota(jnp.int32, (width, BLOCK), 1)
+    row = lax.broadcasted_iota(jnp.int32, (width, BLOCK), 0)
+
+    def chained(part, j, p):
+        if part.dtype == f32:
+            return part[j, p]
+        at = (j * share + p) * width
+        notes = part[ITERS * share * width :, :].astype(f32)
+        notes = notes[at // BLOCK : at // BLOCK + 1, :]
+        number = jnp.where(lane == at % BLOCK + row, notes, 0.0)
+        scale = noted_range(jnp.sum(number, axis=1, keepdims=True)) * (1.0 / LEVELS)
+        return part[at : at + width, :].astype(f32) * scale
+
     sums = {}
     for p in range(share):
         now = [starts[p]]
         for j in range(ITERS):
-            now.append(jnp.concatenate([part[j, p] for part in parts], 0))
+            now.append(jnp.concatenate([chained(part, j, p) for part in parts], 0))
         past = None
         chosen = [now[0]]
         for k in range(ITERS):
@@ -491,6 +519,7 @@
 
     gathered = devices * slots * BLOCK * (BLOCK + width) * 2
     noted = slots * (4 + width) <= BLOCK and width % NOTE_ROWS == 0 and devices * blocks < 2**15
+    noted = noted and ITERS * -(-slots // columns) * width <= NOTE_ROWS * BLOCK
     whole = gathered <= GATHER_BYTES and noted and devices % 2 == 0 and not exchange
     units = slots if whole else blocks
     share = -(-units // columns)

time: 55.5 us -> 54.7 us (0.986)
  waiting for transfers between devices: 4 us -> 2.5 us
    ppermute x15, waiting for transfers between devices: 3.34 us -> 1.83 us  [shift(): return lax.ppermute(x, axis, [(i, (i - by) % size) for i in range(size)])]
  transfers between devices with their start and end apart: 17 -> 17, of which waited for: 4 -> 4; matrix products, arithmetic and copies ran while one was open for 3% -> 3% of each run, Pallas kernels for 15% -> 16%
where the time goes in v8:
time: 54.7 us; the launch traced here: 54.5 us
  starting transfers between devices  23.4 us (43%)
  Pallas kernels  15.8 us (29%)
  blocking collectives  9.82 us (18%)
  waiting for transfers between devices  2.5 us (5%)
  between operations  1.49 us (3%)
  other arithmetic  1.03 us (2%)
    ppermute x15, starting transfers between devices, shift(): return lax.ppermute(x, axis, [(i, (i - by) % size) for i in range(size)])  22.7 us
    pallas_call x6, Pallas kernels, call(): pl.pallas_call(kernel, out_shape=outs, in_specs=specs, out_specs=tuple([V...  15.8 us
    all_to_all x1, blocking collectives, on_device(): grams = lax.all_to_all(gram, ('cols', 'rows'), 0, 0, tiled=True)  9.82 us
    ppermute x15, waiting for transfers between devices, shift(): return lax.ppermute(x, axis, [(i, (i - by) % size) for i in range(size)])  1.83 us
  transfers between devices with their start and end apart: 17, of which 4 were waited for; matrix products, arithmetic and copies ran while one was open for 3% of the time, Pallas kernels for 16%

profile of v8, /device:TPU:0, one launch (start us, length us, event | category | flops | bytes accessed | tf_op | source)
XLA Modules:
  0.0 54.5 jit_solution(5975765615683395849)
XLA Ops:
  1.3 2.2 %shard_map.86 = s16[496,128]{1,0:T(8,128)(2,1)} custom-call(s32[4]{0:T(128)} %local.1, s32[4]{0:T(128)} %remote.1, s32[1]{0:T(128)} %copy.16.count, f32[32,1024]{1,0:T(8,128)} %gradient.3, f32[8,128,128]{2,1,0:T(8,128)} %jacobi.5, bf16[4,128,128]{2,1,0:T(8,128)(2,1)} %tiles.1), custom_call_target="tpu_custom_call" | custom-call | tf_op jit(solution)/shard_map/pallas_call | solution.py:35
  3.6 3.0 %collective-permute-start.5 = (f32[32,128]{1,0:T(8,128)S(1)}, f32[32,128]{1,0:T(8,128)S(1)}, u32[]{:S(2)}, u32[]{:S(2)}) collective-permute-start(f32[32,128]{1,0:T(8,128)S(1)} %bitcast.15), channel_id=1, source_target_pairs={{0,8},{8,16},{16,24},{24,0},{1,9},{9,17},{17,25},{25,1},{2,10},{10... | collective-permute-start | bytes 49160 | tf_op jit(solution)/shard_map/ppermute | solution.py:181
  6.6 1.5 %collective-permute-start.4 = (f32[32,128]{1,0:T(8,128)S(1)}, f32[32,128]{1,0:T(8,128)S(1)}, u32[]{:S(2)}, u32[]{:S(2)}) collective-permute-start(f32[32,128]{1,0:T(8,128)S(1)} %bitcast.16), channel_id=1, source_target_pairs={{0,16},{8,24},{16,0},{24,8},{1,17},{9,25},{17,1},{25,9},{2,18},{10... | collective-permute-start | bytes 49160 | tf_op jit(solution)/shard_map/ppermute | solution.py:181
  8.1 1.6 %collective-permute-start.2 = (s16[496,128]{1,0:T(8,128)(2,1)}, s16[496,128]{1,0:T(8,128)(2,1)S(1)}, u32[]{:S(2)}, u32[]{:S(2)}) collective-permute-start(s16[496,128]{1,0:T(8,128)(2,1)} %shard_map.86), channel_id=1, source_target_pairs={{0,2},{1,3},{2,4},{3,5},{4,6},{5,7},{6,0},{7,1},{8,10},{9,11},{10,... | collective-permute-start | bytes 380936 | tf_op jit(solution)/shard_map/ppermute | solution.py:181
  9.7 2.6 %collective-permute-start.1 = (s16[496,128]{1,0:T(8,128)(2,1)}, s16[496,128]{1,0:T(8,128)(2,1)S(1)}, u32[]{:S(2)}, u32[]{:S(2)}) collective-permute-start(s16[496,128]{1,0:T(8,128)(2,1)} %shard_map.86), channel_id=1, source_target_pairs={{0,4},{1,5},{2,6},{3,7},{4,0},{5,1},{6,2},{7,3},{8,12},{9,13},{10,... | collective-permute-start | bytes 380936 | tf_op jit(solution)/shard_map/ppermute | solution.py:181
  12.3 1.3 %collective-permute-start = (s16[496,128]{1,0:T(8,128)(2,1)}, s16[496,128]{1,0:T(8,128)(2,1)S(1)}, u32[]{:S(2)}, u32[]{:S(2)}) collective-permute-start(s16[496,128]{1,0:T(8,128)(2,1)} %shard_map.86), channel_id=1, source_target_pairs={{0,6},{1,7},{2,0},{3,1},{4,2},{5,3},{6,4},{7,5},{8,14},{9,15},{10,... | collective-permute-start | bytes 380936 | tf_op jit(solution)/shard_map/ppermute | solution.py:181
  13.6 0.2 fusion.8
  13.8 0.2 select_reduce_fusion.2
  14.0 1.5 %collective-permute-start.3 = (f32[32,128]{1,0:T(8,128)S(1)}, f32[32,128]{1,0:T(8,128)S(1)}, u32[]{:S(2)}, u32[]{:S(2)}) collective-permute-start(f32[32,128]{1,0:T(8,128)S(1)} %bitcast.17), channel_id=1, source_target_pairs={{0,24},{8,0},{16,8},{24,16},{1,25},{9,1},{17,9},{25,17},{2,26},{10... | collective-permute-start | bytes 49160 | tf_op jit(solution)/shard_map/ppermute | solution.py:181
  15.6 0.6 %collective-permute-start.13 = (f32[32,1024]{1,0:T(8,128)S(1)}, f32[32,1024]{1,0:T(8,128)S(1)}, u32[]{:S(2)}, u32[]{:S(2)}) collective-permute-start(f32[32,1024]{1,0:T(8,128)S(1)} %copy-done.1), channel_id=1, source_target_pairs={{0,8},{8,16},{16,24},{24,0},{1,9},{9,17},{17,25},{25,1},{2,10},{10... | collective-permute-start | bytes 393224 | tf_op jit(solution)/shard_map/ppermute | solution.py:181
  16.2 1.7 %collective-permute-done.3.refs_1_ = f32[32,128]{1,0:T(8,128)S(1)} collective-permute-done((f32[32,128]{1,0:T(8,128)S(1)}, f32[32,128]{1,0:T(8,128)S(1)}, u32[]{:S(2)}, u32[]{:S(2)}) %collective-permute-start.3) | collective-permute-done | bytes 16416 | tf_op jit(solution)/shard_map/ppermute | solution.py:181
  17.9 0.6 %collective-permute-start.12 = (f32[32,1024]{1,0:T(8,128)S(1)}, f32[32,1024]{1,0:T(8,128)S(1)}, u32[]{:S(2)}, u32[]{:S(2)}) collective-permute-start(f32[32,1024]{1,0:T(8,128)S(1)} %copy-done.1), channel_id=1, source_target_pairs={{0,16},{8,24},{16,0},{24,8},{1,17},{9,25},{17,1},{25,9},{2,18},{10... | collective-permute-start | bytes 393224 | tf_op jit(solution)/shard_map/ppermute | solution.py:181
  18.5 2.0 %shard_map.87 = (f32[128,128]{1,0:T(8,128)S(1)}, f32[224,128]{1,0:T(8,128)S(1)}, f32[8,128]{1,0:T(8,128)S(1)}) custom-call(s32[1]{0:T(128)} %bitcast.1.turn, f32[32,128]{1,0:T(8,128)S(1)} %bitcast.18, f32[32,128]{1,0:T(8,128)S(1)} %collective-permute-done.3.refs_1_, f32[32,128]{1,0:T(8,128)S(1)} %collective-permute-done.4.refs_2_, ...), custom_call_target="tpu_custom_call" | custom-call | tf_op jit(solution)/shard_map/pallas_call | solution.py:35
  20.6 2.2 %collective-permute-start.11 = (f32[32,1024]{1,0:T(8,128)S(1)}, f32[32,1024]{1,0:T(8,128)S(1)}, u32[]{:S(2)}, u32[]{:S(2)}) collective-permute-start(f32[32,1024]{1,0:T(8,128)S(1)} %copy-done.1), channel_id=1, source_target_pairs={{0,24},{8,0},{16,8},{24,16},{1,25},{9,1},{17,9},{25,17},{2,26},{10... | collective-permute-start | bytes 393224 | tf_op jit(solution)/shard_map/ppermute | solution.py:181
  23.1 0.6 %collective-permute-start.7 = (s16[4,496,128]{2,1,0:T(8,128)(2,1)S(1)}, s16[4,496,128]{2,1,0:T(8,128)(2,1)S(1)}, u32[]{:S(2)}, u32[]{:S(2)}) collective-permute-start(s16[4,496,128]{2,1,0:T(8,128)(2,1)S(1)} %pad_add_fusion.near), channel_id=1, source_target_pairs={{0,1},{1,0},{2,3},{3,2},{4,5},{5,4},{6,7},{7,6},{8,9},{9,8},{10,11... | collective-permute-start | bytes 1523720 | tf_op jit(solution)/shard_map/ppermute | solution.py:229
  23.7 0.4 collective-permute-done.6
  24.5 0.2 select_reduce_fusion
  24.7 0.1 and_select_fusion
  24.9 0.1 select_n.103.sources
  25.0 0.2 collective-permute-done.7.far
  25.2 4.1 %shard_map.88 = (s16[208,128]{1,0:T(8,128)(2,1)S(1)}, s16[208,128]{1,0:T(8,128)(2,1)S(1)}, s16[208,128]{1,0:T(8,128)(2,1)S(1)}, s16[208,128]{1,0:T(8,128)(2,1)S(1)}) custom-call(s32[72]{0:T(128)S(1)} %select_n.103.sources, s32[4]{0:T(128)S(1)} %compare_select_fusion.give, s16[4,496,128]{2,1,0:T(8,128)(2,1)S(1)} %pad_add_fusion.near, ...), custom_call_target="tpu_custom_call" | custom-call | tf_op jit(solution)/shard_map/pallas_call | solution.py:35
  29.3 0.8 %collective-permute-start.8 = (s16[208,128]{1,0:T(8,128)(2,1)S(1)}, s16[208,128]{1,0:T(8,128)(2,1)S(1)}, u32[]{:S(2)}, u32[]{:S(2)}) collective-permute-start(s16[208,128]{1,0:T(8,128)(2,1)S(1)} %get-tuple-element.46), channel_id=1, source_target_pairs={{0,24},{8,0},{16,8},{24,16},{1,25},{9,1},{17,9},{25,17},{2,26},{10... | collective-permute-start | bytes 159752 | tf_op jit(solution)/shard_map/ppermute | solution.py:181
  30.0 0.9 %collective-permute-start.9 = (s16[208,128]{1,0:T(8,128)(2,1)S(1)}, s16[208,128]{1,0:T(8,128)(2,1)S(1)}, u32[]{:S(2)}, u32[]{:S(2)}) collective-permute-start(s16[208,128]{1,0:T(8,128)(2,1)S(1)} %get-tuple-element.47), channel_id=1, source_target_pairs={{0,16},{8,24},{16,0},{24,8},{1,17},{9,25},{17,1},{25,9},{2,18},{10... | collective-permute-start | bytes 159752 | tf_op jit(solution)/shard_map/ppermute | solution.py:181
  30.9 1.9 %collective-permute-start.10 = (s16[208,128]{1,0:T(8,128)(2,1)S(1)}, s16[208,128]{1,0:T(8,128)(2,1)S(1)}, u32[]{:S(2)}, u32[]{:S(2)}) collective-permute-start(s16[208,128]{1,0:T(8,128)(2,1)S(1)} %get-tuple-element.48), channel_id=1, source_target_pairs={{0,8},{8,16},{16,24},{24,0},{1,9},{9,17},{17,25},{25,1},{2,10},{10... | collective-permute-start | bytes 159752 | tf_op jit(solution)/shard_map/ppermute | solution.py:181
  33.0 2.8 %shard_map.89 = (f32[8,192,128]{2,1,0:T(8,128)S(1)}, f32[8,192,128]{2,1,0:T(8,128)S(1)}, f32[1,128]{1,0:T(1,128)S(1)}, f32[1,128,128]{2,1,0:T(8,128)S(1)}) custom-call(s32[8]{0:T(128)S(1)} %select_reduce_fusion.1.where, s32[4]{0:T(128)S(1)} %get-tuple-element.63.held, f32[224,128]{1,0:T(8,128)S(1)} %get-tuple-element.49.powers, f32[8,128,128]{2,1,0:T(8,128)S(1)} %copy-done, ...), custom_call_target="tpu_custom_call" | custom-call | tf_op jit(solution)/shard_map/pallas_call | solution.py:35
  35.8 0.1 collective-permute-done.10.refs_3_
  35.9 2.5 %shard_map.90 = (f32[32,1,128]{2,1,0:T(1,128)S(1)}, f32[6,1,32,128]{3,2,1,0:T(8,128)S(1)}, f32[6,1,32,128]{3,2,1,0:T(8,128)S(1)}, f32[6,1,32,128]{3,2,1,0:T(8,128)S(1)}, f32[6,1,32,128]{3,2,1,0:T(8,128)S(1)}) custom-call(s32[4]{0:T(128)S(1)} %get-tuple-element.63.held, s32[4]{0:T(128)S(1)} %get-tuple-element.62.used, ...), custom_call_target="tpu_custom_call" | custom-call | tf_op jit(solution)/shard_map/pallas_call | solution.py:35
  38.5 1.1 %collective-permute-start.14 = (f32[6,1,32,128]{3,2,1,0:T(8,128)S(1)}, f32[6,1,32,128]{3,2,1,0:T(8,128)S(1)}, u32[]{:S(2)}, u32[]{:S(2)}) collective-permute-start(f32[6,1,32,128]{3,2,1,0:T(8,128)S(1)} %get-tuple-element.59), channel_id=1, source_target_pairs={{0,8},{8,16},{16,24},{24,0},{1,9},{9,17},{17,25},{25,1},{2,10},{10... | collective-permute-start | bytes 294920 | tf_op jit(solution)/shard_map/ppermute | solution.py:181
  39.6 0.5 collective-permute-start.15
  40.1 2.5 %collective-permute-start.16 = (f32[6,1,32,128]{3,2,1,0:T(8,128)S(1)}, f32[6,1,32,128]{3,2,1,0:T(8,128)S(1)}, u32[]{:S(2)}, u32[]{:S(2)}) collective-permute-start(f32[6,1,32,128]{3,2,1,0:T(8,128)S(1)} %get-tuple-element.61), channel_id=1, source_target_pairs={{0,24},{8,0},{16,8},{24,16},{1,25},{9,1},{17,9},{25,17},{2,26},{10... | collective-permute-start | bytes 294920 | tf_op jit(solution)/shard_map/ppermute | solution.py:181
  42.6 9.8 %all_to_all.5.grams = f32[32,1,128]{2,1,0:T(1,128)S(1)} all-to-all(f32[32,1,128]{2,1,0:T(1,128)S(1)} %get-tuple-element.54), channel_id=1, replica_groups=mesh['cols'=4,'rows'=8] {'cols','rows'}, dimensions={0} | all-to-all | bytes 32768 | tf_op jit(solution)/shard_map/all_to_all | solution.py:596
  52.4 2.1 %shard_map.91 = (f32[32,1024]{1,0:T(8,128)}, f32[32,1024]{1,0:T(8,128)}) custom-call(s32[4]{0:T(128)S(1)} %get-tuple-element.63.held, s32[8]{0:T(128)S(1)} %select_reduce_fusion.1.where, f32[32,1,128]{2,1,0:T(1,128)S(1)} %all_to_all.5.grams, f32[8,128]{1,0:T(8,128)S(1)} %get-tuple-element.55.scale, f32[32,1024]{1,0:T(8,128)S(1)} %copy-done.1, ...), custom_call_target="tpu_custom_call" | custom-call | tf_op jit(solution)/shard_map/pallas_call | solution.py:35
  (45 shorter events, 0.9 us)
Async XLA Ops:
  1.3 2.3 %copy-start.2 = (f32[128,32]{0,1:T(8,128)S(1)}, f32[128,32]{0,1:T(8,128)}, u32[]{:S(2)}) copy-start(f32[128,32]{0,1:T(8,128)} %param.9) | copy-start | bytes 49156
  1.3 12.3 %copy-start.4 = (s32[4]{0:T(128)S(1)}, s32[4]{0:T(128)}, u32[]{:S(2)}) copy-start(s32[4]{0:T(128)} %local.1) | copy-start | bytes 52
  1.3 14.2 %copy-start.1 = (f32[32,1024]{1,0:T(8,128)S(1)}, f32[32,1024]{1,0:T(8,128)}, u32[]{:S(2)}) copy-start(f32[32,1024]{1,0:T(8,128)} %gradient.3) | copy-start | bytes 393220
  3.5 19.3 %copy-start.3 = (s16[496,128]{1,0:T(8,128)(2,1)S(1)}, s16[496,128]{1,0:T(8,128)(2,1)}, u32[]{:S(2)}) copy-start(s16[496,128]{1,0:T(8,128)(2,1)} %shard_map.86) | copy-start | bytes 380932
  3.6 10.5 %collective-permute-start.5 = (f32[32,128]{1,0:T(8,128)S(1)}, f32[32,128]{1,0:T(8,128)S(1)}, u32[]{:S(2)}, u32[]{:S(2)}) collective-permute-start(f32[32,128]{1,0:T(8,128)S(1)} %bitcast.15), channel_id=1, source_target_pairs={{0,8},{8,16},{16,24},{24,0},{1,9},{9,17},{17,25},{25,1},{2,10},{10... | collective-permute-start | bytes 49160 | tf_op jit(solution)/shard_map/ppermute | solution.py:181
  6.6 9.0 %collective-permute-start.4 = (f32[32,128]{1,0:T(8,128)S(1)}, f32[32,128]{1,0:T(8,128)S(1)}, u32[]{:S(2)}, u32[]{:S(2)}) collective-permute-start(f32[32,128]{1,0:T(8,128)S(1)} %bitcast.16), channel_id=1, source_target_pairs={{0,16},{8,24},{16,0},{24,8},{1,17},{9,25},{17,1},{25,9},{2,18},{10... | collective-permute-start | bytes 49160 | tf_op jit(solution)/shard_map/ppermute | solution.py:181
  8.1 12.5 %collective-permute-start.2 = (s16[496,128]{1,0:T(8,128)(2,1)}, s16[496,128]{1,0:T(8,128)(2,1)S(1)}, u32[]{:S(2)}, u32[]{:S(2)}) collective-permute-start(s16[496,128]{1,0:T(8,128)(2,1)} %shard_map.86), channel_id=1, source_target_pairs={{0,2},{1,3},{2,4},{3,5},{4,6},{5,7},{6,0},{7,1},{8,10},{9,11},{10,... | collective-permute-start | bytes 380936 | tf_op jit(solution)/shard_map/ppermute | solution.py:181
  9.7 13.1 %collective-permute-start.1 = (s16[496,128]{1,0:T(8,128)(2,1)}, s16[496,128]{1,0:T(8,128)(2,1)S(1)}, u32[]{:S(2)}, u32[]{:S(2)}) collective-permute-start(s16[496,128]{1,0:T(8,128)(2,1)} %shard_map.86), channel_id=1, source_target_pairs={{0,4},{1,5},{2,6},{3,7},{4,0},{5,1},{6,2},{7,3},{8,12},{9,13},{10,... | collective-permute-start | bytes 380936 | tf_op jit(solution)/shard_map/ppermute | solution.py:181
  12.3 10.5 %collective-permute-start = (s16[496,128]{1,0:T(8,128)(2,1)}, s16[496,128]{1,0:T(8,128)(2,1)S(1)}, u32[]{:S(2)}, u32[]{:S(2)}) collective-permute-start(s16[496,128]{1,0:T(8,128)(2,1)} %shard_map.86), channel_id=1, source_target_pairs={{0,6},{1,7},{2,0},{3,1},{4,2},{5,3},{6,4},{7,5},{8,14},{9,15},{10,... | collective-permute-start | bytes 380936 | tf_op jit(solution)/shard_map/ppermute | solution.py:181
  14.0 3.9 %collective-permute-start.3 = (f32[32,128]{1,0:T(8,128)S(1)}, f32[32,128]{1,0:T(8,128)S(1)}, u32[]{:S(2)}, u32[]{:S(2)}) collective-permute-start(f32[32,128]{1,0:T(8,128)S(1)} %bitcast.17), channel_id=1, source_target_pairs={{0,24},{8,0},{16,8},{24,16},{1,25},{9,1},{17,9},{25,17},{2,26},{10... | collective-permute-start | bytes 49160 | tf_op jit(solution)/shard_map/ppermute | solution.py:181
  15.6 15.4 %collective-permute-start.13 = (f32[32,1024]{1,0:T(8,128)S(1)}, f32[32,1024]{1,0:T(8,128)S(1)}, u32[]{:S(2)}, u32[]{:S(2)}) collective-permute-start(f32[32,1024]{1,0:T(8,128)S(1)} %copy-done.1), channel_id=1, source_target_pairs={{0,8},{8,16},{16,24},{24,0},{1,9},{9,17},{17,25},{25,1},{2,10},{10... | collective-permute-start | bytes 393224 | tf_op jit(solution)/shard_map/ppermute | solution.py:181
  17.9 15.1 %collective-permute-start.12 = (f32[32,1024]{1,0:T(8,128)S(1)}, f32[32,1024]{1,0:T(8,128)S(1)}, u32[]{:S(2)}, u32[]{:S(2)}) collective-permute-start(f32[32,1024]{1,0:T(8,128)S(1)} %copy-done.1), channel_id=1, source_target_pairs={{0,16},{8,24},{16,0},{24,8},{1,17},{9,25},{17,1},{25,9},{2,18},{10... | collective-permute-start | bytes 393224 | tf_op jit(solution)/shard_map/ppermute | solution.py:181
  20.6 12.4 %collective-permute-start.11 = (f32[32,1024]{1,0:T(8,128)S(1)}, f32[32,1024]{1,0:T(8,128)S(1)}, u32[]{:S(2)}, u32[]{:S(2)}) collective-permute-start(f32[32,1024]{1,0:T(8,128)S(1)} %copy-done.1), channel_id=1, source_target_pairs={{0,24},{8,0},{16,8},{24,16},{1,25},{9,1},{17,9},{25,17},{2,26},{10... | collective-permute-start | bytes 393224 | tf_op jit(solution)/shard_map/ppermute | solution.py:181
  22.9 1.2 %collective-permute-start.6 = (s16[4,16,128]{2,1,0:T(8,128)(2,1)S(1)}, s16[4,16,128]{2,1,0:T(8,128)(2,1)S(1)}, u32[]{:S(2)}, u32[]{:S(2)}) collective-permute-start(s16[4,16,128]{2,1,0:T(8,128)(2,1)S(1)} %slice.30), channel_id=1, source_target_pairs={{0,1},{1,0},{2,3},{3,2},{4,5},{5,4},{6,7},{7,6},{8,9},{9,8},{10,11... | collective-permute-start | bytes 49160 | tf_op jit(solution)/shard_map/ppermute | solution.py:228
  23.1 2.1 %collective-permute-start.7 = (s16[4,496,128]{2,1,0:T(8,128)(2,1)S(1)}, s16[4,496,128]{2,1,0:T(8,128)(2,1)S(1)}, u32[]{:S(2)}, u32[]{:S(2)}) collective-permute-start(s16[4,496,128]{2,1,0:T(8,128)(2,1)S(1)} %pad_add_fusion.near), channel_id=1, source_target_pairs={{0,1},{1,0},{2,3},{3,2},{4,5},{5,4},{6,7},{7,6},{8,9},{9,8},{10,11... | collective-permute-start | bytes 1523720 | tf_op jit(solution)/shard_map/ppermute | solution.py:229
  24.8 8.1 %copy-start = (f32[8,128,128]{2,1,0:T(8,128)S(1)}, f32[8,128,128]{2,1,0:T(8,128)}, u32[]{:S(2)}) copy-start(f32[8,128,128]{2,1,0:T(8,128)} %jacobi.5) | copy-start | bytes 1572868
  29.3 6.6 %collective-permute-start.8 = (s16[208,128]{1,0:T(8,128)(2,1)S(1)}, s16[208,128]{1,0:T(8,128)(2,1)S(1)}, u32[]{:S(2)}, u32[]{:S(2)}) collective-permute-start(s16[208,128]{1,0:T(8,128)(2,1)S(1)} %get-tuple-element.46), channel_id=1, source_target_pairs={{0,24},{8,0},{16,8},{24,16},{1,25},{9,1},{17,9},{25,17},{2,26},{10... | collective-permute-start | bytes 159752 | tf_op jit(solution)/shard_map/ppermute | solution.py:181
  30.0 5.8 %collective-permute-start.9 = (s16[208,128]{1,0:T(8,128)(2,1)S(1)}, s16[208,128]{1,0:T(8,128)(2,1)S(1)}, u32[]{:S(2)}, u32[]{:S(2)}) collective-permute-start(s16[208,128]{1,0:T(8,128)(2,1)S(1)} %get-tuple-element.47), channel_id=1, source_target_pairs={{0,16},{8,24},{16,0},{24,8},{1,17},{9,25},{17,1},{25,9},{2,18},{10... | collective-permute-start | bytes 159752 | tf_op jit(solution)/shard_map/ppermute | solution.py:181
  30.9 5.0 %collective-permute-start.10 = (s16[208,128]{1,0:T(8,128)(2,1)S(1)}, s16[208,128]{1,0:T(8,128)(2,1)S(1)}, u32[]{:S(2)}, u32[]{:S(2)}) collective-permute-start(s16[208,128]{1,0:T(8,128)(2,1)S(1)} %get-tuple-element.48), channel_id=1, source_target_pairs={{0,8},{8,16},{16,24},{24,0},{1,9},{9,17},{17,25},{25,1},{2,10},{10... | collective-permute-start | bytes 159752 | tf_op jit(solution)/shard_map/ppermute | solution.py:181
  38.5 13.9 %collective-permute-start.14 = (f32[6,1,32,128]{3,2,1,0:T(8,128)S(1)}, f32[6,1,32,128]{3,2,1,0:T(8,128)S(1)}, u32[]{:S(2)}, u32[]{:S(2)}) collective-permute-start(f32[6,1,32,128]{3,2,1,0:T(8,128)S(1)} %get-tuple-element.59), channel_id=1, source_target_pairs={{0,8},{8,16},{16,24},{24,0},{1,9},{9,17},{17,25},{25,1},{2,10},{10... | collective-permute-start | bytes 294920 | tf_op jit(solution)/shard_map/ppermute | solution.py:181
  39.6 12.8 %collective-permute-start.15 = (f32[6,1,32,128]{3,2,1,0:T(8,128)S(1)}, f32[6,1,32,128]{3,2,1,0:T(8,128)S(1)}, u32[]{:S(2)}, u32[]{:S(2)}) collective-permute-start(f32[6,1,32,128]{3,2,1,0:T(8,128)S(1)} %get-tuple-element.60), channel_id=1, source_target_pairs={{0,16},{8,24},{16,0},{24,8},{1,17},{9,25},{17,1},{25,9},{2,18},{10... | collective-permute-start | bytes 294920 | tf_op jit(solution)/shard_map/ppermute | solution.py:181
  40.1 12.3 %collective-permute-start.16 = (f32[6,1,32,128]{3,2,1,0:T(8,128)S(1)}, f32[6,1,32,128]{3,2,1,0:T(8,128)S(1)}, u32[]{:S(2)}, u32[]{:S(2)}) collective-permute-start(f32[6,1,32,128]{3,2,1,0:T(8,128)S(1)} %get-tuple-element.61), channel_id=1, source_target_pairs={{0,24},{8,0},{16,8},{24,16},{1,25},{9,1},{17,9},{25,17},{2,26},{10... | collective-permute-start | bytes 294920 | tf_op jit(solution)/shard_map/ppermute | solution.py:181

commit v9 on v7

--- a/solution.py
+++ b/solution.py
@@ -165,7 +165,7 @@
 
 def shift(x, axis, by):
     size = lax.axis_size(axis)
-    return lax.ppermute(x, axis, [(i, (i - by) % size) for i in range(size)])
+    return lax.ppermute(x, axis, [(i, i ^ by) for i in range(size)])
 
 
 def whole_pieces(x):
@@ -218,8 +218,7 @@
 
     me = lax.axis_index("rows")
     position = jnp.arange(devices, dtype=jnp.int32)
-    base = me ^ (position // groups)
-    device = (base + 2 * (position % groups)) % devices
+    device = me ^ (position // groups) ^ (2 * (position % groups))
     locals_, remotes, lives = (
         told[:, i * slots : (i + 1) * slots].astype(jnp.int32) for i in range(3)
     )
@@ -311,11 +310,16 @@
     return result
 
 
-def powers_kernel(turn, *refs):
+def powers_kernel(me, *refs):
     pieces, (scaled, powers, scale) = refs[:-3], refs[-3:]
     width = pieces[0].shape[0]
     factor = jnp.concatenate([piece[...] for piece in pieces], 0)
-    factor = pltpu.roll(factor, turn[0], 1)
+    lane = lax.broadcasted_iota(jnp.int32, factor.shape, 1)
+    for bit in range((len(pieces) - 1).bit_length()):
+        size = width << bit
+        ahead, behind = pltpu.roll(factor, BLOCK - size, 1), pltpu.roll(factor, size, 1)
+        swapped = jnp.where((lane // size) % 2 == 0, ahead, behind)
+        factor = jnp.where((me[0] >> bit) % 2 == 1, swapped, factor)
     norm = jnp.max(jnp.sum(jnp.abs(factor), axis=1, keepdims=True), axis=0, keepdims=True)
     power = factor / norm
     for _ in range(3):
@@ -365,7 +369,6 @@
 def make_powers(pieces):
     width = pieces[0].shape[0]
     shape = jax.ShapeDtypeStruct
-    turn = (BLOCK - width * lax.axis_index("cols")) % BLOCK
     return call(
         powers_kernel,
         (
@@ -373,7 +376,7 @@
             shape(((ITERS + 1) * width, BLOCK), f32),
             shape((8, BLOCK), f32),
         ),
-        turn.astype(jnp.int32).reshape(1),
+        lax.axis_index("cols").astype(jnp.int32).reshape(1),
         *pieces,
         scalars=1,
     )
@@ -491,11 +494,11 @@
 
     gathered = devices * slots * BLOCK * (BLOCK + width) * 2
     noted = slots * (4 + width) <= BLOCK and width % NOTE_ROWS == 0 and devices * blocks < 2**15
-    whole = gathered <= GATHER_BYTES and noted and devices % 2 == 0 and not exchange
+    whole = gathered <= GATHER_BYTES and noted and devices & (devices - 1) == 0 and not exchange
     units = slots if whole else blocks
     share = -(-units // columns)
     numbers = jnp.arange(columns * share, dtype=jnp.int32)
-    dealer = (lax.axis_index("cols") + columns - numbers // share) % columns
+    dealer = lax.axis_index("cols") ^ (numbers // share)
     order = dealer * share + numbers % share
     if whole:
         local = lists[0]
@@ -566,7 +569,7 @@
     )
     grams = lax.all_to_all(gram, ("cols", "rows"), 0, 0, tiled=True)
     for o in range(1, columns):
-        backs[o] = shift(backs[o], "cols", -o)
+        backs[o] = shift(backs[o], "cols", o)
     return call(
         finish_kernel,
         (shape((width, rows), f32), shape((width, rows), f32)),

time: 55.5 us -> 56.9 us (1.025)
  blocking collectives: 10.1 us -> 11.4 us
  starting transfers between devices: 22.9 us -> 21.8 us
  other arithmetic: 1.03 us -> 1.9 us
  local copies, waits for them, and re-layouts: 0.54 us -> 1.19 us
    all_to_all x1, blocking collectives: 10.1 us -> 11.4 us  [on_device(): grams = lax.all_to_all(gram, ('cols', 'rows'), 0, 0, tiled=True)]
    ppermute x15, starting transfers between devices: 22.2 us -> 21.2 us  [shift(): return lax.ppermute(x, axis, [(i, i ^ by) for i in range(size)])]
    another operation x1, other arithmetic: 0.06 us -> 0.95 us  [chain_gathered(): near = jnp.stack(near)]
    unnamed x12 -> x10, local copies, waits for them, and re-layouts: 0.03 us -> 0.68 us
  transfers between devices with their start and end apart: 17 -> 17, of which waited for: 4 -> 6; matrix products, arithmetic and copies ran while one was open for 3% -> 4% of each run, Pallas kernels for 15% -> 15%
where the time goes in v9:
time: 56.9 us; the launch traced here: 56.7 us
  starting transfers between devices  21.8 us (38%)
  Pallas kernels  15.4 us (27%)
  blocking collectives  11.4 us (20%)
  waiting for transfers between devices  3.52 us (6%)
  other arithmetic  1.9 us (3%)
  between operations  1.45 us (3%)
  local copies, waits for them, and re-layouts  1.19 us (2%)
    ppermute x15, starting transfers between devices, shift(): return lax.ppermute(x, axis, [(i, i ^ by) for i in range(size)])  21.2 us
    pallas_call x6, Pallas kernels, call(): pl.pallas_call(kernel, out_shape=outs, in_specs=specs, out_specs=tuple([V...  15.4 us
    all_to_all x1, blocking collectives, on_device(): grams = lax.all_to_all(gram, ('cols', 'rows'), 0, 0, tiled=True)  11.4 us
    ppermute x15, waiting for transfers between devices, shift(): return lax.ppermute(x, axis, [(i, i ^ by) for i in range(size)])  2.85 us
  transfers between devices with their start and end apart: 17, of which 6 were waited for; matrix products, arithmetic and copies ran while one was open for 4% of the time, Pallas kernels for 15%

profile of v9, /device:TPU:0, one launch (start us, length us, event | category | flops | bytes accessed | tf_op | source)
XLA Modules:
  0.0 56.7 jit_solution(17739432982661696963)
XLA Ops:
  1.3 2.2 %shard_map.86 = s16[496,128]{1,0:T(8,128)(2,1)} custom-call(s32[4]{0:T(128)} %local.1, s32[4]{0:T(128)} %remote.1, s32[1]{0:T(128)} %copy.16.count, f32[32,1024]{1,0:T(8,128)} %gradient.3, f32[8,128,128]{2,1,0:T(8,128)} %jacobi.5, bf16[4,128,128]{2,1,0:T(8,128)(2,1)} %tiles.1), custom_call_target="tpu_custom_call" | custom-call | tf_op jit(solution)/shard_map/pallas_call | solution.py:35
  3.5 4.0 %collective-permute-start.5 = (f32[32,128]{1,0:T(8,128)S(1)}, f32[32,128]{1,0:T(8,128)S(1)}, u32[]{:S(2)}, u32[]{:S(2)}) collective-permute-start(f32[32,128]{1,0:T(8,128)S(1)} %bitcast.15), channel_id=1, source_target_pairs={{0,24},{8,16},{16,8},{24,0},{1,25},{9,17},{17,9},{25,1},{2,26},{10... | collective-permute-start | bytes 49160 | tf_op jit(solution)/shard_map/ppermute | solution.py:168
  7.5 0.5 collective-permute-start.4
  8.0 3.6 %collective-permute-start.2 = (s16[496,128]{1,0:T(8,128)(2,1)}, s16[496,128]{1,0:T(8,128)(2,1)S(1)}, u32[]{:S(2)}, u32[]{:S(2)}) collective-permute-start(s16[496,128]{1,0:T(8,128)(2,1)} %shard_map.86), channel_id=1, source_target_pairs={{0,6},{1,7},{2,4},{3,5},{4,2},{5,3},{6,0},{7,1},{8,14},{9,15},{10,... | collective-permute-start | bytes 380936 | tf_op jit(solution)/shard_map/ppermute | solution.py:168
  11.6 0.8 %collective-permute-start = (s16[496,128]{1,0:T(8,128)(2,1)}, s16[496,128]{1,0:T(8,128)(2,1)S(1)}, u32[]{:S(2)}, u32[]{:S(2)}) collective-permute-start(s16[496,128]{1,0:T(8,128)(2,1)} %shard_map.86), channel_id=1, source_target_pairs={{0,2},{1,3},{2,0},{3,1},{4,6},{5,7},{6,4},{7,5},{8,10},{9,11},{10,... | collective-permute-start | bytes 380936 | tf_op jit(solution)/shard_map/ppermute | solution.py:168
  12.4 0.7 %copy-done.3 = s32[4]{0:T(128)S(1)} copy-done((s32[4]{0:T(128)S(1)}, s32[4]{0:T(128)}, u32[]{:S(2)}) %copy-start.3) | copy-done | bytes 40
  13.1 0.2 fusion.8
  13.3 0.2 select_reduce_fusion.2
  13.5 0.4 collective-permute-start.3
  13.9 2.7 %collective-permute-start.13 = (f32[32,1024]{1,0:T(8,128)S(1)}, f32[32,1024]{1,0:T(8,128)S(1)}, u32[]{:S(2)}, u32[]{:S(2)}) collective-permute-start(f32[32,1024]{1,0:T(8,128)S(1)} %copy-done.1), channel_id=1, source_target_pairs={{0,24},{8,16},{16,8},{24,0},{1,25},{9,17},{17,9},{25,1},{2,26},{10... | collective-permute-start | bytes 393224 | tf_op jit(solution)/shard_map/ppermute | solution.py:168
  16.6 0.9 %collective-permute-done.3.refs_1_ = f32[32,128]{1,0:T(8,128)S(1)} collective-permute-done((f32[32,128]{1,0:T(8,128)S(1)}, f32[32,128]{1,0:T(8,128)S(1)}, u32[]{:S(2)}, u32[]{:S(2)}) %collective-permute-start.3) | collective-permute-done | bytes 16416 | tf_op jit(solution)/shard_map/ppermute | solution.py:168
  17.5 1.3 %collective-permute-start.12 = (f32[32,1024]{1,0:T(8,128)S(1)}, f32[32,1024]{1,0:T(8,128)S(1)}, u32[]{:S(2)}, u32[]{:S(2)}) collective-permute-start(f32[32,1024]{1,0:T(8,128)S(1)} %copy-done.1), channel_id=1, source_target_pairs={{0,16},{8,24},{16,0},{24,8},{1,17},{9,25},{17,1},{25,9},{2,18},{10... | collective-permute-start | bytes 393224 | tf_op jit(solution)/shard_map/ppermute | solution.py:168
  18.8 2.1 %shard_map.87 = (f32[128,128]{1,0:T(8,128)S(1)}, f32[224,128]{1,0:T(8,128)S(1)}, f32[8,128]{1,0:T(8,128)S(1)}) custom-call(s32[1]{0:T(128)} %bitcast.1.me, f32[32,128]{1,0:T(8,128)S(1)} %bitcast.18, f32[32,128]{1,0:T(8,128)S(1)} %collective-permute-done.3.refs_1_, f32[32,128]{1,0:T(8,128)S(1)} %collective-permute-done.4.refs_2_, ...), custom_call_target="tpu_custom_call" | custom-call | tf_op jit(solution)/shard_map/pallas_call | solution.py:35
  21.0 0.8 %collective-permute-start.11 = (f32[32,1024]{1,0:T(8,128)S(1)}, f32[32,1024]{1,0:T(8,128)S(1)}, u32[]{:S(2)}, u32[]{:S(2)}) collective-permute-start(f32[32,1024]{1,0:T(8,128)S(1)} %copy-done.1), channel_id=1, source_target_pairs={{0,8},{8,0},{16,24},{24,16},{1,9},{9,1},{17,25},{25,17},{2,10},{10... | collective-permute-start | bytes 393224 | tf_op jit(solution)/shard_map/ppermute | solution.py:168
  21.7 0.3 collective-permute-done.1
  22.0 1.0 %pad_add_fusion.near = s16[4,496,128]{2,1,0:T(8,128)(2,1)S(1)} fusion(s16[1,496,128]{2,1,0:T(8,128)(2,1)S(1)} %bitcast.20, s16[1,496,128]{2,1,0:T(8,128)(2,1)S(1)} %bitcast.21, s16[1,496,128]{2,1,0:T(8,128)(2,1)S(1)} %bitcast.22, s16[1,496,128]{2,1,0:T(8,128)(2,1)} %bitcast.19), kind=kLoop, calls=%fused_computation | loop fusion | flops 761856 | bytes 1015808 | tf_op jit(solution)/shard_map/stack | solution.py:212
  23.2 0.6 collective-permute-start.7
  23.8 0.4 collective-permute-done.6
  24.6 0.2 select_reduce_fusion
  25.1 0.2 collective-permute-done.7.far
  25.3 3.7 %shard_map.88 = (f32[6,1,32,128]{3,2,1,0:T(8,128)S(1)}, f32[6,1,32,128]{3,2,1,0:T(8,128)S(1)}, f32[6,1,32,128]{3,2,1,0:T(8,128)S(1)}, f32[6,1,32,128]{3,2,1,0:T(8,128)S(1)}) custom-call(s32[72]{0:T(128)S(1)} %select_n.78.sources, s32[4]{0:T(128)S(1)} %compare_select_fusion.give, s16[4,496,128]{2,1,0:T(8,128)(2,1)S(1)} %pad_add_fusion.near, ...), custom_call_target="tpu_custom_call" | custom-call | tf_op jit(solution)/shard_map/pallas_call | solution.py:35
  29.0 1.1 %collective-permute-start.8 = (f32[6,1,32,128]{3,2,1,0:T(8,128)S(1)}, f32[6,1,32,128]{3,2,1,0:T(8,128)S(1)}, u32[]{:S(2)}, u32[]{:S(2)}) collective-permute-start(f32[6,1,32,128]{3,2,1,0:T(8,128)S(1)} %get-tuple-element.46), channel_id=1, source_target_pairs={{0,8},{8,0},{16,24},{24,16},{1,9},{9,1},{17,25},{25,17},{2,10},{10... | collective-permute-start | bytes 294920 | tf_op jit(solution)/shard_map/ppermute | solution.py:168
  30.1 1.0 %collective-permute-start.9 = (f32[6,1,32,128]{3,2,1,0:T(8,128)S(1)}, f32[6,1,32,128]{3,2,1,0:T(8,128)S(1)}, u32[]{:S(2)}, u32[]{:S(2)}) collective-permute-start(f32[6,1,32,128]{3,2,1,0:T(8,128)S(1)} %get-tuple-element.47), channel_id=1, source_target_pairs={{0,16},{8,24},{16,0},{24,8},{1,17},{9,25},{17,1},{25,9},{2,18},{10... | collective-permute-start | bytes 294920 | tf_op jit(solution)/shard_map/ppermute | solution.py:168
  31.1 1.4 %collective-permute-start.10 = (f32[6,1,32,128]{3,2,1,0:T(8,128)S(1)}, f32[6,1,32,128]{3,2,1,0:T(8,128)S(1)}, u32[]{:S(2)}, u32[]{:S(2)}) collective-permute-start(f32[6,1,32,128]{3,2,1,0:T(8,128)S(1)} %get-tuple-element.48), channel_id=1, source_target_pairs={{0,24},{8,16},{16,8},{24,0},{1,25},{9,17},{17,9},{25,1},{2,26},{10... | collective-permute-start | bytes 294920 | tf_op jit(solution)/shard_map/ppermute | solution.py:168
  32.6 2.8 %shard_map.89 = (f32[8,192,128]{2,1,0:T(8,128)S(1)}, f32[8,192,128]{2,1,0:T(8,128)S(1)}, f32[1,128]{1,0:T(1,128)S(1)}, f32[1,128,128]{2,1,0:T(8,128)S(1)}) custom-call(s32[8]{0:T(128)S(1)} %select_reduce_fusion.1.where, s32[4]{0:T(128)S(1)} %get-tuple-element.63.held, f32[224,128]{1,0:T(8,128)S(1)} %get-tuple-element.49.powers, f32[8,128,128]{2,1,0:T(8,128)S(1)} %copy-done, ...), custom_call_target="tpu_custom_call" | custom-call | tf_op jit(solution)/shard_map/pallas_call | solution.py:35
  35.5 1.6 %collective-permute-done.10.refs_3_ = f32[6,1,32,128]{3,2,1,0:T(8,128)S(1)} collective-permute-done((f32[6,1,32,128]{3,2,1,0:T(8,128)S(1)}, f32[6,1,32,128]{3,2,1,0:T(8,128)S(1)}, u32[]{:S(2)}, u32[]{:S(2)}) %collective-permute-start.10) | collective-permute-done | bytes 98336 | tf_op jit(solution)/shard_map/ppermute | solution.py:168
  37.2 2.4 %shard_map.90 = (f32[32,1,128]{2,1,0:T(1,128)S(1)}, f32[6,1,32,128]{3,2,1,0:T(8,128)S(1)}, f32[6,1,32,128]{3,2,1,0:T(8,128)S(1)}, f32[6,1,32,128]{3,2,1,0:T(8,128)S(1)}, f32[6,1,32,128]{3,2,1,0:T(8,128)S(1)}) custom-call(s32[4]{0:T(128)S(1)} %get-tuple-element.63.held, s32[4]{0:T(128)S(1)} %get-tuple-element.62.used, ...), custom_call_target="tpu_custom_call" | custom-call | tf_op jit(solution)/shard_map/pallas_call | solution.py:35
  39.6 1.0 %collective-permute-start.14 = (f32[6,1,32,128]{3,2,1,0:T(8,128)S(1)}, f32[6,1,32,128]{3,2,1,0:T(8,128)S(1)}, u32[]{:S(2)}, u32[]{:S(2)}) collective-permute-start(f32[6,1,32,128]{3,2,1,0:T(8,128)S(1)} %get-tuple-element.59), channel_id=1, source_target_pairs={{0,8},{8,0},{16,24},{24,16},{1,9},{9,1},{17,25},{25,17},{2,10},{10... | collective-permute-start | bytes 294920 | tf_op jit(solution)/shard_map/ppermute | solution.py:168
  40.6 1.4 %collective-permute-start.15 = (f32[6,1,32,128]{3,2,1,0:T(8,128)S(1)}, f32[6,1,32,128]{3,2,1,0:T(8,128)S(1)}, u32[]{:S(2)}, u32[]{:S(2)}) collective-permute-start(f32[6,1,32,128]{3,2,1,0:T(8,128)S(1)} %get-tuple-element.60), channel_id=1, source_target_pairs={{0,16},{8,24},{16,0},{24,8},{1,17},{9,25},{17,1},{25,9},{2,18},{10... | collective-permute-start | bytes 294920 | tf_op jit(solution)/shard_map/ppermute | solution.py:168
  42.0 1.2 %collective-permute-start.16 = (f32[6,1,32,128]{3,2,1,0:T(8,128)S(1)}, f32[6,1,32,128]{3,2,1,0:T(8,128)S(1)}, u32[]{:S(2)}, u32[]{:S(2)}) collective-permute-start(f32[6,1,32,128]{3,2,1,0:T(8,128)S(1)} %get-tuple-element.61), channel_id=1, source_target_pairs={{0,24},{8,16},{16,8},{24,0},{1,25},{9,17},{17,9},{25,1},{2,26},{10... | collective-permute-start | bytes 294920 | tf_op jit(solution)/shard_map/ppermute | solution.py:168
  43.2 11.4 %all_to_all.5.grams = f32[32,1,128]{2,1,0:T(1,128)S(1)} all-to-all(f32[32,1,128]{2,1,0:T(1,128)S(1)} %get-tuple-element.54), channel_id=1, replica_groups=mesh['cols'=4,'rows'=8] {'cols','rows'}, dimensions={0} | all-to-all | bytes 32768 | tf_op jit(solution)/shard_map/all_to_all | solution.py:570
  54.6 2.1 %shard_map.91 = (f32[32,1024]{1,0:T(8,128)}, f32[32,1024]{1,0:T(8,128)}) custom-call(s32[4]{0:T(128)S(1)} %get-tuple-element.63.held, s32[8]{0:T(128)S(1)} %select_reduce_fusion.1.where, f32[32,1,128]{2,1,0:T(1,128)S(1)} %all_to_all.5.grams, f32[8,128]{1,0:T(8,128)S(1)} %get-tuple-element.55.scale, f32[32,1024]{1,0:T(8,128)S(1)} %copy-done.1, ...), custom_call_target="tpu_custom_call" | custom-call | tf_op jit(solution)/shard_map/pallas_call | solution.py:35
  (43 shorter events, 1.1 us)
Async XLA Ops:
  1.3 2.2 %copy-start.2 = (f32[128,32]{0,1:T(8,128)S(1)}, f32[128,32]{0,1:T(8,128)}, u32[]{:S(2)}) copy-start(f32[128,32]{0,1:T(8,128)} %param.9) | copy-start | bytes 49156
  1.3 12.6 %copy-start.1 = (f32[32,1024]{1,0:T(8,128)S(1)}, f32[32,1024]{1,0:T(8,128)}, u32[]{:S(2)}) copy-start(f32[32,1024]{1,0:T(8,128)} %gradient.3) | copy-start | bytes 393220
  3.5 9.9 %collective-permute-start.5 = (f32[32,128]{1,0:T(8,128)S(1)}, f32[32,128]{1,0:T(8,128)S(1)}, u32[]{:S(2)}, u32[]{:S(2)}) collective-permute-start(f32[32,128]{1,0:T(8,128)S(1)} %bitcast.15), channel_id=1, source_target_pairs={{0,24},{8,16},{16,8},{24,0},{1,25},{9,17},{17,9},{25,1},{2,26},{10... | collective-permute-start | bytes 49160 | tf_op jit(solution)/shard_map/ppermute | solution.py:168
  7.5 6.3 %collective-permute-start.4 = (f32[32,128]{1,0:T(8,128)S(1)}, f32[32,128]{1,0:T(8,128)S(1)}, u32[]{:S(2)}, u32[]{:S(2)}) collective-permute-start(f32[32,128]{1,0:T(8,128)S(1)} %bitcast.16), channel_id=1, source_target_pairs={{0,16},{8,24},{16,0},{24,8},{1,17},{9,25},{17,1},{25,9},{2,18},{10... | collective-permute-start | bytes 49160 | tf_op jit(solution)/shard_map/ppermute | solution.py:168
  8.0 12.9 %collective-permute-start.2 = (s16[496,128]{1,0:T(8,128)(2,1)}, s16[496,128]{1,0:T(8,128)(2,1)S(1)}, u32[]{:S(2)}, u32[]{:S(2)}) collective-permute-start(s16[496,128]{1,0:T(8,128)(2,1)} %shard_map.86), channel_id=1, source_target_pairs={{0,6},{1,7},{2,4},{3,5},{4,2},{5,3},{6,0},{7,1},{8,14},{9,15},{10,... | collective-permute-start | bytes 380936 | tf_op jit(solution)/shard_map/ppermute | solution.py:168
  11.6 10.4 %collective-permute-start.1 = (s16[496,128]{1,0:T(8,128)(2,1)}, s16[496,128]{1,0:T(8,128)(2,1)S(1)}, u32[]{:S(2)}, u32[]{:S(2)}) collective-permute-start(s16[496,128]{1,0:T(8,128)(2,1)} %shard_map.86), channel_id=1, source_target_pairs={{0,4},{1,5},{2,6},{3,7},{4,0},{5,1},{6,2},{7,3},{8,12},{9,13},{10,... | collective-permute-start | bytes 380936 | tf_op jit(solution)/shard_map/ppermute | solution.py:168
  11.6 10.4 %collective-permute-start = (s16[496,128]{1,0:T(8,128)(2,1)}, s16[496,128]{1,0:T(8,128)(2,1)S(1)}, u32[]{:S(2)}, u32[]{:S(2)}) collective-permute-start(s16[496,128]{1,0:T(8,128)(2,1)} %shard_map.86), channel_id=1, source_target_pairs={{0,2},{1,3},{2,0},{3,1},{4,6},{5,7},{6,4},{7,5},{8,10},{9,11},{10,... | collective-permute-start | bytes 380936 | tf_op jit(solution)/shard_map/ppermute | solution.py:168
  12.4 0.7 %copy-start.3 = (s32[4]{0:T(128)S(1)}, s32[4]{0:T(128)}, u32[]{:S(2)}) copy-start(s32[4]{0:T(128)} %local.1) | copy-start | bytes 52
  13.5 4.0 %collective-permute-start.3 = (f32[32,128]{1,0:T(8,128)S(1)}, f32[32,128]{1,0:T(8,128)S(1)}, u32[]{:S(2)}, u32[]{:S(2)}) collective-permute-start(f32[32,128]{1,0:T(8,128)S(1)} %bitcast.17), channel_id=1, source_target_pairs={{0,8},{8,0},{16,24},{24,16},{1,9},{9,1},{17,25},{25,17},{2,10},{10... | collective-permute-start | bytes 49160 | tf_op jit(solution)/shard_map/ppermute | solution.py:168
  13.9 17.2 %collective-permute-start.13 = (f32[32,1024]{1,0:T(8,128)S(1)}, f32[32,1024]{1,0:T(8,128)S(1)}, u32[]{:S(2)}, u32[]{:S(2)}) collective-permute-start(f32[32,1024]{1,0:T(8,128)S(1)} %copy-done.1), channel_id=1, source_target_pairs={{0,24},{8,16},{16,8},{24,0},{1,25},{9,17},{17,9},{25,1},{2,26},{10... | collective-permute-start | bytes 393224 | tf_op jit(solution)/shard_map/ppermute | solution.py:168
  17.5 15.2 %collective-permute-start.12 = (f32[32,1024]{1,0:T(8,128)S(1)}, f32[32,1024]{1,0:T(8,128)S(1)}, u32[]{:S(2)}, u32[]{:S(2)}) collective-permute-start(f32[32,1024]{1,0:T(8,128)S(1)} %copy-done.1), channel_id=1, source_target_pairs={{0,16},{8,24},{16,0},{24,8},{1,17},{9,25},{17,1},{25,9},{2,18},{10... | collective-permute-start | bytes 393224 | tf_op jit(solution)/shard_map/ppermute | solution.py:168
  21.0 11.7 %collective-permute-start.11 = (f32[32,1024]{1,0:T(8,128)S(1)}, f32[32,1024]{1,0:T(8,128)S(1)}, u32[]{:S(2)}, u32[]{:S(2)}) collective-permute-start(f32[32,1024]{1,0:T(8,128)S(1)} %copy-done.1), channel_id=1, source_target_pairs={{0,8},{8,0},{16,24},{24,16},{1,9},{9,1},{17,25},{25,17},{2,10},{10... | collective-permute-start | bytes 393224 | tf_op jit(solution)/shard_map/ppermute | solution.py:168
  23.0 1.2 %collective-permute-start.6 = (s16[4,16,128]{2,1,0:T(8,128)(2,1)S(1)}, s16[4,16,128]{2,1,0:T(8,128)(2,1)S(1)}, u32[]{:S(2)}, u32[]{:S(2)}) collective-permute-start(s16[4,16,128]{2,1,0:T(8,128)(2,1)S(1)} %slice.30), channel_id=1, source_target_pairs={{0,1},{1,0},{2,3},{3,2},{4,5},{5,4},{6,7},{7,6},{8,9},{9,8},{10,11... | collective-permute-start | bytes 49160 | tf_op jit(solution)/shard_map/ppermute | solution.py:215
  23.2 2.1 %collective-permute-start.7 = (s16[4,496,128]{2,1,0:T(8,128)(2,1)S(1)}, s16[4,496,128]{2,1,0:T(8,128)(2,1)S(1)}, u32[]{:S(2)}, u32[]{:S(2)}) collective-permute-start(s16[4,496,128]{2,1,0:T(8,128)(2,1)S(1)} %pad_add_fusion.near), channel_id=1, source_target_pairs={{0,1},{1,0},{2,3},{3,2},{4,5},{5,4},{6,7},{7,6},{8,9},{9,8},{10,11... | collective-permute-start | bytes 1523720 | tf_op jit(solution)/shard_map/ppermute | solution.py:216
  24.9 7.7 %copy-start = (f32[8,128,128]{2,1,0:T(8,128)S(1)}, f32[8,128,128]{2,1,0:T(8,128)}, u32[]{:S(2)}) copy-start(f32[8,128,128]{2,1,0:T(8,128)} %jacobi.5) | copy-start | bytes 1572868
  29.0 6.5 %collective-permute-start.8 = (f32[6,1,32,128]{3,2,1,0:T(8,128)S(1)}, f32[6,1,32,128]{3,2,1,0:T(8,128)S(1)}, u32[]{:S(2)}, u32[]{:S(2)}) collective-permute-start(f32[6,1,32,128]{3,2,1,0:T(8,128)S(1)} %get-tuple-element.46), channel_id=1, source_target_pairs={{0,8},{8,0},{16,24},{24,16},{1,9},{9,1},{17,25},{25,17},{2,10},{10... | collective-permute-start | bytes 294920 | tf_op jit(solution)/shard_map/ppermute | solution.py:168
  30.1 5.5 %collective-permute-start.9 = (f32[6,1,32,128]{3,2,1,0:T(8,128)S(1)}, f32[6,1,32,128]{3,2,1,0:T(8,128)S(1)}, u32[]{:S(2)}, u32[]{:S(2)}) collective-permute-start(f32[6,1,32,128]{3,2,1,0:T(8,128)S(1)} %get-tuple-element.47), channel_id=1, source_target_pairs={{0,16},{8,24},{16,0},{24,8},{1,17},{9,25},{17,1},{25,9},{2,18},{10... | collective-permute-start | bytes 294920 | tf_op jit(solution)/shard_map/ppermute | solution.py:168
  31.1 6.1 %collective-permute-start.10 = (f32[6,1,32,128]{3,2,1,0:T(8,128)S(1)}, f32[6,1,32,128]{3,2,1,0:T(8,128)S(1)}, u32[]{:S(2)}, u32[]{:S(2)}) collective-permute-start(f32[6,1,32,128]{3,2,1,0:T(8,128)S(1)} %get-tuple-element.48), channel_id=1, source_target_pairs={{0,24},{8,16},{16,8},{24,0},{1,25},{9,17},{17,9},{25,1},{2,26},{10... | collective-permute-start | bytes 294920 | tf_op jit(solution)/shard_map/ppermute | solution.py:168
  39.6 15.0 %collective-permute-start.14 = (f32[6,1,32,128]{3,2,1,0:T(8,128)S(1)}, f32[6,1,32,128]{3,2,1,0:T(8,128)S(1)}, u32[]{:S(2)}, u32[]{:S(2)}) collective-permute-start(f32[6,1,32,128]{3,2,1,0:T(8,128)S(1)} %get-tuple-element.59), channel_id=1, source_target_pairs={{0,8},{8,0},{16,24},{24,16},{1,9},{9,1},{17,25},{25,17},{2,10},{10... | collective-permute-start | bytes 294920 | tf_op jit(solution)/shard_map/ppermute | solution.py:168
  40.6 14.0 %collective-permute-start.15 = (f32[6,1,32,128]{3,2,1,0:T(8,128)S(1)}, f32[6,1,32,128]{3,2,1,0:T(8,128)S(1)}, u32[]{:S(2)}, u32[]{:S(2)}) collective-permute-start(f32[6,1,32,128]{3,2,1,0:T(8,128)S(1)} %get-tuple-element.60), channel_id=1, source_target_pairs={{0,16},{8,24},{16,0},{24,8},{1,17},{9,25},{17,1},{25,9},{2,18},{10... | collective-permute-start | bytes 294920 | tf_op jit(solution)/shard_map/ppermute | solution.py:168
  42.0 12.6 %collective-permute-start.16 = (f32[6,1,32,128]{3,2,1,0:T(8,128)S(1)}, f32[6,1,32,128]{3,2,1,0:T(8,128)S(1)}, u32[]{:S(2)}, u32[]{:S(2)}) collective-permute-start(f32[6,1,32,128]{3,2,1,0:T(8,128)S(1)} %get-tuple-element.61), channel_id=1, source_target_pairs={{0,24},{8,16},{16,8},{24,0},{1,25},{9,17},{17,9},{25,1},{2,26},{10... | collective-permute-start | bytes 294920 | tf_op jit(solution)/shard_map/ppermute | solution.py:168

commit v10 on v7

--- a/solution.py
+++ b/solution.py
@@ -23,10 +23,6 @@
 f32 = jnp.float32
 VMEM = pl.BlockSpec(memory_space=pltpu.VMEM)
 SMEM = pl.BlockSpec(memory_space=pltpu.SMEM)
-
-
-def dot(a, b):
-    return jnp.dot(a, b, precision=highest, preferred_element_type=f32)
 
 
 def call(kernel, outs, *args, scalars=0, scratch=(), place=VMEM, grant=GRANT_BYTES):
@@ -160,7 +156,7 @@
                 send[j, p] = held[give[o * share + p]]
         return carry
 
-    lax.fori_loop(0, ITERS, step, 0)
+    lax.fori_loop(0, ITERS, step, 0, unroll=True)
 
 
 def shift(x, axis, by):
@@ -332,7 +328,7 @@
     lane = lax.broadcasted_iota(jnp.int32, (width, BLOCK), 1)
     kept = [(row == lane).astype(f32)]
     for k in range(ITERS):
-        value = dot(kept[k], factor) - kept[k]
+        value = dot3(kept[k], factor) - kept[k]
         kept.append(2.0 * value - kept[k - 1] if k else value)
     powers[...] = jnp.concatenate(kept, 0)
 

time: 55.5 us -> 55 us (level)
  Pallas kernels: 15.3 us -> 14.4 us
    pallas_call x6, Pallas kernels: 15.3 us -> 14.4 us  [call(): pl.pallas_call(kernel, out_shape=outs, in_specs=specs, out_specs=tuple([V...]
  transfers between devices with their start and end apart: 17 -> 17, of which waited for: 4 -> 4; matrix products, arithmetic and copies ran while one was open for 3% -> 3% of each run, Pallas kernels for 15% -> 14%
where the time goes in v10:
time: 55 us; the launch traced here: 54.8 us
  starting transfers between devices  22.8 us (41%)
  Pallas kernels  14.4 us (26%)
  blocking collectives  10.6 us (19%)
  waiting for transfers between devices  3.99 us (7%)
  between operations  1.49 us (3%)
  other arithmetic  1.03 us (2%)
    ppermute x15, starting transfers between devices, shift(): return lax.ppermute(x, axis, [(i, (i - by) % size) for i in range(size)])  22.2 us
    pallas_call x6, Pallas kernels, call(): pl.pallas_call(kernel, out_shape=outs, in_specs=specs, out_specs=tuple([V...  14.4 us
    all_to_all x1, blocking collectives, on_device(): grams = lax.all_to_all(gram, ('cols', 'rows'), 0, 0, tiled=True)  10.6 us
    ppermute x15, waiting for transfers between devices, shift(): return lax.ppermute(x, axis, [(i, (i - by) % size) for i in range(size)])  3.32 us
  transfers between devices with their start and end apart: 17, of which 4 were waited for; matrix products, arithmetic and copies ran while one was open for 3% of the time, Pallas kernels for 14%

profile of v10, /device:TPU:0, one launch (start us, length us, event | category | flops | bytes accessed | tf_op | source)
XLA Modules:
  0.0 54.8 jit_solution(14051674903016346030)
XLA Ops:
  1.3 2.2 %shard_map.86 = s16[496,128]{1,0:T(8,128)(2,1)} custom-call(s32[4]{0:T(128)} %local.1, s32[4]{0:T(128)} %remote.1, s32[1]{0:T(128)} %copy.16.count, f32[32,1024]{1,0:T(8,128)} %gradient.3, f32[8,128,128]{2,1,0:T(8,128)} %jacobi.5, bf16[4,128,128]{2,1,0:T(8,128)(2,1)} %tiles.1), custom_call_target="tpu_custom_call" | custom-call | tf_op jit(solution)/shard_map/pallas_call | solution.py:31
  3.6 3.0 %collective-permute-start.5 = (f32[32,128]{1,0:T(8,128)S(1)}, f32[32,128]{1,0:T(8,128)S(1)}, u32[]{:S(2)}, u32[]{:S(2)}) collective-permute-start(f32[32,128]{1,0:T(8,128)S(1)} %bitcast.15), channel_id=1, source_target_pairs={{0,8},{8,16},{16,24},{24,0},{1,9},{9,17},{17,25},{25,1},{2,10},{10... | collective-permute-start | bytes 49160 | tf_op jit(solution)/shard_map/ppermute | solution.py:164
  6.6 1.5 %collective-permute-start.4 = (f32[32,128]{1,0:T(8,128)S(1)}, f32[32,128]{1,0:T(8,128)S(1)}, u32[]{:S(2)}, u32[]{:S(2)}) collective-permute-start(f32[32,128]{1,0:T(8,128)S(1)} %bitcast.16), channel_id=1, source_target_pairs={{0,16},{8,24},{16,0},{24,8},{1,17},{9,25},{17,1},{25,9},{2,18},{10... | collective-permute-start | bytes 49160 | tf_op jit(solution)/shard_map/ppermute | solution.py:164
  8.1 1.6 %collective-permute-start.2 = (s16[496,128]{1,0:T(8,128)(2,1)}, s16[496,128]{1,0:T(8,128)(2,1)S(1)}, u32[]{:S(2)}, u32[]{:S(2)}) collective-permute-start(s16[496,128]{1,0:T(8,128)(2,1)} %shard_map.86), channel_id=1, source_target_pairs={{0,2},{1,3},{2,4},{3,5},{4,6},{5,7},{6,0},{7,1},{8,10},{9,11},{10,... | collective-permute-start | bytes 380936 | tf_op jit(solution)/shard_map/ppermute | solution.py:164
  9.7 2.6 %collective-permute-start.1 = (s16[496,128]{1,0:T(8,128)(2,1)}, s16[496,128]{1,0:T(8,128)(2,1)S(1)}, u32[]{:S(2)}, u32[]{:S(2)}) collective-permute-start(s16[496,128]{1,0:T(8,128)(2,1)} %shard_map.86), channel_id=1, source_target_pairs={{0,4},{1,5},{2,6},{3,7},{4,0},{5,1},{6,2},{7,3},{8,12},{9,13},{10,... | collective-permute-start | bytes 380936 | tf_op jit(solution)/shard_map/ppermute | solution.py:164
  12.3 1.3 %collective-permute-start = (s16[496,128]{1,0:T(8,128)(2,1)}, s16[496,128]{1,0:T(8,128)(2,1)S(1)}, u32[]{:S(2)}, u32[]{:S(2)}) collective-permute-start(s16[496,128]{1,0:T(8,128)(2,1)} %shard_map.86), channel_id=1, source_target_pairs={{0,6},{1,7},{2,0},{3,1},{4,2},{5,3},{6,4},{7,5},{8,14},{9,15},{10,... | collective-permute-start | bytes 380936 | tf_op jit(solution)/shard_map/ppermute | solution.py:164
  13.6 0.2 fusion.8
  13.8 0.2 select_reduce_fusion.2
  14.0 1.5 %collective-permute-start.3 = (f32[32,128]{1,0:T(8,128)S(1)}, f32[32,128]{1,0:T(8,128)S(1)}, u32[]{:S(2)}, u32[]{:S(2)}) collective-permute-start(f32[32,128]{1,0:T(8,128)S(1)} %bitcast.17), channel_id=1, source_target_pairs={{0,24},{8,0},{16,8},{24,16},{1,25},{9,1},{17,9},{25,17},{2,26},{10... | collective-permute-start | bytes 49160 | tf_op jit(solution)/shard_map/ppermute | solution.py:164
  15.6 0.6 %collective-permute-start.13 = (f32[32,1024]{1,0:T(8,128)S(1)}, f32[32,1024]{1,0:T(8,128)S(1)}, u32[]{:S(2)}, u32[]{:S(2)}) collective-permute-start(f32[32,1024]{1,0:T(8,128)S(1)} %copy-done.1), channel_id=1, source_target_pairs={{0,8},{8,16},{16,24},{24,0},{1,9},{9,17},{17,25},{25,1},{2,10},{10... | collective-permute-start | bytes 393224 | tf_op jit(solution)/shard_map/ppermute | solution.py:164
  16.2 1.7 %collective-permute-done.3.refs_1_ = f32[32,128]{1,0:T(8,128)S(1)} collective-permute-done((f32[32,128]{1,0:T(8,128)S(1)}, f32[32,128]{1,0:T(8,128)S(1)}, u32[]{:S(2)}, u32[]{:S(2)}) %collective-permute-start.3) | collective-permute-done | bytes 16416 | tf_op jit(solution)/shard_map/ppermute | solution.py:164
  17.9 0.6 %collective-permute-start.12 = (f32[32,1024]{1,0:T(8,128)S(1)}, f32[32,1024]{1,0:T(8,128)S(1)}, u32[]{:S(2)}, u32[]{:S(2)}) collective-permute-start(f32[32,1024]{1,0:T(8,128)S(1)} %copy-done.1), channel_id=1, source_target_pairs={{0,16},{8,24},{16,0},{24,8},{1,17},{9,25},{17,1},{25,9},{2,18},{10... | collective-permute-start | bytes 393224 | tf_op jit(solution)/shard_map/ppermute | solution.py:164
  18.5 1.6 %shard_map.87 = (f32[128,128]{1,0:T(8,128)S(1)}, f32[224,128]{1,0:T(8,128)S(1)}, f32[8,128]{1,0:T(8,128)S(1)}) custom-call(s32[1]{0:T(128)} %bitcast.1.turn, f32[32,128]{1,0:T(8,128)S(1)} %bitcast.18, f32[32,128]{1,0:T(8,128)S(1)} %collective-permute-done.3.refs_1_, f32[32,128]{1,0:T(8,128)S(1)} %collective-permute-done.4.refs_2_, ...), custom_call_target="tpu_custom_call" | custom-call | tf_op jit(solution)/shard_map/pallas_call | solution.py:31
  20.1 2.2 %collective-permute-start.11 = (f32[32,1024]{1,0:T(8,128)S(1)}, f32[32,1024]{1,0:T(8,128)S(1)}, u32[]{:S(2)}, u32[]{:S(2)}) collective-permute-start(f32[32,1024]{1,0:T(8,128)S(1)} %copy-done.1), channel_id=1, source_target_pairs={{0,24},{8,0},{16,8},{24,16},{1,25},{9,1},{17,9},{25,17},{2,26},{10... | collective-permute-start | bytes 393224 | tf_op jit(solution)/shard_map/ppermute | solution.py:164
  22.7 0.6 %collective-permute-start.7 = (s16[4,496,128]{2,1,0:T(8,128)(2,1)S(1)}, s16[4,496,128]{2,1,0:T(8,128)(2,1)S(1)}, u32[]{:S(2)}, u32[]{:S(2)}) collective-permute-start(s16[4,496,128]{2,1,0:T(8,128)(2,1)S(1)} %pad_add_fusion.near), channel_id=1, source_target_pairs={{0,1},{1,0},{2,3},{3,2},{4,5},{5,4},{6,7},{7,6},{8,9},{9,8},{10,11... | collective-permute-start | bytes 1523720 | tf_op jit(solution)/shard_map/ppermute | solution.py:212
  23.2 0.4 collective-permute-done.6
  24.0 0.2 select_reduce_fusion
  24.3 0.1 and_select_fusion
  24.4 0.1 select_n.103.sources
  24.5 0.2 collective-permute-done.7.far
  24.7 3.2 %shard_map.88 = (f32[6,1,32,128]{3,2,1,0:T(8,128)S(1)}, f32[6,1,32,128]{3,2,1,0:T(8,128)S(1)}, f32[6,1,32,128]{3,2,1,0:T(8,128)S(1)}, f32[6,1,32,128]{3,2,1,0:T(8,128)S(1)}) custom-call(s32[72]{0:T(128)S(1)} %select_n.103.sources, s32[4]{0:T(128)S(1)} %compare_select_fusion.give, s16[4,496,128]{2,1,0:T(8,128)(2,1)S(1)} %pad_add_fusion.near, ...), custom_call_target="tpu_custom_call" | custom-call | tf_op jit(solution)/shard_map/pallas_call | solution.py:31
  27.9 0.8 %collective-permute-start.8 = (f32[6,1,32,128]{3,2,1,0:T(8,128)S(1)}, f32[6,1,32,128]{3,2,1,0:T(8,128)S(1)}, u32[]{:S(2)}, u32[]{:S(2)}) collective-permute-start(f32[6,1,32,128]{3,2,1,0:T(8,128)S(1)} %get-tuple-element.46), channel_id=1, source_target_pairs={{0,24},{8,0},{16,8},{24,16},{1,25},{9,1},{17,9},{25,17},{2,26},{10... | collective-permute-start | bytes 294920 | tf_op jit(solution)/shard_map/ppermute | solution.py:164
  28.7 0.9 %collective-permute-start.9 = (f32[6,1,32,128]{3,2,1,0:T(8,128)S(1)}, f32[6,1,32,128]{3,2,1,0:T(8,128)S(1)}, u32[]{:S(2)}, u32[]{:S(2)}) collective-permute-start(f32[6,1,32,128]{3,2,1,0:T(8,128)S(1)} %get-tuple-element.47), channel_id=1, source_target_pairs={{0,16},{8,24},{16,0},{24,8},{1,17},{9,25},{17,1},{25,9},{2,18},{10... | collective-permute-start | bytes 294920 | tf_op jit(solution)/shard_map/ppermute | solution.py:164
  29.6 1.9 %collective-permute-start.10 = (f32[6,1,32,128]{3,2,1,0:T(8,128)S(1)}, f32[6,1,32,128]{3,2,1,0:T(8,128)S(1)}, u32[]{:S(2)}, u32[]{:S(2)}) collective-permute-start(f32[6,1,32,128]{3,2,1,0:T(8,128)S(1)} %get-tuple-element.48), channel_id=1, source_target_pairs={{0,8},{8,16},{16,24},{24,0},{1,9},{9,17},{17,25},{25,1},{2,10},{10... | collective-permute-start | bytes 294920 | tf_op jit(solution)/shard_map/ppermute | solution.py:164
  31.6 2.8 %shard_map.89 = (f32[8,192,128]{2,1,0:T(8,128)S(1)}, f32[8,192,128]{2,1,0:T(8,128)S(1)}, f32[1,128]{1,0:T(1,128)S(1)}, f32[1,128,128]{2,1,0:T(8,128)S(1)}) custom-call(s32[8]{0:T(128)S(1)} %select_reduce_fusion.1.where, s32[4]{0:T(128)S(1)} %get-tuple-element.63.held, f32[224,128]{1,0:T(8,128)S(1)} %get-tuple-element.49.powers, f32[8,128,128]{2,1,0:T(8,128)S(1)} %copy-done, ...), custom_call_target="tpu_custom_call" | custom-call | tf_op jit(solution)/shard_map/pallas_call | solution.py:31
  34.5 1.6 %collective-permute-done.10.refs_3_ = f32[6,1,32,128]{3,2,1,0:T(8,128)S(1)} collective-permute-done((f32[6,1,32,128]{3,2,1,0:T(8,128)S(1)}, f32[6,1,32,128]{3,2,1,0:T(8,128)S(1)}, u32[]{:S(2)}, u32[]{:S(2)}) %collective-permute-start.10) | collective-permute-done | bytes 98336 | tf_op jit(solution)/shard_map/ppermute | solution.py:164
  36.1 2.4 %shard_map.90 = (f32[32,1,128]{2,1,0:T(1,128)S(1)}, f32[6,1,32,128]{3,2,1,0:T(8,128)S(1)}, f32[6,1,32,128]{3,2,1,0:T(8,128)S(1)}, f32[6,1,32,128]{3,2,1,0:T(8,128)S(1)}, f32[6,1,32,128]{3,2,1,0:T(8,128)S(1)}) custom-call(s32[4]{0:T(128)S(1)} %get-tuple-element.63.held, s32[4]{0:T(128)S(1)} %get-tuple-element.62.used, ...), custom_call_target="tpu_custom_call" | custom-call | tf_op jit(solution)/shard_map/pallas_call | solution.py:31
  38.5 0.3 collective-permute-start.14
  38.9 0.9 %collective-permute-start.15 = (f32[6,1,32,128]{3,2,1,0:T(8,128)S(1)}, f32[6,1,32,128]{3,2,1,0:T(8,128)S(1)}, u32[]{:S(2)}, u32[]{:S(2)}) collective-permute-start(f32[6,1,32,128]{3,2,1,0:T(8,128)S(1)} %get-tuple-element.60), channel_id=1, source_target_pairs={{0,16},{8,24},{16,0},{24,8},{1,17},{9,25},{17,1},{25,9},{2,18},{10... | collective-permute-start | bytes 294920 | tf_op jit(solution)/shard_map/ppermute | solution.py:164
  39.8 2.3 %collective-permute-start.16 = (f32[6,1,32,128]{3,2,1,0:T(8,128)S(1)}, f32[6,1,32,128]{3,2,1,0:T(8,128)S(1)}, u32[]{:S(2)}, u32[]{:S(2)}) collective-permute-start(f32[6,1,32,128]{3,2,1,0:T(8,128)S(1)} %get-tuple-element.61), channel_id=1, source_target_pairs={{0,24},{8,0},{16,8},{24,16},{1,25},{9,1},{17,9},{25,17},{2,26},{10... | collective-permute-start | bytes 294920 | tf_op jit(solution)/shard_map/ppermute | solution.py:164
  42.2 10.6 %all_to_all.5.grams = f32[32,1,128]{2,1,0:T(1,128)S(1)} all-to-all(f32[32,1,128]{2,1,0:T(1,128)S(1)} %get-tuple-element.54), channel_id=1, replica_groups=mesh['cols'=4,'rows'=8] {'cols','rows'}, dimensions={0} | all-to-all | bytes 32768 | tf_op jit(solution)/shard_map/all_to_all | solution.py:563
  52.7 2.1 %shard_map.91 = (f32[32,1024]{1,0:T(8,128)}, f32[32,1024]{1,0:T(8,128)}) custom-call(s32[4]{0:T(128)S(1)} %get-tuple-element.63.held, s32[8]{0:T(128)S(1)} %select_reduce_fusion.1.where, f32[32,1,128]{2,1,0:T(1,128)S(1)} %all_to_all.5.grams, f32[8,128]{1,0:T(8,128)S(1)} %get-tuple-element.55.scale, f32[32,1024]{1,0:T(8,128)S(1)} %copy-done.1, ...), custom_call_target="tpu_custom_call" | custom-call | tf_op jit(solution)/shard_map/pallas_call | solution.py:31
  (45 shorter events, 0.9 us)
Async XLA Ops:
  1.3 2.3 %copy-start.2 = (f32[128,32]{0,1:T(8,128)S(1)}, f32[128,32]{0,1:T(8,128)}, u32[]{:S(2)}) copy-start(f32[128,32]{0,1:T(8,128)} %param.9) | copy-start | bytes 49156
  1.3 12.3 %copy-start.4 = (s32[4]{0:T(128)S(1)}, s32[4]{0:T(128)}, u32[]{:S(2)}) copy-start(s32[4]{0:T(128)} %local.1) | copy-start | bytes 52
  1.3 14.2 %copy-start.1 = (f32[32,1024]{1,0:T(8,128)S(1)}, f32[32,1024]{1,0:T(8,128)}, u32[]{:S(2)}) copy-start(f32[32,1024]{1,0:T(8,128)} %gradient.3) | copy-start | bytes 393220
  3.5 18.8 %copy-start.3 = (s16[496,128]{1,0:T(8,128)(2,1)S(1)}, s16[496,128]{1,0:T(8,128)(2,1)}, u32[]{:S(2)}) copy-start(s16[496,128]{1,0:T(8,128)(2,1)} %shard_map.86) | copy-start | bytes 380932
  3.6 10.5 %collective-permute-start.5 = (f32[32,128]{1,0:T(8,128)S(1)}, f32[32,128]{1,0:T(8,128)S(1)}, u32[]{:S(2)}, u32[]{:S(2)}) collective-permute-start(f32[32,128]{1,0:T(8,128)S(1)} %bitcast.15), channel_id=1, source_target_pairs={{0,8},{8,16},{16,24},{24,0},{1,9},{9,17},{17,25},{25,1},{2,10},{10... | collective-permute-start | bytes 49160 | tf_op jit(solution)/shard_map/ppermute | solution.py:164
  6.6 9.0 %collective-permute-start.4 = (f32[32,128]{1,0:T(8,128)S(1)}, f32[32,128]{1,0:T(8,128)S(1)}, u32[]{:S(2)}, u32[]{:S(2)}) collective-permute-start(f32[32,128]{1,0:T(8,128)S(1)} %bitcast.16), channel_id=1, source_target_pairs={{0,16},{8,24},{16,0},{24,8},{1,17},{9,25},{17,1},{25,9},{2,18},{10... | collective-permute-start | bytes 49160 | tf_op jit(solution)/shard_map/ppermute | solution.py:164
  8.1 12.0 %collective-permute-start.2 = (s16[496,128]{1,0:T(8,128)(2,1)}, s16[496,128]{1,0:T(8,128)(2,1)S(1)}, u32[]{:S(2)}, u32[]{:S(2)}) collective-permute-start(s16[496,128]{1,0:T(8,128)(2,1)} %shard_map.86), channel_id=1, source_target_pairs={{0,2},{1,3},{2,4},{3,5},{4,6},{5,7},{6,0},{7,1},{8,10},{9,11},{10,... | collective-permute-start | bytes 380936 | tf_op jit(solution)/shard_map/ppermute | solution.py:164
  9.7 12.7 %collective-permute-start.1 = (s16[496,128]{1,0:T(8,128)(2,1)}, s16[496,128]{1,0:T(8,128)(2,1)S(1)}, u32[]{:S(2)}, u32[]{:S(2)}) collective-permute-start(s16[496,128]{1,0:T(8,128)(2,1)} %shard_map.86), channel_id=1, source_target_pairs={{0,4},{1,5},{2,6},{3,7},{4,0},{5,1},{6,2},{7,3},{8,12},{9,13},{10,... | collective-permute-start | bytes 380936 | tf_op jit(solution)/shard_map/ppermute | solution.py:164
  12.3 10.1 %collective-permute-start = (s16[496,128]{1,0:T(8,128)(2,1)}, s16[496,128]{1,0:T(8,128)(2,1)S(1)}, u32[]{:S(2)}, u32[]{:S(2)}) collective-permute-start(s16[496,128]{1,0:T(8,128)(2,1)} %shard_map.86), channel_id=1, source_target_pairs={{0,6},{1,7},{2,0},{3,1},{4,2},{5,3},{6,4},{7,5},{8,14},{9,15},{10,... | collective-permute-start | bytes 380936 | tf_op jit(solution)/shard_map/ppermute | solution.py:164
  14.0 3.9 %collective-permute-start.3 = (f32[32,128]{1,0:T(8,128)S(1)}, f32[32,128]{1,0:T(8,128)S(1)}, u32[]{:S(2)}, u32[]{:S(2)}) collective-permute-start(f32[32,128]{1,0:T(8,128)S(1)} %bitcast.17), channel_id=1, source_target_pairs={{0,24},{8,0},{16,8},{24,16},{1,25},{9,1},{17,9},{25,17},{2,26},{10... | collective-permute-start | bytes 49160 | tf_op jit(solution)/shard_map/ppermute | solution.py:164
  15.6 14.0 %collective-permute-start.13 = (f32[32,1024]{1,0:T(8,128)S(1)}, f32[32,1024]{1,0:T(8,128)S(1)}, u32[]{:S(2)}, u32[]{:S(2)}) collective-permute-start(f32[32,1024]{1,0:T(8,128)S(1)} %copy-done.1), channel_id=1, source_target_pairs={{0,8},{8,16},{16,24},{24,0},{1,9},{9,17},{17,25},{25,1},{2,10},{10... | collective-permute-start | bytes 393224 | tf_op jit(solution)/shard_map/ppermute | solution.py:164
  17.9 13.7 %collective-permute-start.12 = (f32[32,1024]{1,0:T(8,128)S(1)}, f32[32,1024]{1,0:T(8,128)S(1)}, u32[]{:S(2)}, u32[]{:S(2)}) collective-permute-start(f32[32,1024]{1,0:T(8,128)S(1)} %copy-done.1), channel_id=1, source_target_pairs={{0,16},{8,24},{16,0},{24,8},{1,17},{9,25},{17,1},{25,9},{2,18},{10... | collective-permute-start | bytes 393224 | tf_op jit(solution)/shard_map/ppermute | solution.py:164
  20.1 11.5 %collective-permute-start.11 = (f32[32,1024]{1,0:T(8,128)S(1)}, f32[32,1024]{1,0:T(8,128)S(1)}, u32[]{:S(2)}, u32[]{:S(2)}) collective-permute-start(f32[32,1024]{1,0:T(8,128)S(1)} %copy-done.1), channel_id=1, source_target_pairs={{0,24},{8,0},{16,8},{24,16},{1,25},{9,1},{17,9},{25,17},{2,26},{10... | collective-permute-start | bytes 393224 | tf_op jit(solution)/shard_map/ppermute | solution.py:164
  22.4 1.2 %collective-permute-start.6 = (s16[4,16,128]{2,1,0:T(8,128)(2,1)S(1)}, s16[4,16,128]{2,1,0:T(8,128)(2,1)S(1)}, u32[]{:S(2)}, u32[]{:S(2)}) collective-permute-start(s16[4,16,128]{2,1,0:T(8,128)(2,1)S(1)} %slice.30), channel_id=1, source_target_pairs={{0,1},{1,0},{2,3},{3,2},{4,5},{5,4},{6,7},{7,6},{8,9},{9,8},{10,11... | collective-permute-start | bytes 49160 | tf_op jit(solution)/shard_map/ppermute | solution.py:211
  22.7 2.1 %collective-permute-start.7 = (s16[4,496,128]{2,1,0:T(8,128)(2,1)S(1)}, s16[4,496,128]{2,1,0:T(8,128)(2,1)S(1)}, u32[]{:S(2)}, u32[]{:S(2)}) collective-permute-start(s16[4,496,128]{2,1,0:T(8,128)(2,1)S(1)} %pad_add_fusion.near), channel_id=1, source_target_pairs={{0,1},{1,0},{2,3},{3,2},{4,5},{5,4},{6,7},{7,6},{8,9},{9,8},{10,11... | collective-permute-start | bytes 1523720 | tf_op jit(solution)/shard_map/ppermute | solution.py:212
  24.4 7.2 %copy-start = (f32[8,128,128]{2,1,0:T(8,128)S(1)}, f32[8,128,128]{2,1,0:T(8,128)}, u32[]{:S(2)}) copy-start(f32[8,128,128]{2,1,0:T(8,128)} %jacobi.5) | copy-start | bytes 1572868
  27.9 6.6 %collective-permute-start.8 = (f32[6,1,32,128]{3,2,1,0:T(8,128)S(1)}, f32[6,1,32,128]{3,2,1,0:T(8,128)S(1)}, u32[]{:S(2)}, u32[]{:S(2)}) collective-permute-start(f32[6,1,32,128]{3,2,1,0:T(8,128)S(1)} %get-tuple-element.46), channel_id=1, source_target_pairs={{0,24},{8,0},{16,8},{24,16},{1,25},{9,1},{17,9},{25,17},{2,26},{10... | collective-permute-start | bytes 294920 | tf_op jit(solution)/shard_map/ppermute | solution.py:164
  28.7 5.8 %collective-permute-start.9 = (f32[6,1,32,128]{3,2,1,0:T(8,128)S(1)}, f32[6,1,32,128]{3,2,1,0:T(8,128)S(1)}, u32[]{:S(2)}, u32[]{:S(2)}) collective-permute-start(f32[6,1,32,128]{3,2,1,0:T(8,128)S(1)} %get-tuple-element.47), channel_id=1, source_target_pairs={{0,16},{8,24},{16,0},{24,8},{1,17},{9,25},{17,1},{25,9},{2,18},{10... | collective-permute-start | bytes 294920 | tf_op jit(solution)/shard_map/ppermute | solution.py:164
  29.6 6.5 %collective-permute-start.10 = (f32[6,1,32,128]{3,2,1,0:T(8,128)S(1)}, f32[6,1,32,128]{3,2,1,0:T(8,128)S(1)}, u32[]{:S(2)}, u32[]{:S(2)}) collective-permute-start(f32[6,1,32,128]{3,2,1,0:T(8,128)S(1)} %get-tuple-element.48), channel_id=1, source_target_pairs={{0,8},{8,16},{16,24},{24,0},{1,9},{9,17},{17,25},{25,1},{2,10},{10... | collective-permute-start | bytes 294920 | tf_op jit(solution)/shard_map/ppermute | solution.py:164
  38.5 14.2 %collective-permute-start.14 = (f32[6,1,32,128]{3,2,1,0:T(8,128)S(1)}, f32[6,1,32,128]{3,2,1,0:T(8,128)S(1)}, u32[]{:S(2)}, u32[]{:S(2)}) collective-permute-start(f32[6,1,32,128]{3,2,1,0:T(8,128)S(1)} %get-tuple-element.59), channel_id=1, source_target_pairs={{0,8},{8,16},{16,24},{24,0},{1,9},{9,17},{17,25},{25,1},{2,10},{10... | collective-permute-start | bytes 294920 | tf_op jit(solution)/shard_map/ppermute | solution.py:164
  38.9 13.8 %collective-permute-start.15 = (f32[6,1,32,128]{3,2,1,0:T(8,128)S(1)}, f32[6,1,32,128]{3,2,1,0:T(8,128)S(1)}, u32[]{:S(2)}, u32[]{:S(2)}) collective-permute-start(f32[6,1,32,128]{3,2,1,0:T(8,128)S(1)} %get-tuple-element.60), channel_id=1, source_target_pairs={{0,16},{8,24},{16,0},{24,8},{1,17},{9,25},{17,1},{25,9},{2,18},{10... | collective-permute-start | bytes 294920 | tf_op jit(solution)/shard_map/ppermute | solution.py:164
  39.8 12.9 %collective-permute-start.16 = (f32[6,1,32,128]{3,2,1,0:T(8,128)S(1)}, f32[6,1,32,128]{3,2,1,0:T(8,128)S(1)}, u32[]{:S(2)}, u32[]{:S(2)}) collective-permute-start(f32[6,1,32,128]{3,2,1,0:T(8,128)S(1)} %get-tuple-element.61), channel_id=1, source_target_pairs={{0,24},{8,0},{16,8},{24,16},{1,25},{9,1},{17,9},{25,17},{2,26},{10... | collective-permute-start | bytes 294920 | tf_op jit(solution)/shard_map/ppermute | solution.py:164
